TPU v7x, 32 devices: a whole 2x2x4 slice. The times are simulated.
32 devices in a mesh: chan: 8 (over y, x, core), tm: 4 (over z).
Axes of the slice: x: 2, y: 2, z: 4, core: 2. Of those that a mesh axis runs over, the one named last changes fastest.
Arguments:
- record: bfloat16 [20480, 8192], P('chan', 'tm'), may hold values from -6 to 6
- fir_taps: bfloat16 [129], replicated, may hold values from -0.5 to 0.5
- space_taps: float32 [9], replicated, may hold values from -2 to 2
- range_probe: bfloat16 [8192, 128], P('tm'), may hold values from -0.0625 to 0.0625
- corange_probe: bfloat16 [20480, 256], P('chan'), may hold values from -0.0625 to 0.0625
Outputs:
- range_sketch: float32 [20480, 128], P(('chan', 'tm'))
- corange_sketch: float32 [256, 8192], P('chan', 'tm')
All inputs are finite; a program needn't handle non-finite values.
Results may differ from a plain program's by a relative error of at most 0.0041.
Values may be sent and summed in bfloat16 or wider, within the bound.
No kernel may reach another device: no remote copies, remote signals or barrier semaphores. Data moves between devices by JAX's collectives and lax.ppermute only.
A program may use at most 192 MiB of HBM per device.

v0:
```python
import jax
import jax.numpy as jnp
from jax import lax
from jax.sharding import PartitionSpec as P

CHTAPS = 9


def with_halo(block, sides, width):
    for axis, dim in sides:
        count = lax.axis_size(axis)
        forward = [(i, i + 1) for i in range(count - 1)]
        backward = [(target, source) for source, target in forward]
        low = lax.ppermute(
            lax.slice_in_dim(block, block.shape[dim] - width, None, axis=dim), axis, forward
        )
        high = lax.ppermute(lax.slice_in_dim(block, 0, width, axis=dim), axis, backward)
        block = jnp.concatenate([low, block, high], axis=dim)
    return block


def toeplitz(fir_taps):
    extended = jnp.concatenate([fir_taps, jnp.zeros((128,), fir_taps.dtype)])
    tiled = jnp.tile(extended, 128)[: 128 * 256].reshape(128, 256)
    return tiled.T


def apply_band(padded, band_matrix, length):
    channels = padded.shape[0]
    low_part = padded[:, :length].reshape(-1, 128)
    high_part = padded[:, 128 : length + 128].reshape(-1, 128)
    summed = jnp.dot(low_part, band_matrix[:128], preferred_element_type=jnp.float32)
    summed = summed + jnp.dot(high_part, band_matrix[128:], preferred_element_type=jnp.float32)
    return summed.reshape(channels, length)


def on_device(record, fir_taps, space_taps, range_probe, corange_probe):
    channels, samples = record.shape
    band_matrix = toeplitz(fir_taps)
    padded = with_halo(record, (("tm", 1),), 64)
    filtered = apply_band(padded, band_matrix, samples).astype(jnp.bfloat16)
    channel_pad = with_halo(filtered, (("chan", 0),), 4)
    summed = jnp.zeros((channels, samples), jnp.float32)
    for offset in range(CHTAPS):
        summed = summed + space_taps[offset] * channel_pad[offset : offset + channels].astype(
            jnp.float32
        )
    mixed_field = summed.astype(jnp.bfloat16)
    range_sketch = lax.psum_scatter(
        jnp.dot(mixed_field, range_probe, preferred_element_type=jnp.float32),
        "tm",
        scatter_dimension=0,
        tiled=True,
    )
    partial_value = lax.dot_general(
        corange_probe, mixed_field, (((0,), (0,)), ((), ())), preferred_element_type=jnp.float32
    )
    corange_sketch = lax.psum_scatter(partial_value, "chan", scatter_dimension=0, tiled=True)
    return (range_sketch, corange_sketch)


def solution(mesh):
    return jax.shard_map(
        on_device,
        mesh=mesh,
        in_specs=(P("chan", "tm"), P(), P(), P("tm", None), P("chan", None)),
        out_specs=(P(("chan", "tm"), None), P("chan", "tm")),
        check_vma=False,
    )
```

profile of v0, /device:TPU:0, one launch (start us, length us, event | category | flops | bytes accessed | tf_op | source)
XLA Modules:
  0.0 277.5 jit_solution(4850656096720585798)
XLA Ops:
  7.2 0.0 copy-start
  7.2 0.0 reduce-scatter.5.cloned.1.call-start
  7.2 1.6 fusion.8
  8.9 0.2 copy.16
  9.1 4.9 %collective-permute-start = (bf16[2560,64]{0,1:T(8,128)(2,1)S(1)}, bf16[2560,64]{0,1:T(8,128)(2,1)S(1)}, u32[]{:S(2)}, u32[]{:S(2)}) collective-permute-start(bf16[2560,64]{0,1:T(8,128)(2,1)S(1)} %copy.16), channel_id=1, source_target_pairs={{0,1},{1,2},{2,3},{4,5},{5,6},{6,7},{8,9},{9,10},{10,11},{12,13},{... | collective-permute-start | bytes 983048 | tf_op jit(solution)/shard_map/ppermute | solution.py:14
  14.1 0.2 copy.17
  14.3 1.3 collective-permute-start.1
  15.6 0.7 concatenate.24
  16.3 0.3 tile.10
  16.7 1.7 fusion.9
  18.3 2.7 collective-permute-done
  21.0 0.3 copy.10
  21.3 4.0 %collective-permute-done.1 = bf16[2560,64]{0,1:T(8,128)(2,1)S(1)} collective-permute-done((bf16[2560,64]{0,1:T(8,128)(2,1)S(1)}, bf16[2560,64]{0,1:T(8,128)(2,1)S(1)}, u32[]{:S(2)}, u32[]{:S(2)}) %collective-permute-start.1) | collective-permute-done | bytes 327712 | tf_op jit(solution)/shard_map/ppermute | solution.py:17
  25.4 0.3 copy.12
  25.7 21.8 %pad_maximum_fusion.2 = (bf16[2560,2048]{1,0:T(8,128)(2,1)}, bf16[2560,2048]{1,0:T(8,128)(2,1)}) fusion(bf16[2560,2048]{1,0:T(8,128)(2,1)} %param.5, bf16[2560,64]{1,0:T(8,128)(2,1)S(1)} %copy.10, bf16[2560,64]{1,0:T(8,128)(2,1)S(1)} %copy.12), kind=kLoop, calls=%fused_computation.12 | loop fusion | flops 41943040 | bytes 32112640 | tf_op jit(solution)/shard_map/concatenate | solution.py:18
  47.5 16.5 %reshape.20 = bf16[40960,128]{1,0:T(8,128)(2,1)} reshape(bf16[2560,2048]{1,0:T(8,128)(2,1)} %get-tuple-element.11) | data formatting | bytes 20971520 | tf_op jit(solution)/shard_map/reshape | solution.py:31
  64.0 16.5 %reshape.18 = bf16[40960,128]{1,0:T(8,128)(2,1)} reshape(bf16[2560,2048]{1,0:T(8,128)(2,1)} %get-tuple-element.10) | data formatting | bytes 20971520 | tf_op jit(solution)/shard_map/reshape | solution.py:30
  80.5 11.0 %fusion.4 = f32[40960,128]{1,0:T(8,128)} fusion(bf16[40960,128]{1,0:T(8,128)(2,1)} %reshape.20, bf16[256,128]{0,1:T(8,128)(2,1)S(1)} %bitcast.19), kind=kOutput, calls=%fused_computation.14 | convolution fusion | flops 1342177280 | bytes 31490048 | tf_op jit(solution)/shard_map/dot_general | solution.py:33
  91.5 15.7 %fusion = bf16[40960,128]{1,0:T(8,128)(2,1)} fusion(f32[40960,128]{1,0:T(8,128)} %fusion.4, bf16[40960,128]{1,0:T(8,128)(2,1)} %reshape.18, bf16[256,128]{0,1:T(8,128)(2,1)S(1)} %bitcast.20), kind=kOutput, calls=%fused_computation.1 | convolution fusion | flops 1352663040 | bytes 41975808 | tf_op jit(solution)/shard_map/dot_general | solution.py:32
  107.2 16.3 %convert_element_type.37 = bf16[2560,2048]{1,0:T(8,128)(2,1)} reshape(bf16[40960,128]{1,0:T(8,128)(2,1)} %fusion) | data formatting | bytes 20971520 | tf_op jit(solution)/shard_map/convert_element_type | solution.py:41
  123.5 0.7 fusion.7
  124.3 1.3 collective-permute-start.3
  125.5 10.2 %constant_dynamic-update-slice_fusion.1 = bf16[2564,2048]{1,0:T(8,128)(2,1)} fusion(bf16[2560,2048]{1,0:T(8,128)(2,1)} %convert_element_type.37), kind=kLoop, calls=%fused_computation.18 | loop fusion | bytes 20971520
  135.7 3.2 %collective-permute-start.2 = (bf16[4,2048]{1,0:T(4,128)(2,1)S(1)}, bf16[4,2048]{1,0:T(4,128)(2,1)S(1)}, u32[]{:S(2)}, u32[]{:S(2)}) collective-permute-start(bf16[4,2048]{1,0:T(4,128)(2,1)S(1)} %slice.103), channel_id=1, source_target_pairs={{0,4},{4,8},{8,12},{12,16},{16,20},{20,24},{24,28},{1,5},{5,9},{9,... | collective-permute-start | bytes 49160 | tf_op jit(solution)/shard_map/ppermute | solution.py:14
  138.9 0.0 collective-permute-done.3
  139.0 0.6 constant_dynamic-update-slice_fusion
  139.6 0.0 collective-permute-done.2
  139.6 0.0 copy-start.2
  139.6 45.7 %add_convert_fusion = bf16[2560,2048]{1,0:T(8,128)(2,1)S(1)} fusion(bf16[2560,2048]{1,0:T(8,128)(2,1)} %convert_element_type.37, bf16[4,2048]{1,0:T(4,128)(2,1)S(1)} %collective-permute-done.2, bf16[2564,2048]{1,0:T(8,128)(2,1)} %constant_dynamic-update-slice_fusion, f32[]{:T(128)} %bitcast.9, f32[]{:T(128)} %bitcast.8, f32[]{:T(128)} %bitcast.7, f32[]{:T(128)} %bitcast.6, ...), kind=kLoop, calls=%fused_computation.2 | loop fusion | flops 204472320 | bytes 62930980 | tf_op jit(solution)/shard_map/convert_element_type | solution.py:48
  185.3 0.0 copy-start.1
  185.3 4.0 %copy-done.1 = bf16[2560,2048]{1,0:T(8,128)(2,1)} copy-done((bf16[2560,2048]{1,0:T(8,128)(2,1)}, bf16[2560,2048]{1,0:T(8,128)(2,1)S(1)}, u32[]{:S(2)}) %copy-start.1) | copy-done | bytes 10485784
  189.3 0.0 copy-done.2
  189.3 4.1 %fusion.10 = f32[2560,128]{1,0:T(8,128)} fusion(bf16[2560,2048]{1,0:T(8,128)(2,1)S(1)} %add_convert_fusion, bf16[2048,128]{1,0:T(8,128)(2,1)S(1)} %copy-done.2), kind=kOutput, calls=%fused_computation.22 | convolution fusion | flops 1342177280 | bytes 12320768 | tf_op jit(solution)/shard_map/dot_general | solution.py:50
  193.3 0.0 reduce-scatter.5.cloned.1.call-update
  193.4 0.0 reduce-scatter.7.cloned.1.call-start
  193.4 0.0 copy-done
  193.4 5.6 %convolution_bitcast_fusion = f32[256,2048]{0,1:T(8,128)S(1)} fusion(bf16[2560,2048]{1,0:T(8,128)(2,1)} %copy-done.1, bf16[2560,256]{1,0:T(8,128)(2,1)S(1)} %copy-done), kind=kOutput, calls=%fused_computation.13 | convolution fusion | flops 2684354560 | bytes 13893632 | tf_op jit(solution)/shard_map/dot_general | solution.py:55
  199.1 1.8 copy.14
  200.9 0.0 reduce-scatter.7.cloned.1.call-update
  200.9 25.8 %reduce-scatter.5.cloned.1.call-done = f32[640,128]{1,0:T(8,128)} async-done(((f32[2560,128]{1,0:T(8,128)}), f32[640,128]{1,0:T(8,128)}) %reduce-scatter.5.cloned.1.call-update) | async-done | bytes 327696 | tf_op jit(solution)/shard_map/reduce_scatter | solution.py:49
  226.8 43.9 %reduce-scatter.7.cloned.1.call-done = f32[32,2048]{1,0:T(8,128)} async-done(((f32[256,2048]{1,0:T(8,128)}), f32[32,2048]{1,0:T(8,128)}) %reduce-scatter.7.cloned.1.call-update) | async-done | bytes 262160
  (5 shorter events, 0.1 us)
Async XLA Ops:
  7.2 186.2 %copy-start = (bf16[2560,256]{1,0:T(8,128)(2,1)S(1)}, bf16[2560,256]{1,0:T(8,128)(2,1)}, u32[]{:S(2)}) copy-start(bf16[2560,256]{1,0:T(8,128)(2,1)} %param.9) | copy-start | bytes 3932164
  7.2 219.6 %reduce-scatter.5.cloned.1.call-start = ((), (), s32[]{:S(2)}) async-start(), calls=%async_computation.2 | async-start | bytes 1638400 | tf_op jit(solution)/shard_map/reduce_scatter | solution.py:49
  9.1 11.9 %collective-permute-start = (bf16[2560,64]{0,1:T(8,128)(2,1)S(1)}, bf16[2560,64]{0,1:T(8,128)(2,1)S(1)}, u32[]{:S(2)}, u32[]{:S(2)}) collective-permute-start(bf16[2560,64]{0,1:T(8,128)(2,1)S(1)} %copy.16), channel_id=1, source_target_pairs={{0,1},{1,2},{2,3},{4,5},{5,6},{6,7},{8,9},{9,10},{10,11},{12,13},{... | collective-permute-start | bytes 983048 | tf_op jit(solution)/shard_map/ppermute | solution.py:14
  14.3 11.1 %collective-permute-start.1 = (bf16[2560,64]{0,1:T(8,128)(2,1)S(1)}, bf16[2560,64]{0,1:T(8,128)(2,1)S(1)}, u32[]{:S(2)}, u32[]{:S(2)}) collective-permute-start(bf16[2560,64]{0,1:T(8,128)(2,1)S(1)} %copy.17), channel_id=1, source_target_pairs={{1,0},{2,1},{3,2},{5,4},{6,5},{7,6},{9,8},{10,9},{11,10},{13,12},{... | collective-permute-start | bytes 983048 | tf_op jit(solution)/shard_map/ppermute | solution.py:17
  124.3 14.7 %collective-permute-start.3 = (bf16[4,2048]{1,0:T(4,128)(2,1)S(1)}, bf16[4,2048]{1,0:T(4,128)(2,1)S(1)}, u32[]{:S(2)}, u32[]{:S(2)}) collective-permute-start(bf16[4,2048]{1,0:T(4,128)(2,1)S(1)} %slice.114), channel_id=1, source_target_pairs={{4,0},{8,4},{12,8},{16,12},{20,16},{24,20},{28,24},{5,1},{9,5},{13... | collective-permute-start | bytes 49160 | tf_op jit(solution)/shard_map/ppermute | solution.py:17
  135.7 3.9 %collective-permute-start.2 = (bf16[4,2048]{1,0:T(4,128)(2,1)S(1)}, bf16[4,2048]{1,0:T(4,128)(2,1)S(1)}, u32[]{:S(2)}, u32[]{:S(2)}) collective-permute-start(bf16[4,2048]{1,0:T(4,128)(2,1)S(1)} %slice.103), channel_id=1, source_target_pairs={{0,4},{4,8},{8,12},{12,16},{16,20},{20,24},{24,28},{1,5},{5,9},{9,... | collective-permute-start | bytes 49160 | tf_op jit(solution)/shard_map/ppermute | solution.py:14
  139.6 49.7 %copy-start.2 = (bf16[2048,128]{1,0:T(8,128)(2,1)S(1)}, bf16[2048,128]{1,0:T(8,128)(2,1)}, u32[]{:S(2)}) copy-start(bf16[2048,128]{1,0:T(8,128)(2,1)} %param.8) | copy-start | bytes 1572868
  185.3 4.0 %copy-start.1 = (bf16[2560,2048]{1,0:T(8,128)(2,1)}, bf16[2560,2048]{1,0:T(8,128)(2,1)S(1)}, u32[]{:S(2)}) copy-start(bf16[2560,2048]{1,0:T(8,128)(2,1)S(1)} %add_convert_fusion) | copy-start | bytes 31457284
  193.4 77.3 %reduce-scatter.7.cloned.1.call-start = ((), (), s32[]{:S(2)}) async-start(), calls=%async_computation.3 | async-start | bytes 2359296
Sparse Core Ops, SparseCore 0:
  193.5 33.2 reduce-scatter.4
  230.6 40.0 reduce-scatter.6
where the time goes:
time: 279 us; the launch traced here: 278 us
  waiting for transfers between devices  76.5 us (27%)
  local copies, waits for them, and re-layouts  72.1 us (26%)
  other arithmetic  67.5 us (24%)
  matrix products  36.4 us (13%)
  between operations  14.2 us (5%)
  starting transfers between devices  10.8 us (4%)
    convert_element_type x1, other arithmetic, on_device(): mixed_field = summed.astype(jnp.bfloat16)  45.7 us
    unnamed x3, waiting for transfers between devices  44 us
    reduce_scatter x1, waiting for transfers between devices, on_device(): lax.psum_scatter(jnp.dot(mixed_field, range_probe, preferred_element_type...  25.8 us
    concatenate x1, other arithmetic, with_halo(): block = jnp.concatenate([low, block, high], axis=dim)  21.8 us
    reshape x1, local copies, waits for them, and re-layouts, apply_band(): low_part = padded[:, :length].reshape(-1, 128)  16.5 us
    reshape x1, local copies, waits for them, and re-layouts, apply_band(): high_part = padded[:, 128:length + 128].reshape(-1, 128)  16.5 us
    unnamed x10, local copies, waits for them, and re-layouts  16.5 us
    convert_element_type x1, local copies, waits for them, and re-layouts, on_device(): filtered = apply_band(padded, band_matrix, samples).astype(jnp.bfloat16)  16.3 us
  transfers between devices with their start and end apart: 6, of which 4 were waited for; matrix products, arithmetic and copies ran while one was open for 8% of the time, Pallas kernels for 0%

commit v1 on v0

v1 whole, which is shorter than its diff:
```python
import functools

import jax
import jax.numpy as jnp
from jax import lax
from jax.experimental import pallas as pl
from jax.experimental.pallas import tpu as pltpu
from jax.sharding import PartitionSpec as P

TAPS = 129
HALF = 64
CHTAPS = 9
EDGE = 8
F32 = jnp.float32
BF16 = jnp.bfloat16
NT = (((1,), (1,)), ((), ()))
VMEM_LIMIT = 56 << 20

whole = functools.partial(pl.BlockSpec, memory_space=pltpu.VMEM)
smem = functools.partial(pl.BlockSpec, memory_space=pltpu.SMEM)


def split(value):
    high = value.astype(BF16)
    return high, (value - high.astype(F32)).astype(BF16)


def diagonals(row, rows, lanes, shift):
    spread = jnp.broadcast_to(row, (rows, lanes))
    return pltpu.roll(spread, shift % lanes, 1, stride=1, stride_axis=0)


def range_kernel(count, record, row_a, row_b, probe, probe_a, probe_b, taps, *rest):
    outs, (padded, probes, total) = rest[:count], rest[count:]
    step = pl.program_id(0)
    rows, samples = record.shape
    width = probe.shape[1]
    channels = total.shape[0] - 2 * EDGE
    tm, chan = lax.axis_index("tm"), lax.axis_index("chan")

    @pl.when(step == 0)
    def _():
        spread = diagonals(taps[...], 256, 512, -128)[:, :128]
        band = spread.T.astype(BF16)
        odd = lax.rem(tm, 2)
        padded[HALF : HALF + samples, :] = probe[...]
        padded[pl.ds(pl.multiple_of((1 - odd) * (HALF + samples), HALF), HALF), :] = probe_a[...]
        padded[pl.ds(pl.multiple_of(odd * (HALF + samples), HALF), HALF), :] = probe_b[...]
        for block in range(samples // 128):
            filtered = jnp.dot(
                band, padded[128 * block : 128 * block + 256, :], preferred_element_type=F32
            )
            high, low = split(filtered)
            probes[128 * block : 128 * block + 128, :width] = high
            probes[128 * block : 128 * block + 128, width:] = low
        odd = lax.rem(chan, 2)
        edges = jnp.concatenate([row_a[...], row_b[...]], axis=0)
        pair = jnp.dot(edges, probes[...], preferred_element_type=F32)
        sums = pair[:, :width] + pair[:, width:]
        total[pl.ds(pl.multiple_of((1 - odd) * (EDGE + channels), EDGE), EDGE), :] = sums[:EDGE]
        total[pl.ds(pl.multiple_of(odd * (EDGE + channels), EDGE), EDGE), :] = sums[EDGE:]

    pair = jnp.dot(record[...], probes[...], preferred_element_type=F32)
    total[pl.ds(pl.multiple_of(EDGE + step * rows, EDGE), rows), :] = pair[:, :width] + pair[:, width:]

    @pl.when(step == pl.num_programs(0) - 1)
    def _():
        share = channels // count
        for distance in range(count):
            owner = lax.bitwise_xor(tm, distance)
            start = pl.multiple_of(owner * share, EDGE)
            outs[distance][...] = total[pl.ds(start, share + 2 * EDGE), :].astype(
                outs[distance].dtype
            )


def range_partials(record, row_a, row_b, probe, probe_a, probe_b, taps, count):
    channels, samples = record.shape
    width = probe.shape[1]
    rows = channels // 5
    share = channels // count + 2 * EDGE
    return pl.pallas_call(
        functools.partial(range_kernel, count),
        grid=(channels // rows,),
        in_specs=[pl.BlockSpec((rows, samples), lambda i: (i, 0))] + [whole()] * 6,
        out_specs=[whole()] * count,
        out_shape=[
            jax.ShapeDtypeStruct((share, width), F32 if distance == 0 else BF16)
            for distance in range(count)
        ],
        scratch_shapes=[
            pltpu.VMEM((samples + 2 * HALF, width), BF16),
            pltpu.VMEM((samples, 2 * width), BF16),
            pltpu.VMEM((channels + 2 * EDGE, width), F32),
        ],
        compiler_params=pltpu.CompilerParams(vmem_limit_bytes=VMEM_LIMIT),
        cost_estimate=pl.CostEstimate(
            flops=4 * channels * samples * width,
            bytes_accessed=2 * channels * samples,
            transcendentals=0,
        ),
        name="range_partials",
    )(record, row_a, row_b, probe, probe_a, probe_b, taps)


def corange_kernel(
    count, record, row_a, row_b, probe, taps, space, other, mine, padded, filtered, rim, acc, pairs, full
):
    step = pl.program_id(0)
    rows, samples = record.shape
    channels, width = probe.shape
    chan = lax.axis_index("chan")
    odd = lax.rem(chan, 2)

    @pl.when(step == 0)
    def _():
        lane = lax.broadcasted_iota(jnp.int32, (1, 256), 1)
        row = jnp.zeros((1, 256), F32)
        for tap in range(CHTAPS):
            row = jnp.where(lane == tap + 188, space[tap], row)
        band = diagonals(row, 256, 256, 0)[:, :128].T
        bands = jnp.concatenate(list(split(band)), axis=0)
        padded[:192, :] = jnp.zeros((192, width), BF16)
        padded[192 : 192 + channels, :] = probe[...]
        padded[192 + channels :, :] = jnp.zeros((192, width), BF16)

        def block_of(block):
            both = jnp.dot(
                bands, padded[128 * block : 128 * block + 256, :], preferred_element_type=F32
            )
            return (both[:128] + both[128:]).T.astype(BF16)

        last = channels // 128 + 1
        for block in range(1, last):
            filtered[:, 128 * block - 128 : 128 * block] = block_of(block)
        lanes = lax.broadcasted_iota(jnp.int32, (width, 128), 1)
        ends = jnp.where(lanes < 64, block_of(last).astype(F32), block_of(0).astype(F32)).astype(BF16)
        rim[...] = jnp.zeros_like(rim)
        rim[pl.ds(pl.multiple_of(odd * (128 - EDGE), EDGE), EDGE), :] = row_a[...].astype(F32)
        rim[pl.ds(pl.multiple_of((1 - odd) * (128 - EDGE), EDGE), EDGE), :] = row_b[...].astype(F32)
        acc[...] = jnp.dot(ends, rim[...].astype(BF16), preferred_element_type=F32)

    part = filtered[:, pl.ds(pl.multiple_of(step * rows, 128), rows)]
    acc[...] += jnp.dot(part, record[...], preferred_element_type=F32)

    @pl.when(step == pl.num_programs(0) - 1)
    def _():
        band = diagonals(pltpu.roll(jnp.broadcast_to(taps[...], (8, 512)), HALF, 1)[:1], 256, 512, 0).astype(BF16)
        pairs[:, :128] = jnp.zeros((2 * width, 128), BF16)
        pairs[:, 128 + samples :] = jnp.zeros((2 * width, 128), BF16)
        high, low = split(acc[...])
        pairs[:width, 128 : 128 + samples] = high
        pairs[width:, 128 : 128 + samples] = low
        for block in range(samples // 256):
            both = lax.dot_general(
                pairs[:, 256 * block : 256 * block + 512], band, NT, preferred_element_type=F32
            )
            full[:, 256 * block : 256 * block + 256] = both[:width] + both[width:]
        both = lax.dot_general(
            pairs[:, 128:256], band[:128, 256:384], NT, preferred_element_type=F32
        )
        both = both + lax.dot_general(
            pairs[:, samples : 128 + samples], band[:128, :128], NT, preferred_element_type=F32
        )
        full[:, samples:] = both[:width] + both[width:]
        share = width // count
        chip = lax.div(chan, 2)
        for distance in range(count // 2):
            base = 2 * lax.bitwise_xor(chip, distance)
            keep = pl.multiple_of((base + odd) * share, share)
            give = pl.multiple_of((base + 1 - odd) * share, share)
            mine[distance] = full[pl.ds(keep, share), :]
            other[distance] = full[pl.ds(give, share), :].astype(BF16)


def corange_partials(record, row_a, row_b, probe, taps, space, count):
    channels, samples = record.shape
    width = probe.shape[1]
    rows = channels // 5
    shape = (count // 2, width // count, samples + 128)
    return pl.pallas_call(
        functools.partial(corange_kernel, count),
        grid=(channels // rows,),
        in_specs=[pl.BlockSpec((rows, samples), lambda i: (i, 0))] + [whole()] * 4 + [smem()],
        out_specs=[whole()] * 2,
        out_shape=[jax.ShapeDtypeStruct(shape, BF16), jax.ShapeDtypeStruct(shape, F32)],
        scratch_shapes=[
            pltpu.VMEM((channels + 384, width), BF16),
            pltpu.VMEM((width, channels), BF16),
            pltpu.VMEM((128, samples), F32),
            pltpu.VMEM((width, samples), F32),
            pltpu.VMEM((2 * width, samples + 256), BF16),
            pltpu.VMEM((width, samples + 128), F32),
        ],
        compiler_params=pltpu.CompilerParams(vmem_limit_bytes=VMEM_LIMIT),
        cost_estimate=pl.CostEstimate(
            flops=2 * channels * samples * width,
            bytes_accessed=2 * channels * samples,
            transcendentals=0,
        ),
        name="corange_partials",
    )(record, row_a, row_b, probe, taps, space)


def pair_sum_kernel(mine, got, *outs):
    for distance, out in enumerate(outs):
        out[...] = (mine[distance] + got[distance].astype(F32)).astype(out.dtype)


def pair_sum(mine, got):
    count, share, length = mine.shape
    return pl.pallas_call(
        pair_sum_kernel,
        in_specs=[whole()] * 2,
        out_specs=[whole()] * count,
        out_shape=[
            jax.ShapeDtypeStruct((share, length), F32 if distance == 0 else BF16)
            for distance in range(count)
        ],
        compiler_params=pltpu.CompilerParams(vmem_limit_bytes=VMEM_LIMIT),
        name="pair_sum",
    )(mine, got)


def corange_sum_kernel(*refs):
    parts, main, edge = refs[:-2], refs[-2], refs[-1]
    samples = main.shape[1]
    value = parts[0][...]
    for part in parts[1:]:
        value = value + part[...].astype(F32)
    main[...] = value[:, :samples]
    edge[...] = value[:, samples:]


def corange_sum(parts):
    share, length = parts[0].shape
    return pl.pallas_call(
        corange_sum_kernel,
        in_specs=[whole()] * len(parts),
        out_specs=[whole()] * 2,
        out_shape=[
            jax.ShapeDtypeStruct((share, length - 128), F32),
            jax.ShapeDtypeStruct((share, 128), F32),
        ],
        compiler_params=pltpu.CompilerParams(vmem_limit_bytes=VMEM_LIMIT),
        name="corange_sum",
    )(*parts)


def corange_edges_kernel(main, edge_a, edge_b, out):
    odd = lax.rem(lax.axis_index("tm"), 2)
    samples = main.shape[1]
    lane = lax.broadcasted_iota(jnp.int32, edge_a.shape, 1)
    before = jnp.where(odd == 1, edge_a[...], edge_b[...])
    after = jnp.where(odd == 1, edge_b[...], edge_a[...])
    out[...] = main[...]
    out[:, :128] = main[:, :128] + jnp.where(lane < HALF, before, 0.0)
    out[:, samples - 128 :] = main[:, samples - 128 :] + jnp.where(lane >= HALF, after, 0.0)


def corange_edges(main, edge_a, edge_b):
    return pl.pallas_call(
        corange_edges_kernel,
        in_specs=[whole()] * 3,
        out_specs=whole(),
        out_shape=jax.ShapeDtypeStruct(main.shape, F32),
        name="corange_edges",
    )(main, edge_a, edge_b)


def range_sum_kernel(space, *refs):
    parts, out, total = refs[:-2], refs[-2], refs[-1]
    value = parts[0][...]
    for part in parts[1:]:
        value = value + part[...].astype(F32)
    total[...] = value
    share = out.shape[0]
    result = space[0] * total[4 : 4 + share, :]
    for tap in range(1, CHTAPS):
        result = result + space[tap] * total[4 + tap : 4 + tap + share, :]
    out[...] = result


def range_sum(space, parts):
    rows, width = parts[0].shape
    return pl.pallas_call(
        range_sum_kernel,
        in_specs=[smem()] + [whole()] * len(parts),
        out_specs=whole(),
        out_shape=jax.ShapeDtypeStruct((rows - 2 * EDGE, width), F32),
        scratch_shapes=[pltpu.VMEM((rows, width), F32)],
        name="range_sum",
    )(space, *parts)


def swaps(first, second, axis):
    count = lax.axis_size(axis)
    low = [(i, i ^ 1) for i in range(count)]
    high = [(i, i + 1) for i in range(1, count - 1, 2)]
    high = high + [(target, source) for source, target in high]
    return lax.ppermute(first, axis, low), lax.ppermute(second, axis, high)


def ends(block, width, axis):
    even = lax.axis_index(axis) % 2 == 0
    low, high = block[:width], block[-width:]
    return jnp.where(even, high, low), jnp.where(even, low, high)


def on_device(record, fir_taps, space_taps, range_probe, corange_probe):
    n_tm, n_chan = lax.axis_size("tm"), lax.axis_size("chan")
    taps = jnp.pad(fir_taps.astype(F32), (0, 512 - TAPS)).reshape(1, 512)
    row_a, row_b = swaps(*ends(record, EDGE, "chan"), "chan")
    probe_a, probe_b = swaps(*ends(range_probe, HALF, "tm"), "tm")
    shares = range_partials(record, row_a, row_b, range_probe, probe_a, probe_b, taps, n_tm)
    got = [shares[0]]
    for distance in range(n_tm - 1, 0, -1):
        pairs = [(i, i ^ distance) for i in range(n_tm)]
        got.append(lax.ppermute(shares[distance], "tm", pairs))
    other, mine = corange_partials(record, row_a, row_b, corange_probe, taps, space_taps, n_chan)
    other = lax.ppermute(other, "chan", [(i, i ^ 1) for i in range(n_chan)])
    sums = pair_sum(mine, other)
    parts = [sums[0]]
    for distance in range(n_chan // 2 - 1, 0, -1):
        pairs = [(i, i ^ (2 * distance)) for i in range(n_chan)]
        parts.append(lax.ppermute(sums[distance], "chan", pairs))
    main, edge = corange_sum(parts)
    corange_sketch = corange_edges(main, *swaps(edge, edge, "tm"))
    range_sketch = range_sum(space_taps, got)
    return (range_sketch, corange_sketch)


def solution(mesh):
    return jax.shard_map(
        on_device,
        mesh=mesh,
        in_specs=(P("chan", "tm"), P(), P(), P("tm", None), P("chan", None)),
        out_specs=(P(("chan", "tm"), None), P("chan", "tm")),
        check_vma=False,
    )
```

time: 279 us -> 64.5 us (0.23)
  waiting for transfers between devices: 76.5 us -> 6.52 us
  local copies, waits for them, and re-layouts: 72.1 us -> 4.58 us
  other arithmetic: 67.5 us -> 2.77 us
  matrix products: 36.4 us -> 0 us
  Pallas kernels: 0 us -> 28.9 us
  between operations: 14.2 us -> 0.78 us
  starting transfers between devices: 10.8 us -> 20.4 us
    convert_element_type x1 -> x0, other arithmetic: 45.7 us -> none  [on_device(): mixed_field = summed.astype(jnp.bfloat16)]
    unnamed x3 -> x0, waiting for transfers between devices: 44 us -> none
    dot_general x4 -> x0, matrix products: 36.4 us -> none  [the longest x1 15.7 us: apply_band(): jnp.dot(low_part, band_matrix[:128], preferred_element_type=jnp.float32)]
    reshape x3 -> x0, local copies, waits for them, and re-layouts: 33 us -> none  [the longest x1 16.5 us: apply_band(): low_part = padded[:, :length].reshape(-1, 128)]
    pallas_call x0 -> x6, Pallas kernels: none -> 28.9 us  [the longest x1 11.7 us: corange_partials(): pl.pallas_call(functools.partial(corange_kernel, count), grid=(channels /...]
    reduce_scatter x1 -> x0, waiting for transfers between devices: 25.8 us -> none  [on_device(): lax.psum_scatter(jnp.dot(mixed_field, range_probe, preferred_element_type...]
    concatenate x1 -> x0, other arithmetic: 21.8 us -> none  [with_halo(): block = jnp.concatenate([low, block, high], axis=dim)]
    convert_element_type x1 -> x0, local copies, waits for them, and re-layouts: 16.3 us -> none  [on_device(): filtered = apply_band(padded, band_matrix, samples).astype(jnp.bfloat16)]
  transfers between devices with their start and end apart: 6 -> 13, of which waited for: 4 -> 2; matrix products, arithmetic and copies ran while one was open for 8% -> 3% of each run, Pallas kernels for 0% -> 24%
where the time goes in v1:
time: 64.5 us; the launch traced here: 64 us
  Pallas kernels  28.9 us (45%)
  starting transfers between devices  20.4 us (32%)
  waiting for transfers between devices  6.52 us (10%)
  local copies, waits for them, and re-layouts  4.58 us (7%)
  other arithmetic  2.77 us (4%)
  between operations  0.78 us (1%)
    pallas_call x1, Pallas kernels, corange_partials(): pl.pallas_call(functools.partial(corange_kernel, count), grid=(channels /...  11.7 us
    pallas_call x1, Pallas kernels, range_partials(): pl.pallas_call(functools.partial(range_kernel, count), grid=(channels //...  8.99 us
    ppermute x3, waiting for transfers between devices, on_device(): parts.append(lax.ppermute(sums[distance], 'chan', pairs))  6.5 us
    ppermute x6, starting transfers between devices, swaps(): return (lax.ppermute(first, axis, low), lax.ppermute(second, axis, high))  6.46 us
    ppermute x3, starting transfers between devices, on_device(): got.append(lax.ppermute(shares[distance], 'tm', pairs))  5.86 us
    unnamed x30, local copies, waits for them, and re-layouts  4.58 us
    ppermute x1, starting transfers between devices, on_device(): other = lax.ppermute(other, 'chan', [(i, i ^ 1) for i in range(n_chan)])  4.19 us
    ppermute x3, starting transfers between devices, on_device(): parts.append(lax.ppermute(sums[distance], 'chan', pairs))  3.91 us
  transfers between devices with their start and end apart: 13, of which 2 were waited for; matrix products, arithmetic and copies ran while one was open for 3% of the time, Pallas kernels for 24%

profile of v1, /device:TPU:0, one launch (start us, length us, event | category | flops | bytes accessed | tf_op | source)
XLA Modules:
  0.0 64.0 jit_solution(2607608782792446786)
XLA Ops:
  0.6 0.8 %broadcast_select_fusion = (bf16[8,2048]{1,0:T(8,128)(2,1)S(1)}, bf16[8,2048]{1,0:T(8,128)(2,1)S(1)}) fusion(pred[]{:T(512)S(6)} %eq.9, bf16[2560,2048]{1,0:T(8,128)(2,1)} %record.3), kind=kLoop, calls=%fused_computation | loop fusion | flops 32768 | bytes 131073 | tf_op jit(solution)/shard_map/jit(_where)/select_n | solution.py:307
  1.4 0.5 collective-permute-start
  1.9 0.7 %collective-permute-start.1 = (bf16[8,2048]{1,0:T(8,128)(2,1)S(1)}, bf16[8,2048]{1,0:T(8,128)(2,1)S(1)}, u32[]{:S(2)}, u32[]{:S(2)}) collective-permute-start(bf16[8,2048]{1,0:T(8,128)(2,1)S(1)} %get-tuple-element.26), channel_id=1, source_target_pairs={{4,8},{12,16},{20,24},{8,4},{16,12},{24,20},{5,9},{13,17},{21,25},... | collective-permute-start | bytes 98312 | tf_op jit(solution)/shard_map/ppermute | solution.py:301
  2.6 1.2 %pad_convert_fusion = f32[512]{0:T(512)} fusion(bf16[129]{0:T(256)(128)(2,1)} %param.6), kind=kLoop, calls=%fused_computation.4 | loop fusion | flops 512 | bytes 2306 | tf_op jit(solution)/shard_map/reshape | solution.py:312
  3.8 0.0 collective-permute-done.row_a
  3.9 0.0 collective-permute-done.1.row_b
  3.9 0.6 copy-done.7
  4.5 0.0 copy-done.8
  4.5 11.7 %corange_partials.1 = (bf16[4,32,2176]{2,1,0:T(8,128)(2,1)}, f32[4,32,2176]{2,1,0:T(8,128)}) custom-call(bf16[2560,2048]{1,0:T(8,128)(2,1)} %record.3, bf16[8,2048]{1,0:T(8,128)(2,1)} %copy-done.7, bf16[8,2048]{1,0:T(8,128)(2,1)} %copy-done.8, bf16[2560,256]{1,0:T(8,128)(2,1)} %probe.3, f32[1,512]{1,0:T(1,128)} %bitcast.1, f32[9]{0:T(128)} %space.3), custom_call_target="tpu_custom_call" | custom-call | flops 2684354560 | bytes 10485760 | tf_op jit(solution)/shard_map/corange_partials/pallas_call | solution.py:181
  16.2 4.2 %collective-permute-start.7 = (bf16[4,32,2176]{2,1,0:T(8,128)(2,1)}, bf16[4,32,2176]{2,1,0:T(8,128)(2,1)S(1)}, u32[]{:S(2)}, u32[]{:S(2)}) collective-permute-start(bf16[4,32,2176]{2,1,0:T(8,128)(2,1)} %get-tuple-element.19), channel_id=1, source_target_pairs={{0,4},{4,0},{8,12},{12,8},{16,20},{20,16},{24,28},{28,24},{1,5},{5... | collective-permute-start | bytes 1671176 | tf_op jit(solution)/shard_map/ppermute | solution.py:321
  20.4 0.7 %broadcast_select_fusion.2 = (bf16[64,128]{1,0:T(8,128)(2,1)S(1)}, bf16[64,128]{1,0:T(8,128)(2,1)S(1)}) fusion(pred[]{:T(512)S(6)} %eq.10, bf16[2048,128]{1,0:T(8,128)(2,1)} %probe.2), kind=kLoop, calls=%fused_computation.2 | loop fusion | flops 16384 | bytes 65537 | tf_op jit(solution)/shard_map/jit(_where)/select_n | solution.py:307
  21.2 2.3 %collective-permute-start.2 = (bf16[64,128]{1,0:T(8,128)(2,1)S(1)}, bf16[64,128]{1,0:T(8,128)(2,1)S(1)}, u32[]{:S(2)}, u32[]{:S(2)}) collective-permute-start(bf16[64,128]{1,0:T(8,128)(2,1)S(1)} %get-tuple-element.29), channel_id=1, source_target_pairs={{0,1},{1,0},{2,3},{3,2},{4,5},{5,4},{6,7},{7,6},{8,9},{9,8},{10,11... | collective-permute-start | bytes 49160 | tf_op jit(solution)/shard_map/ppermute | solution.py:301
  23.4 0.7 %collective-permute-start.3 = (bf16[64,128]{1,0:T(8,128)(2,1)S(1)}, bf16[64,128]{1,0:T(8,128)(2,1)S(1)}, u32[]{:S(2)}, u32[]{:S(2)}) collective-permute-start(bf16[64,128]{1,0:T(8,128)(2,1)S(1)} %get-tuple-element.28), channel_id=1, source_target_pairs={{1,2},{2,1},{5,6},{6,5},{9,10},{10,9},{13,14},{14,13},{17,18},{18,... | collective-permute-start | bytes 49160 | tf_op jit(solution)/shard_map/ppermute | solution.py:301
  24.1 0.0 collective-permute-done.7.got
  24.1 0.0 copy-start
  24.1 0.8 %copy-done = bf16[4,32,2176]{2,1,0:T(8,128)(2,1)} copy-done((bf16[4,32,2176]{2,1,0:T(8,128)(2,1)}, bf16[4,32,2176]{2,1,0:T(8,128)(2,1)S(1)}, u32[]{:S(2)}) %copy-start) | copy-done | bytes 557080
  24.9 2.3 %pair_sum.1 = (f32[32,2176]{1,0:T(8,128)}, bf16[32,2176]{1,0:T(8,128)(2,1)}, bf16[32,2176]{1,0:T(8,128)(2,1)}, bf16[32,2176]{1,0:T(8,128)(2,1)}) custom-call(f32[4,32,2176]{2,1,0:T(8,128)} %get-tuple-element.18.mine, bf16[4,32,2176]{2,1,0:T(8,128)(2,1)} %copy-done), custom_call_target="tpu_custom_call" | custom-call | tf_op jit(solution)/shard_map/pair_sum/pallas_call | solution.py:212
  27.2 2.4 %collective-permute-start.10 = (bf16[32,2176]{1,0:T(8,128)(2,1)}, bf16[32,2176]{1,0:T(8,128)(2,1)S(1)}, u32[]{:S(2)}, u32[]{:S(2)}) collective-permute-start(bf16[32,2176]{1,0:T(8,128)(2,1)} %get-tuple-element.23), channel_id=1, source_target_pairs={{0,8},{4,12},{8,0},{12,4},{16,24},{20,28},{24,16},{28,20},{1,9},{5... | collective-permute-start | bytes 417800 | tf_op jit(solution)/shard_map/ppermute | solution.py:326
  29.5 0.0 collective-permute-done.2.probe_a
  29.5 0.0 collective-permute-done.3.probe_b
  29.5 0.6 copy-done.9
  30.1 0.6 copy-done.10
  30.7 9.0 %range_partials.1 = (f32[656,128]{1,0:T(8,128)}, bf16[656,128]{1,0:T(8,128)(2,1)}, bf16[656,128]{1,0:T(8,128)(2,1)}, bf16[656,128]{1,0:T(8,128)(2,1)}) custom-call(bf16[2560,2048]{1,0:T(8,128)(2,1)} %record.3, bf16[8,2048]{1,0:T(8,128)(2,1)} %copy-done.7, bf16[8,2048]{1,0:T(8,128)(2,1)} %copy-done.8, bf16[2048,128]{1,0:T(8,128)(2,1)} %probe.2, ...), custom_call_target="tpu_custom_call" | custom-call | flops 2684354560 | bytes 10485760 | tf_op jit(solution)/shard_map/range_partials/pallas_call | solution.py:82
  39.7 2.5 %collective-permute-start.4 = (bf16[656,128]{1,0:T(8,128)(2,1)}, bf16[656,128]{1,0:T(8,128)(2,1)S(1)}, u32[]{:S(2)}, u32[]{:S(2)}) collective-permute-start(bf16[656,128]{1,0:T(8,128)(2,1)} %get-tuple-element.15), channel_id=1, source_target_pairs={{0,3},{1,2},{2,1},{3,0},{4,7},{5,6},{6,5},{7,4},{8,11},{9,10},{10,... | collective-permute-start | bytes 503816 | tf_op jit(solution)/shard_map/ppermute | solution.py:319
  42.2 3.4 %collective-permute-start.5 = (bf16[656,128]{1,0:T(8,128)(2,1)}, bf16[656,128]{1,0:T(8,128)(2,1)S(1)}, u32[]{:S(2)}, u32[]{:S(2)}) collective-permute-start(bf16[656,128]{1,0:T(8,128)(2,1)} %get-tuple-element.16), channel_id=1, source_target_pairs={{0,2},{1,3},{2,0},{3,1},{4,6},{5,7},{6,4},{7,5},{8,10},{9,11},{10,... | collective-permute-start | bytes 503816 | tf_op jit(solution)/shard_map/ppermute | solution.py:319
  45.6 0.0 collective-permute-start.6
  45.6 1.1 %collective-permute-start.8 = (bf16[32,2176]{1,0:T(8,128)(2,1)S(1)}, bf16[32,2176]{1,0:T(8,128)(2,1)S(1)}, u32[]{:S(2)}, u32[]{:S(2)}) collective-permute-start(bf16[32,2176]{1,0:T(8,128)(2,1)S(1)} %copy-done.14), channel_id=1, source_target_pairs={{0,24},{4,28},{8,16},{12,20},{16,8},{20,12},{24,0},{28,4},{1,25},{... | collective-permute-start | bytes 417800 | tf_op jit(solution)/shard_map/ppermute | solution.py:326
  46.6 0.0 collective-permute-done.10.refs_3_
  46.7 0.5 collective-permute-start.9
  47.1 4.5 %collective-permute-done.8.refs_1_ = bf16[32,2176]{1,0:T(8,128)(2,1)S(1)} collective-permute-done((bf16[32,2176]{1,0:T(8,128)(2,1)S(1)}, bf16[32,2176]{1,0:T(8,128)(2,1)S(1)}, u32[]{:S(2)}, u32[]{:S(2)}) %collective-permute-start.8) | collective-permute-done | bytes 139296 | tf_op jit(solution)/shard_map/ppermute | solution.py:326
  51.6 2.0 %collective-permute-done.9.refs_2_ = bf16[32,2176]{1,0:T(8,128)(2,1)S(1)} collective-permute-done((bf16[32,2176]{1,0:T(8,128)(2,1)S(1)}, bf16[32,2176]{1,0:T(8,128)(2,1)S(1)}, u32[]{:S(2)}, u32[]{:S(2)}) %collective-permute-start.9) | collective-permute-done | bytes 139296 | tf_op jit(solution)/shard_map/ppermute | solution.py:326
  53.6 0.6 copy-done.6
  54.3 1.9 %corange_sum.1 = (f32[32,2048]{1,0:T(8,128)}, f32[32,128]{1,0:T(8,128)}) custom-call(f32[32,2176]{1,0:T(8,128)} %get-tuple-element.20.refs_0_, bf16[32,2176]{1,0:T(8,128)(2,1)} %copy-done.5, bf16[32,2176]{1,0:T(8,128)(2,1)} %copy-done.6, bf16[32,2176]{1,0:T(8,128)(2,1)} %copy-done.4), custom_call_target="tpu_custom_call" | custom-call | tf_op jit(solution)/shard_map/corange_sum/pallas_call | solution.py:237
  56.2 1.7 %collective-permute-start.11 = (f32[32,128]{1,0:T(8,128)}, f32[32,128]{1,0:T(8,128)S(1)}, u32[]{:S(2)}, u32[]{:S(2)}) collective-permute-start(f32[32,128]{1,0:T(8,128)} %get-tuple-element.25), channel_id=1, source_target_pairs={{0,1},{1,0},{2,3},{3,2},{4,5},{5,4},{6,7},{7,6},{8,9},{9,8},{10,11... | collective-permute-start | bytes 49160 | tf_op jit(solution)/shard_map/ppermute | solution.py:301
  57.9 0.7 %collective-permute-start.12 = (f32[32,128]{1,0:T(8,128)}, f32[32,128]{1,0:T(8,128)S(1)}, u32[]{:S(2)}, u32[]{:S(2)}) collective-permute-start(f32[32,128]{1,0:T(8,128)} %get-tuple-element.25), channel_id=1, source_target_pairs={{1,2},{2,1},{5,6},{6,5},{9,10},{10,9},{13,14},{14,13},{17,18},{18,... | collective-permute-start | bytes 49160 | tf_op jit(solution)/shard_map/ppermute | solution.py:301
  58.6 0.0 collective-permute-done.4.refs_1_
  58.6 0.0 collective-permute-done.5.refs_2_
  58.6 0.0 copy-start.2
  58.6 0.0 collective-permute-done.6.refs_3_
  58.6 0.0 copy-start.3
  58.6 0.6 copy-done.1
  59.3 0.1 copy-done.2
  59.3 0.0 copy-done.3
  59.4 2.4 %range_sum.1 = f32[640,128]{1,0:T(8,128)} custom-call(f32[9]{0:T(128)} %space.3, f32[656,128]{1,0:T(8,128)} %get-tuple-element.14.refs_0_, bf16[656,128]{1,0:T(8,128)(2,1)} %copy-done.1, bf16[656,128]{1,0:T(8,128)(2,1)} %copy-done.2, bf16[656,128]{1,0:T(8,128)(2,1)} %copy-done.3), custom_call_target="tpu_custom_call" | custom-call | tf_op jit(solution)/shard_map/range_sum/pallas_call | solution.py:286
  61.7 0.0 collective-permute-done.11.edge_a
  61.7 0.0 collective-permute-done.12.edge_b
  61.7 0.6 copy-done.11
  62.3 1.7 %corange_edges.1 = f32[32,2048]{1,0:T(8,128)} custom-call(f32[32,2048]{1,0:T(8,128)} %get-tuple-element.24.main, f32[32,128]{1,0:T(8,128)} %copy-done.11, f32[32,128]{1,0:T(8,128)} %copy-done.12), custom_call_target="tpu_custom_call" | custom-call | tf_op jit(solution)/shard_map/corange_edges/pallas_call | solution.py:262
  (17 shorter events, 0.0 us)
Async XLA Ops:
  1.4 2.4 %collective-permute-start = (bf16[8,2048]{1,0:T(8,128)(2,1)S(1)}, bf16[8,2048]{1,0:T(8,128)(2,1)S(1)}, u32[]{:S(2)}, u32[]{:S(2)}) collective-permute-start(bf16[8,2048]{1,0:T(8,128)(2,1)S(1)} %get-tuple-element.27), channel_id=1, source_target_pairs={{0,4},{4,0},{8,12},{12,8},{16,20},{20,16},{24,28},{28,24},{1,5},{5... | collective-permute-start | bytes 98312 | tf_op jit(solution)/shard_map/ppermute | solution.py:301
  1.9 1.9 %collective-permute-start.1 = (bf16[8,2048]{1,0:T(8,128)(2,1)S(1)}, bf16[8,2048]{1,0:T(8,128)(2,1)S(1)}, u32[]{:S(2)}, u32[]{:S(2)}) collective-permute-start(bf16[8,2048]{1,0:T(8,128)(2,1)S(1)} %get-tuple-element.26), channel_id=1, source_target_pairs={{4,8},{12,16},{20,24},{8,4},{16,12},{24,20},{5,9},{13,17},{21,25},... | collective-permute-start | bytes 98312 | tf_op jit(solution)/shard_map/ppermute | solution.py:301
  3.8 0.6 copy-start.7
  3.9 0.6 copy-start.8
  16.2 7.9 %collective-permute-start.7 = (bf16[4,32,2176]{2,1,0:T(8,128)(2,1)}, bf16[4,32,2176]{2,1,0:T(8,128)(2,1)S(1)}, u32[]{:S(2)}, u32[]{:S(2)}) collective-permute-start(bf16[4,32,2176]{2,1,0:T(8,128)(2,1)} %get-tuple-element.19), channel_id=1, source_target_pairs={{0,4},{4,0},{8,12},{12,8},{16,20},{20,16},{24,28},{28,24},{1,5},{5... | collective-permute-start | bytes 1671176 | tf_op jit(solution)/shard_map/ppermute | solution.py:321
  21.2 8.4 %collective-permute-start.2 = (bf16[64,128]{1,0:T(8,128)(2,1)S(1)}, bf16[64,128]{1,0:T(8,128)(2,1)S(1)}, u32[]{:S(2)}, u32[]{:S(2)}) collective-permute-start(bf16[64,128]{1,0:T(8,128)(2,1)S(1)} %get-tuple-element.29), channel_id=1, source_target_pairs={{0,1},{1,0},{2,3},{3,2},{4,5},{5,4},{6,7},{7,6},{8,9},{9,8},{10,11... | collective-permute-start | bytes 49160 | tf_op jit(solution)/shard_map/ppermute | solution.py:301
  23.4 6.1 %collective-permute-start.3 = (bf16[64,128]{1,0:T(8,128)(2,1)S(1)}, bf16[64,128]{1,0:T(8,128)(2,1)S(1)}, u32[]{:S(2)}, u32[]{:S(2)}) collective-permute-start(bf16[64,128]{1,0:T(8,128)(2,1)S(1)} %get-tuple-element.28), channel_id=1, source_target_pairs={{1,2},{2,1},{5,6},{6,5},{9,10},{10,9},{13,14},{14,13},{17,18},{18,... | collective-permute-start | bytes 49160 | tf_op jit(solution)/shard_map/ppermute | solution.py:301
  24.1 0.8 %copy-start = (bf16[4,32,2176]{2,1,0:T(8,128)(2,1)}, bf16[4,32,2176]{2,1,0:T(8,128)(2,1)S(1)}, u32[]{:S(2)}) copy-start(bf16[4,32,2176]{2,1,0:T(8,128)(2,1)S(1)} %collective-permute-done.7.got) | copy-start | bytes 1671172
  27.1 18.4 %copy-start.14 = (bf16[32,2176]{1,0:T(8,128)(2,1)S(1)}, bf16[32,2176]{1,0:T(8,128)(2,1)}, u32[]{:S(2)}) copy-start(bf16[32,2176]{1,0:T(8,128)(2,1)} %get-tuple-element.21) | copy-start | bytes 417796
  27.2 19.5 %copy-start.13 = (bf16[32,2176]{1,0:T(8,128)(2,1)S(1)}, bf16[32,2176]{1,0:T(8,128)(2,1)}, u32[]{:S(2)}) copy-start(bf16[32,2176]{1,0:T(8,128)(2,1)} %get-tuple-element.22) | copy-start | bytes 417796
  27.2 19.5 %collective-permute-start.10 = (bf16[32,2176]{1,0:T(8,128)(2,1)}, bf16[32,2176]{1,0:T(8,128)(2,1)S(1)}, u32[]{:S(2)}, u32[]{:S(2)}) collective-permute-start(bf16[32,2176]{1,0:T(8,128)(2,1)} %get-tuple-element.23), channel_id=1, source_target_pairs={{0,8},{4,12},{8,0},{12,4},{16,24},{20,28},{24,16},{28,20},{1,9},{5... | collective-permute-start | bytes 417800 | tf_op jit(solution)/shard_map/ppermute | solution.py:326
  29.5 0.6 copy-start.9
  30.1 0.6 copy-start.10
  39.7 18.9 %collective-permute-start.4 = (bf16[656,128]{1,0:T(8,128)(2,1)}, bf16[656,128]{1,0:T(8,128)(2,1)S(1)}, u32[]{:S(2)}, u32[]{:S(2)}) collective-permute-start(bf16[656,128]{1,0:T(8,128)(2,1)} %get-tuple-element.15), channel_id=1, source_target_pairs={{0,3},{1,2},{2,1},{3,0},{4,7},{5,6},{6,5},{7,4},{8,11},{9,10},{10,... | collective-permute-start | bytes 503816 | tf_op jit(solution)/shard_map/ppermute | solution.py:319
  42.2 16.4 %collective-permute-start.5 = (bf16[656,128]{1,0:T(8,128)(2,1)}, bf16[656,128]{1,0:T(8,128)(2,1)S(1)}, u32[]{:S(2)}, u32[]{:S(2)}) collective-permute-start(bf16[656,128]{1,0:T(8,128)(2,1)} %get-tuple-element.16), channel_id=1, source_target_pairs={{0,2},{1,3},{2,0},{3,1},{4,6},{5,7},{6,4},{7,5},{8,10},{9,11},{10,... | collective-permute-start | bytes 503816 | tf_op jit(solution)/shard_map/ppermute | solution.py:319
  45.6 13.1 %collective-permute-start.6 = (bf16[656,128]{1,0:T(8,128)(2,1)}, bf16[656,128]{1,0:T(8,128)(2,1)S(1)}, u32[]{:S(2)}, u32[]{:S(2)}) collective-permute-start(bf16[656,128]{1,0:T(8,128)(2,1)} %get-tuple-element.17), channel_id=1, source_target_pairs={{0,1},{1,0},{2,3},{3,2},{4,5},{5,4},{6,7},{7,6},{8,9},{9,8},{10,11... | collective-permute-start | bytes 503816 | tf_op jit(solution)/shard_map/ppermute | solution.py:319
  45.6 6.1 %collective-permute-start.8 = (bf16[32,2176]{1,0:T(8,128)(2,1)S(1)}, bf16[32,2176]{1,0:T(8,128)(2,1)S(1)}, u32[]{:S(2)}, u32[]{:S(2)}) collective-permute-start(bf16[32,2176]{1,0:T(8,128)(2,1)S(1)} %copy-done.14), channel_id=1, source_target_pairs={{0,24},{4,28},{8,16},{12,20},{16,8},{20,12},{24,0},{28,4},{1,25},{... | collective-permute-start | bytes 417800 | tf_op jit(solution)/shard_map/ppermute | solution.py:326
  46.7 7.0 %copy-start.4 = (bf16[32,2176]{1,0:T(8,128)(2,1)}, bf16[32,2176]{1,0:T(8,128)(2,1)S(1)}, u32[]{:S(2)}) copy-start(bf16[32,2176]{1,0:T(8,128)(2,1)S(1)} %collective-permute-done.10.refs_3_) | copy-start | bytes 417796
  46.7 7.0 %collective-permute-start.9 = (bf16[32,2176]{1,0:T(8,128)(2,1)S(1)}, bf16[32,2176]{1,0:T(8,128)(2,1)S(1)}, u32[]{:S(2)}, u32[]{:S(2)}) collective-permute-start(bf16[32,2176]{1,0:T(8,128)(2,1)S(1)} %copy-done.13), channel_id=1, source_target_pairs={{0,16},{4,20},{8,24},{12,28},{16,0},{20,4},{24,8},{28,12},{1,17},{... | collective-permute-start | bytes 417800 | tf_op jit(solution)/shard_map/ppermute | solution.py:326
  51.6 2.0 %copy-start.5 = (bf16[32,2176]{1,0:T(8,128)(2,1)}, bf16[32,2176]{1,0:T(8,128)(2,1)S(1)}, u32[]{:S(2)}) copy-start(bf16[32,2176]{1,0:T(8,128)(2,1)S(1)} %collective-permute-done.8.refs_1_) | copy-start | bytes 417796
  53.6 0.6 %copy-start.6 = (bf16[32,2176]{1,0:T(8,128)(2,1)}, bf16[32,2176]{1,0:T(8,128)(2,1)S(1)}, u32[]{:S(2)}) copy-start(bf16[32,2176]{1,0:T(8,128)(2,1)S(1)} %collective-permute-done.9.refs_2_) | copy-start | bytes 417796
  56.2 5.5 %collective-permute-start.11 = (f32[32,128]{1,0:T(8,128)}, f32[32,128]{1,0:T(8,128)S(1)}, u32[]{:S(2)}, u32[]{:S(2)}) collective-permute-start(f32[32,128]{1,0:T(8,128)} %get-tuple-element.25), channel_id=1, source_target_pairs={{0,1},{1,0},{2,3},{3,2},{4,5},{5,4},{6,7},{7,6},{8,9},{9,8},{10,11... | collective-permute-start | bytes 49160 | tf_op jit(solution)/shard_map/ppermute | solution.py:301
  57.9 3.8 %collective-permute-start.12 = (f32[32,128]{1,0:T(8,128)}, f32[32,128]{1,0:T(8,128)S(1)}, u32[]{:S(2)}, u32[]{:S(2)}) collective-permute-start(f32[32,128]{1,0:T(8,128)} %get-tuple-element.25), channel_id=1, source_target_pairs={{1,2},{2,1},{5,6},{6,5},{9,10},{10,9},{13,14},{14,13},{17,18},{18,... | collective-permute-start | bytes 49160 | tf_op jit(solution)/shard_map/ppermute | solution.py:301
  58.6 0.7 %copy-start.1 = (bf16[656,128]{1,0:T(8,128)(2,1)}, bf16[656,128]{1,0:T(8,128)(2,1)S(1)}, u32[]{:S(2)}) copy-start(bf16[656,128]{1,0:T(8,128)(2,1)S(1)} %collective-permute-done.4.refs_1_) | copy-start | bytes 503812
  58.6 0.7 %copy-start.2 = (bf16[656,128]{1,0:T(8,128)(2,1)}, bf16[656,128]{1,0:T(8,128)(2,1)S(1)}, u32[]{:S(2)}) copy-start(bf16[656,128]{1,0:T(8,128)(2,1)S(1)} %collective-permute-done.5.refs_2_) | copy-start | bytes 503812
  58.6 0.7 %copy-start.3 = (bf16[656,128]{1,0:T(8,128)(2,1)}, bf16[656,128]{1,0:T(8,128)(2,1)S(1)}, u32[]{:S(2)}) copy-start(bf16[656,128]{1,0:T(8,128)(2,1)S(1)} %collective-permute-done.6.refs_3_) | copy-start | bytes 503812
  61.7 0.6 copy-start.11
  61.7 0.6 copy-start.12

commit v2 on v0

v2 whole, which is shorter than its diff:
```python
import functools

import jax
import jax.numpy as jnp
from jax import lax
from jax.experimental import pallas as pl
from jax.experimental.pallas import tpu as pltpu
from jax.sharding import PartitionSpec as P

TAPS = 129
HALF = 64
CHTAPS = 9
EDGE = 8
CHUNKS = 5
F32 = jnp.float32
BF16 = jnp.bfloat16
NT = (((1,), (1,)), ((), ()))
VMEM_LIMIT = 24 << 20

whole = functools.partial(pl.BlockSpec, memory_space=pltpu.VMEM)
smem = functools.partial(pl.BlockSpec, memory_space=pltpu.SMEM)
anywhere = functools.partial(pl.BlockSpec, memory_space=pl.ANY)
params = pltpu.CompilerParams(vmem_limit_bytes=VMEM_LIMIT)


def near(value):
    return pltpu.with_memory_space_constraint(value, pltpu.VMEM)


def split(value):
    high = value.astype(BF16)
    return high, (value - high.astype(F32)).astype(BF16)


def diagonals(row, rows, lanes, shift):
    spread = jnp.broadcast_to(row, (rows, lanes))
    return pltpu.roll(spread, shift % lanes, 1, stride=1, stride_axis=0)


def far(value):
    return pltpu.with_memory_space_constraint(value, pltpu.HBM)


def quick():
    return pl.CostEstimate(flops=0, bytes_accessed=0, transcendentals=0)


def taps_row(fir):
    taps = fir[...].astype(F32).reshape(1, TAPS)
    return jnp.concatenate([taps, jnp.zeros((1, 512 - TAPS), F32)], axis=1)


def range_part(give, keep, record, row_a, row_b, probe, probe_a, probe_b, fir, padded, probes, total):
    channels, samples = record.shape
    width = probe.shape[1]
    tm, chan = lax.axis_index("tm"), lax.axis_index("chan")
    count = lax.axis_size("tm")
    lead = diagonals(taps_row(fir), 256, 512, -128)[:, :128].T.astype(BF16)
    odd = lax.rem(chan, 2)
    padded[HALF : HALF + samples, :] = probe[...]
    padded[pl.ds(pl.multiple_of(odd * (HALF + samples), HALF), HALF), :] = probe_a[...]
    padded[pl.ds(pl.multiple_of((1 - odd) * (HALF + samples), HALF), HALF), :] = probe_b[...]
    for block in range(samples // 128):
        high, low = split(
            jnp.dot(lead, padded[128 * block : 128 * block + 256, :], preferred_element_type=F32)
        )
        probes[128 * block : 128 * block + 128, :width] = high
        probes[128 * block : 128 * block + 128, width:] = low
    edges = jnp.concatenate([row_a[...], row_b[...]], axis=0)
    pair = jnp.dot(edges, probes[...], preferred_element_type=F32)
    sums = pair[:, :width] + pair[:, width:]
    total[pl.ds(pl.multiple_of((1 - odd) * (EDGE + channels), EDGE), EDGE), :] = sums[:EDGE]
    total[pl.ds(pl.multiple_of(odd * (EDGE + channels), EDGE), EDGE), :] = sums[EDGE:]
    rows = channels // CHUNKS
    @pl.loop(0, CHUNKS)
    def _(step):
        start = pl.multiple_of(step * rows, 16)
        pair = jnp.dot(record[pl.ds(start, rows), :], probes[...], preferred_element_type=F32)
        total[pl.ds(pl.multiple_of(start + EDGE, EDGE), rows), :] = pair[:, :width] + pair[:, width:]

    share = channels // count
    for target, first in ((give, lax.bitwise_xor(tm, 1)), (keep, tm)):
        for index in range(count // 2):
            start = pl.multiple_of(lax.bitwise_xor(first, 2 * index) * share, EDGE)
            target[index] = total[pl.ds(start, share + 2 * EDGE), :].astype(target.dtype)


def corange_part(other, mine, record, row_a, row_b, probe, fir, space, padded, filtered, rim, pairs, full):
    channels, samples = record.shape
    width = probe.shape[1]
    count = lax.axis_size("chan")
    late = pltpu.roll(jnp.broadcast_to(taps_row(fir), (8, 512)), HALF, 1)[:1]
    band = diagonals(late, 256, 512, 0).astype(BF16)
    lane = lax.broadcasted_iota(jnp.int32, (1, 256), 1)
    row = jnp.zeros((1, 256), F32)
    for tap in range(CHTAPS):
        row = jnp.where(lane == tap + 188, space[tap], row)
    both = jnp.concatenate(list(split(diagonals(row, 256, 256, 0)[:, :128].T)), axis=0)
    padded[:192, :] = jnp.zeros((192, width), BF16)
    padded[192 : 192 + channels, :] = probe[...]
    padded[192 + channels :, :] = jnp.zeros((192, width), BF16)

    def block_of(block):
        pair = jnp.dot(both, padded[128 * block : 128 * block + 256, :], preferred_element_type=F32)
        return (pair[:128] + pair[128:]).T

    last = channels // 128 + 1
    for block in range(1, last):
        filtered[:, 128 * block - 128 : 128 * block] = block_of(block).astype(BF16)
    lanes = lax.broadcasted_iota(jnp.int32, (width, 128), 1)
    ends = jnp.where(lanes < 64, block_of(last), block_of(0)).astype(BF16)
    chan = lax.axis_index("chan")
    odd = lax.rem(chan, 2)
    rim[...] = jnp.zeros_like(rim)
    rim[pl.ds(pl.multiple_of(odd * (128 - EDGE), EDGE), EDGE), :] = row_a[...].astype(F32)
    rim[pl.ds(pl.multiple_of((1 - odd) * (128 - EDGE), EDGE), EDGE), :] = row_b[...].astype(F32)
    pairs[:, :128] = jnp.zeros((2 * width, 128), BF16)
    pairs[:, 128 + samples :] = jnp.zeros((2 * width, 128), BF16)
    for block in range(0, samples, 512):
        value = jnp.dot(filtered[...], record[:, block : block + 512], preferred_element_type=F32)
        value = value + jnp.dot(
            ends, rim[:, block : block + 512].astype(BF16), preferred_element_type=F32
        )
        high, low = split(value)
        pairs[:width, 128 + block : 640 + block] = high
        pairs[width:, 128 + block : 640 + block] = low
    for block in range(samples // 256):
        pair = lax.dot_general(
            pairs[:, 256 * block : 256 * block + 512], band, NT, preferred_element_type=F32
        )
        full[:, 256 * block : 256 * block + 256] = pair[:width] + pair[width:]
    pair = lax.dot_general(pairs[:, 128:256], band[:128, 256:384], NT, preferred_element_type=F32)
    pair = pair + lax.dot_general(
        pairs[:, samples : 128 + samples], band[:128, :128], NT, preferred_element_type=F32
    )
    full[:, samples:] = pair[:width] + pair[width:]
    share = width // count
    chip = lax.div(chan, 2)
    for distance in range(count // 2):
        base = 2 * lax.bitwise_xor(chip, distance)
        keep = pl.multiple_of((base + odd) * share, share)
        give = pl.multiple_of((base + 1 - odd) * share, share)
        mine[distance] = full[pl.ds(keep, share), :]
        other[distance] = full[pl.ds(give, share), :].astype(BF16)


def partials_kernel(
    record, row_a, row_b, range_probe, probe_a, probe_b, corange_source, fir, space, other, mine, give, keep,
    corange_probe, sem, *scratch,
):
    copy = pltpu.make_async_copy(corange_source, corange_probe, sem)
    copy.start()
    range_part(give, keep, record, row_a, row_b, range_probe, probe_a, probe_b, fir, *scratch[:3])
    copy.wait()
    corange_part(other, mine, record, row_a, row_b, corange_probe, fir, space, *scratch[3:])


def partials(record, row_a, row_b, range_probe, probe_a, probe_b, corange_probe, fir, space):
    n_tm, n_chan = lax.axis_size("tm"), lax.axis_size("chan")
    channels, samples = record.shape
    sketch, corange = range_probe.shape[1], corange_probe.shape[1]
    shape = (n_chan // 2, corange // n_chan, samples + 128)
    shares = (n_tm // 2, channels // n_tm + 2 * EDGE, sketch)
    return pl.pallas_call(
        partials_kernel,
        in_specs=[whole()] * 6 + [anywhere(), whole(), smem()],
        out_specs=[whole()] * 4,
        out_shape=[
            pltpu.VMEM(shape, BF16),
            pltpu.VMEM(shape, F32),
            pltpu.VMEM(shares, BF16),
            pltpu.VMEM(shares, F32),
        ],
        scratch_shapes=[
            pltpu.VMEM(corange_probe.shape, BF16),
            pltpu.SemaphoreType.DMA,
            pltpu.VMEM((samples + 2 * HALF, sketch), BF16),
            pltpu.VMEM((samples, 2 * sketch), BF16),
            pltpu.VMEM((channels + 2 * EDGE, sketch), F32),
            pltpu.VMEM((channels + 384, corange), BF16),
            pltpu.VMEM((corange, channels), BF16),
            pltpu.VMEM((128, samples), F32),
            pltpu.VMEM((2 * corange, samples + 256), BF16),
            pltpu.VMEM((corange, samples + 128), F32),
        ],
        compiler_params=pltpu.CompilerParams(vmem_limit_bytes=30 << 20),
        cost_estimate=quick(),
        name="partials",
    )(
        near(record), near(row_a), near(row_b), near(range_probe), near(probe_a), near(probe_b),
        far(corange_probe), fir, far(space),
    )


def halve_kernel(held, got, after, give, keep):
    for index in range(keep.shape[0]):
        keep[index] = held[2 * index] + got[2 * index].astype(F32)
        give[index] = (held[2 * index + 1] + got[2 * index + 1].astype(F32)).astype(BF16)


def halve(held, got, after):
    shape = (held.shape[0] // 2, *held.shape[1:])
    return pl.pallas_call(
        halve_kernel,
        in_specs=[whole()] * 2 + [anywhere()],
        out_specs=[whole()] * 2,
        out_shape=[pltpu.VMEM(shape, BF16), pltpu.VMEM(shape, F32)],
        compiler_params=params,
        cost_estimate=quick(),
        name="halve",
    )(held, near(got), after)


def range_exchange(give, keep, after):
    count, distance = lax.axis_size("tm"), 1
    while True:
        got = lax.ppermute(give, "tm", [(i, i ^ distance) for i in range(count)])
        distance *= 2
        if distance == count:
            return keep, got
        give, keep = halve(keep, got, after)


def pair_sum_kernel(mine, got, *outs):
    for distance, out in enumerate(outs):
        out[...] = (mine[distance] + got[distance].astype(F32)).astype(out.dtype)


def pair_sum(mine, got):
    count, share, length = mine.shape
    return pl.pallas_call(
        pair_sum_kernel,
        in_specs=[whole()] * 2,
        out_specs=[whole()] * count,
        out_shape=[
            pltpu.VMEM((share, length), F32 if distance == 0 else BF16) for distance in range(count)
        ],
        compiler_params=params,
        cost_estimate=quick(),
        name="pair_sum",
    )(mine, near(got))


def corange_sum_kernel(*refs):
    parts, main, edge = refs[:-2], refs[-2], refs[-1]
    samples = main.shape[1]
    value = parts[0][...]
    for part in parts[1:]:
        value = value + part[...].astype(F32)
    main[...] = value[:, :samples]
    edge[...] = value[:, samples:]


def corange_sum(parts):
    share, length = parts[0].shape
    return pl.pallas_call(
        corange_sum_kernel,
        in_specs=[whole()] * len(parts),
        out_specs=[whole()] * 2,
        out_shape=[
            pltpu.VMEM((share, length - 128), F32),
            pltpu.VMEM((share, 128), F32),
        ],
        compiler_params=params,
        cost_estimate=quick(),
        name="corange_sum",
    )(*[near(part) for part in parts])


def corange_edges_kernel(main, edge_a, edge_b, out):
    odd = lax.rem(lax.axis_index("tm"), 2)
    samples = main.shape[1]
    lane = lax.broadcasted_iota(jnp.int32, edge_a.shape, 1)
    before = jnp.where(odd == 1, edge_a[...], edge_b[...])
    after = jnp.where(odd == 1, edge_b[...], edge_a[...])
    out[...] = main[...]
    out[:, :128] = main[:, :128] + jnp.where(lane < HALF, before, 0.0)
    out[:, samples - 128 :] = main[:, samples - 128 :] + jnp.where(lane >= HALF, after, 0.0)


def corange_edges(main, edge_a, edge_b):
    return pl.pallas_call(
        corange_edges_kernel,
        in_specs=[whole()] * 3,
        out_specs=whole(),
        out_shape=jax.ShapeDtypeStruct(main.shape, F32),
        compiler_params=params,
        cost_estimate=quick(),
        name="corange_edges",
    )(main, near(edge_a), near(edge_b))


def range_sum_kernel(space, *refs):
    parts, out, total = refs[:-2], refs[-2], refs[-1]
    value = parts[0][0] + parts[1][0].astype(F32)
    rows, width = value.shape
    high, low = split(value)
    total[:rows, :width] = high
    total[:rows, width:] = low
    total[rows:, :] = jnp.zeros((total.shape[0] - rows, 2 * width), BF16)
    lane = lax.broadcasted_iota(jnp.int32, (1, 128), 1)
    row = jnp.zeros((1, 128), F32)
    for tap in range(CHTAPS):
        row = jnp.where(lane == tap + 4, space[tap], row)
    band = jnp.concatenate(list(split(diagonals(row, 64, 128, 0))), axis=0)
    for start in range(0, out.shape[0], 64):
        pair = jnp.dot(band, total[start : start + 128, :], preferred_element_type=F32)
        pair = pair[:64] + pair[64:]
        out[start : start + 64, :] = pair[:, :width] + pair[:, width:]


def range_sum(space, parts):
    _, rows, width = parts[0].shape
    return pl.pallas_call(
        range_sum_kernel,
        in_specs=[smem()] + [whole()] * len(parts),
        out_specs=whole(),
        out_shape=jax.ShapeDtypeStruct((rows - 2 * EDGE, width), F32),
        scratch_shapes=[pltpu.VMEM((rows - 2 * EDGE + 64, 2 * width), BF16)],
        compiler_params=params,
        cost_estimate=quick(),
        name="range_sum",
    )(far(space), *[near(part) for part in parts])


def swaps(first, second, axis):
    count = lax.axis_size(axis)
    low = [(i, i ^ 1) for i in range(count)]
    high = [(i, i + 1) for i in range(1, count - 1, 2)]
    high = high + [(target, source) for source, target in high]
    return lax.ppermute(first, axis, low), lax.ppermute(second, axis, high)


def pick_kernel(record, probe, row_a, row_b, probe_a, sems):
    odd = lax.rem(lax.axis_index("chan"), 2)
    far_row, far_probe = record.shape[0] - EDGE, probe.shape[0] - HALF
    copies = [
        pltpu.make_async_copy(source.at[pl.ds(pl.multiple_of(start, size), size)], target, sems.at[slot])
        for slot, (source, start, size, target) in enumerate(
            [
                (record, (1 - odd) * far_row, EDGE, row_a),
                (record, odd * far_row, EDGE, row_b),
                (probe, (1 - odd) * far_probe, HALF, probe_a),
            ]
        )
    ]
    for copy in copies:
        copy.start()
    for copy in copies:
        copy.wait()


def pick(record, probe):
    rows = pltpu.VMEM((EDGE, record.shape[1]), BF16)
    return pl.pallas_call(
        pick_kernel,
        in_specs=[anywhere()] * 2,
        out_specs=[whole()] * 3,
        out_shape=[rows, rows, pltpu.VMEM((HALF, probe.shape[1]), BF16)],
        scratch_shapes=[pltpu.SemaphoreType.DMA((3,))],
        compiler_params=params,
        cost_estimate=pl.CostEstimate(flops=0, bytes_accessed=4 * record.size, transcendentals=0),
        name="pick",
    )(far(record), far(probe))


def probe_ends(edge):
    n_tm, n_chan = lax.axis_size("tm"), lax.axis_size("chan")
    pairs = []
    for chan in range(n_chan):
        for tm in range(n_tm - 1):
            low, high = chan * n_tm + tm, chan * n_tm + tm + 1
            pairs.append((low, high) if chan % 2 == 0 else (high, low))
    got = lax.ppermute(edge, ("chan", "tm"), pairs)
    return got, lax.ppermute(got, "chan", [(i, i ^ 1) for i in range(n_chan)])


def on_device(record, fir_taps, space_taps, range_probe, corange_probe):
    n_chan = lax.axis_size("chan")
    row_a, row_b, edge = pick(record, range_probe)
    probe_a, probe_b = probe_ends(edge)
    row_a, row_b = swaps(row_a, row_b, "chan")
    fir = far(fir_taps)
    other, mine, give, keep = partials(
        record, row_a, row_b, range_probe, probe_a, probe_b, corange_probe, fir, space_taps
    )
    other = lax.ppermute(other, "chan", [(i, i ^ 1) for i in range(n_chan)])
    sums = pair_sum(mine, other)
    parts = [sums[0]]
    for distance in range(1, n_chan // 2):
        pairs = [(i, i ^ (2 * distance)) for i in range(n_chan)]
        parts.append(lax.ppermute(sums[distance], "chan", pairs))
    main, edge = corange_sum(parts)
    got = range_exchange(give, keep, main)
    corange_sketch = corange_edges(main, *swaps(edge, edge, "tm"))
    range_sketch = range_sum(space_taps, got)
    return (range_sketch, corange_sketch)


def solution(mesh):
    return jax.shard_map(
        on_device,
        mesh=mesh,
        in_specs=(P("chan", "tm"), P(), P(), P("tm", None), P("chan", None)),
        out_specs=(P(("chan", "tm"), None), P("chan", "tm")),
        check_vma=False,
    )
```

time: 279 us -> 48.4 us (0.17)
  local copies, waits for them, and re-layouts: 72.1 us -> 0.01 us
  other arithmetic: 67.5 us -> 0 us
  waiting for transfers between devices: 76.5 us -> 12.1 us
  matrix products: 36.4 us -> 0 us
  Pallas kernels: 0 us -> 14.7 us
  between operations: 14.2 us -> 0.73 us
  starting transfers between devices: 10.8 us -> 20.6 us
    convert_element_type x1 -> x0, other arithmetic: 45.7 us -> none  [on_device(): mixed_field = summed.astype(jnp.bfloat16)]
    unnamed x3 -> x0, waiting for transfers between devices: 44 us -> none
    dot_general x4 -> x0, matrix products: 36.4 us -> none  [the longest x1 15.7 us: apply_band(): jnp.dot(low_part, band_matrix[:128], preferred_element_type=jnp.float32)]
    reshape x3 -> x0, local copies, waits for them, and re-layouts: 33 us -> none  [the longest x1 16.5 us: apply_band(): low_part = padded[:, :length].reshape(-1, 128)]
    reduce_scatter x1 -> x0, waiting for transfers between devices: 25.8 us -> none  [on_device(): lax.psum_scatter(jnp.dot(mixed_field, range_probe, preferred_element_type...]
    concatenate x1 -> x0, other arithmetic: 21.8 us -> none  [with_halo(): block = jnp.concatenate([low, block, high], axis=dim)]
    unnamed x10 -> x4, local copies, waits for them, and re-layouts: 16.5 us -> 0.01 us
    convert_element_type x1 -> x0, local copies, waits for them, and re-layouts: 16.3 us -> none  [on_device(): filtered = apply_band(padded, band_matrix, samples).astype(jnp.bfloat16)]
  transfers between devices with their start and end apart: 6 -> 12, of which waited for: 4 -> 6; matrix products, arithmetic and copies ran while one was open for 8% -> 0% of each run, Pallas kernels for 0% -> 2%
where the time goes in v2:
time: 48.4 us; the launch traced here: 48.1 us
  starting transfers between devices  20.6 us (43%)
  Pallas kernels  14.7 us (30%)
  waiting for transfers between devices  12.1 us (25%)
  between operations  0.73 us (2%)
    pallas_call x1, Pallas kernels, partials(): pl.pallas_call(partials_kernel, in_specs=[whole()] * 6 + [anywhere(), who...  11 us
    ppermute x3, waiting for transfers between devices, on_device(): parts.append(lax.ppermute(sums[distance], 'chan', pairs))  7.1 us
    ppermute x1, starting transfers between devices, probe_ends(): got = lax.ppermute(edge, ('chan', 'tm'), pairs)  5.19 us
    ppermute x2, starting transfers between devices, range_exchange(): got = lax.ppermute(give, 'tm', [(i, i ^ distance) for i in range(count)])  4.23 us
    ppermute x3, starting transfers between devices, on_device(): parts.append(lax.ppermute(sums[distance], 'chan', pairs))  3.96 us
    ppermute x4, starting transfers between devices, swaps(): return (lax.ppermute(first, axis, low), lax.ppermute(second, axis, high))  3.6 us
    ppermute x1, starting transfers between devices, probe_ends(): return (got, lax.ppermute(got, 'chan', [(i, i ^ 1) for i in range(n_chan)]))  2.25 us
    pallas_call x1, Pallas kernels, range_sum(): pl.pallas_call(range_sum_kernel, in_specs=[smem()] + [whole()] * len(part...  1.77 us
  transfers between devices with their start and end apart: 12, of which 6 were waited for; matrix products, arithmetic and copies ran while one was open for 0% of the time, Pallas kernels for 2%

profile of v2, /device:TPU:0, one launch (start us, length us, event | category | flops | bytes accessed | tf_op | source)
XLA Modules:
  0.0 48.1 jit_solution(8735771559682349984)
XLA Ops:
  0.6 0.0 copy-start.1
  0.6 0.0 copy-start
  0.6 1.0 %pick.1 = (bf16[8,2048]{1,0:T(8,128)(2,1)S(1)}, bf16[8,2048]{1,0:T(8,128)(2,1)S(1)}, bf16[64,128]{1,0:T(8,128)(2,1)S(1)}) custom-call(bf16[2560,2048]{1,0:T(8,128)(2,1)} %record.3, bf16[2048,128]{1,0:T(8,128)(2,1)} %range_probe.1), custom_call_target="tpu_custom_call" | custom-call | bytes 20971520 | tf_op jit(solution)/shard_map/pick/pallas_call | solution.py:355
  1.6 5.2 %collective-permute-start.2 = (bf16[64,128]{1,0:T(8,128)(2,1)S(1)}, bf16[64,128]{1,0:T(8,128)(2,1)S(1)}, u32[]{:S(2)}, u32[]{:S(2)}) collective-permute-start(bf16[64,128]{1,0:T(8,128)(2,1)S(1)} %get-tuple-element.19), channel_id=1, source_target_pairs={{0,1},{1,2},{2,3},{5,4},{6,5},{7,6},{8,9},{9,10},{10,11},{13,12},{... | collective-permute-start | bytes 49160 | tf_op jit(solution)/shard_map/ppermute | solution.py:374
  6.8 0.1 collective-permute-start
  6.9 0.7 %collective-permute-start.1 = (bf16[8,2048]{1,0:T(8,128)(2,1)S(1)}, bf16[8,2048]{1,0:T(8,128)(2,1)S(1)}, u32[]{:S(2)}, u32[]{:S(2)}) collective-permute-start(bf16[8,2048]{1,0:T(8,128)(2,1)S(1)} %get-tuple-element.18), channel_id=1, source_target_pairs={{4,8},{12,16},{20,24},{8,4},{16,12},{24,20},{5,9},{13,17},{21,25},... | collective-permute-start | bytes 98312 | tf_op jit(solution)/shard_map/ppermute | solution.py:331
  7.6 0.7 %collective-permute-done.2.probe_a = bf16[64,128]{1,0:T(8,128)(2,1)S(1)} collective-permute-done((bf16[64,128]{1,0:T(8,128)(2,1)S(1)}, bf16[64,128]{1,0:T(8,128)(2,1)S(1)}, u32[]{:S(2)}, u32[]{:S(2)}) %collective-permute-start.2) | collective-permute-done | bytes 16416 | tf_op jit(solution)/shard_map/ppermute | solution.py:374
  8.2 2.3 %collective-permute-start.3 = (bf16[64,128]{1,0:T(8,128)(2,1)S(1)}, bf16[64,128]{1,0:T(8,128)(2,1)S(1)}, u32[]{:S(2)}, u32[]{:S(2)}) collective-permute-start(bf16[64,128]{1,0:T(8,128)(2,1)S(1)} %collective-permute-done.2.probe_a), channel_id=1, source_target_pairs={{0,4},{4,0},{8,12},{12,8},{16,20},{20,16},{24,28},{28,24},{1,5},{5... | collective-permute-start | bytes 49160 | tf_op jit(solution)/shard_map/ppermute | solution.py:375
  10.5 0.8 %collective-permute-done.3.probe_b = bf16[64,128]{1,0:T(8,128)(2,1)S(1)} collective-permute-done((bf16[64,128]{1,0:T(8,128)(2,1)S(1)}, bf16[64,128]{1,0:T(8,128)(2,1)S(1)}, u32[]{:S(2)}, u32[]{:S(2)}) %collective-permute-start.3) | collective-permute-done | bytes 16416 | tf_op jit(solution)/shard_map/ppermute | solution.py:375
  11.3 0.0 collective-permute-done.row_a
  11.3 0.0 collective-permute-done.1.row_b
  11.3 0.0 copy-done.1
  11.4 0.0 copy-done
  11.4 11.0 %partials.1 = (bf16[4,32,2176]{2,1,0:T(8,128)(2,1)S(1)}, f32[4,32,2176]{2,1,0:T(8,128)S(1)}, bf16[2,656,128]{2,1,0:T(8,128)(2,1)S(1)}, f32[2,656,128]{2,1,0:T(8,128)S(1)}) custom-call(bf16[2560,2048]{1,0:T(8,128)(2,1)S(1)} %copy-done, bf16[8,2048]{1,0:T(8,128)(2,1)S(1)} %collective-permute-done.row_a, bf16[8,2048]{1,0:T(8,128)(2,1)S(1)} %collective-permute-done.1.row_b, ...), custom_call_target="tpu_custom_call" | custom-call | tf_op jit(solution)/shard_map/partials/pallas_call | solution.py:164
  22.3 1.4 %collective-permute-start.5 = (bf16[4,32,2176]{2,1,0:T(8,128)(2,1)S(1)}, bf16[4,32,2176]{2,1,0:T(8,128)(2,1)S(1)}, u32[]{:S(2)}, u32[]{:S(2)}) collective-permute-start(bf16[4,32,2176]{2,1,0:T(8,128)(2,1)S(1)} %get-tuple-element.23), channel_id=1, source_target_pairs={{0,4},{4,0},{8,12},{12,8},{16,20},{20,16},{24,28},{28,24},{1,5},{5... | collective-permute-start | bytes 1671176 | tf_op jit(solution)/shard_map/ppermute | solution.py:387
  23.7 1.6 %collective-permute-start.4 = (bf16[2,656,128]{2,1,0:T(8,128)(2,1)S(1)}, bf16[2,656,128]{2,1,0:T(8,128)(2,1)S(1)}, u32[]{:S(2)}, u32[]{:S(2)}) collective-permute-start(bf16[2,656,128]{2,1,0:T(8,128)(2,1)S(1)} %get-tuple-element.21), channel_id=1, source_target_pairs={{0,1},{1,0},{2,3},{3,2},{4,5},{5,4},{6,7},{7,6},{8,9},{9,8},{10,11... | collective-permute-start | bytes 1007624 | tf_op jit(solution)/shard_map/ppermute | solution.py:217
  25.3 0.0 collective-permute-done.5.got
  25.3 0.1 pair_sum.1
  25.4 2.4 %collective-permute-start.6 = (bf16[32,2176]{1,0:T(8,128)(2,1)S(1)}, bf16[32,2176]{1,0:T(8,128)(2,1)S(1)}, u32[]{:S(2)}, u32[]{:S(2)}) collective-permute-start(bf16[32,2176]{1,0:T(8,128)(2,1)S(1)} %get-tuple-element.25), channel_id=1, source_target_pairs={{0,8},{4,12},{8,0},{12,4},{16,24},{20,28},{24,16},{28,20},{1,9},{5... | collective-permute-start | bytes 417800 | tf_op jit(solution)/shard_map/ppermute | solution.py:392
  27.8 0.5 %collective-permute-start.7 = (bf16[32,2176]{1,0:T(8,128)(2,1)S(1)}, bf16[32,2176]{1,0:T(8,128)(2,1)S(1)}, u32[]{:S(2)}, u32[]{:S(2)}) collective-permute-start(bf16[32,2176]{1,0:T(8,128)(2,1)S(1)} %get-tuple-element.26), channel_id=1, source_target_pairs={{0,16},{4,20},{8,24},{12,28},{16,0},{20,4},{24,8},{28,12},{1,17},{... | collective-permute-start | bytes 417800 | tf_op jit(solution)/shard_map/ppermute | solution.py:392
  28.3 1.1 %collective-permute-start.8 = (bf16[32,2176]{1,0:T(8,128)(2,1)S(1)}, bf16[32,2176]{1,0:T(8,128)(2,1)S(1)}, u32[]{:S(2)}, u32[]{:S(2)}) collective-permute-start(bf16[32,2176]{1,0:T(8,128)(2,1)S(1)} %get-tuple-element.27), channel_id=1, source_target_pairs={{0,24},{4,28},{8,16},{12,20},{16,8},{20,12},{24,0},{28,4},{1,25},{... | collective-permute-start | bytes 417800 | tf_op jit(solution)/shard_map/ppermute | solution.py:392
  29.4 3.0 %collective-permute-done.6.refs_1_ = bf16[32,2176]{1,0:T(8,128)(2,1)S(1)} collective-permute-done((bf16[32,2176]{1,0:T(8,128)(2,1)S(1)}, bf16[32,2176]{1,0:T(8,128)(2,1)S(1)}, u32[]{:S(2)}, u32[]{:S(2)}) %collective-permute-start.6) | collective-permute-done | bytes 139296 | tf_op jit(solution)/shard_map/ppermute | solution.py:392
  32.3 4.1 %collective-permute-done.7.refs_2_ = bf16[32,2176]{1,0:T(8,128)(2,1)S(1)} collective-permute-done((bf16[32,2176]{1,0:T(8,128)(2,1)S(1)}, bf16[32,2176]{1,0:T(8,128)(2,1)S(1)}, u32[]{:S(2)}, u32[]{:S(2)}) %collective-permute-start.7) | collective-permute-done | bytes 139296 | tf_op jit(solution)/shard_map/ppermute | solution.py:392
  36.5 0.0 collective-permute-done.8.refs_3_
  36.5 0.1 corange_sum.1
  36.5 0.0 collective-permute-done.4.got
  36.6 0.1 halve.1
  36.6 2.7 %collective-permute-start.9 = (bf16[1,656,128]{2,1,0:T(8,128)(2,1)S(1)}, bf16[1,656,128]{2,1,0:T(8,128)(2,1)S(1)}, u32[]{:S(2)}, u32[]{:S(2)}) collective-permute-start(bf16[1,656,128]{2,1,0:T(8,128)(2,1)S(1)} %get-tuple-element.30), channel_id=1, source_target_pairs={{0,2},{1,3},{2,0},{3,1},{4,6},{5,7},{6,4},{7,5},{8,10},{9,11},{10,... | collective-permute-start | bytes 503816 | tf_op jit(solution)/shard_map/ppermute | solution.py:217
  39.3 0.7 %collective-permute-start.11 = (f32[32,128]{1,0:T(8,128)S(1)}, f32[32,128]{1,0:T(8,128)S(1)}, u32[]{:S(2)}, u32[]{:S(2)}) collective-permute-start(f32[32,128]{1,0:T(8,128)S(1)} %get-tuple-element.31), channel_id=1, source_target_pairs={{1,2},{2,1},{5,6},{6,5},{9,10},{10,9},{13,14},{14,13},{17,18},{18,... | collective-permute-start | bytes 49160 | tf_op jit(solution)/shard_map/ppermute | solution.py:331
  40.0 2.2 %collective-permute-start.10 = (f32[32,128]{1,0:T(8,128)S(1)}, f32[32,128]{1,0:T(8,128)S(1)}, u32[]{:S(2)}, u32[]{:S(2)}) collective-permute-start(f32[32,128]{1,0:T(8,128)S(1)} %get-tuple-element.31), channel_id=1, source_target_pairs={{0,1},{1,0},{2,3},{3,2},{4,5},{5,4},{6,7},{7,6},{8,9},{9,8},{10,11... | collective-permute-start | bytes 49160 | tf_op jit(solution)/shard_map/ppermute | solution.py:331
  42.2 0.0 collective-permute-done.11.edge_b
  42.2 1.7 %collective-permute-done.10.edge_a = f32[32,128]{1,0:T(8,128)S(1)} collective-permute-done((f32[32,128]{1,0:T(8,128)S(1)}, f32[32,128]{1,0:T(8,128)S(1)}, u32[]{:S(2)}, u32[]{:S(2)}) %collective-permute-start.10) | collective-permute-done | bytes 16416 | tf_op jit(solution)/shard_map/ppermute | solution.py:331
  43.9 0.7 %corange_edges.1 = f32[32,2048]{1,0:T(8,128)} custom-call(f32[32,2048]{1,0:T(8,128)S(1)} %get-tuple-element.28.after.main, f32[32,128]{1,0:T(8,128)S(1)} %collective-permute-done.10.edge_a, f32[32,128]{1,0:T(8,128)S(1)} %collective-permute-done.11.edge_b), custom_call_target="tpu_custom_call" | custom-call | tf_op jit(solution)/shard_map/corange_edges/pallas_call | solution.py:282
  44.6 1.8 %collective-permute-done.9.refs_1_ = bf16[1,656,128]{2,1,0:T(8,128)(2,1)S(1)} collective-permute-done((bf16[1,656,128]{2,1,0:T(8,128)(2,1)S(1)}, bf16[1,656,128]{2,1,0:T(8,128)(2,1)S(1)}, u32[]{:S(2)}, u32[]{:S(2)}) %collective-permute-start.9) | collective-permute-done | bytes 167968 | tf_op jit(solution)/shard_map/ppermute | solution.py:217
  46.4 1.8 %range_sum.1 = f32[640,128]{1,0:T(8,128)} custom-call(f32[9]{0:T(128)} %space.3, f32[1,656,128]{2,1,0:T(8,128)S(1)} %get-tuple-element.29.refs_0_, bf16[1,656,128]{2,1,0:T(8,128)(2,1)S(1)} %collective-permute-done.9.refs_1_), custom_call_target="tpu_custom_call" | custom-call | tf_op jit(solution)/shard_map/range_sum/pallas_call | solution.py:314
Async XLA Ops:
  0.6 10.7 %copy-start.1 = (bf16[2048,128]{1,0:T(8,128)(2,1)S(1)}, bf16[2048,128]{1,0:T(8,128)(2,1)}, u32[]{:S(2)}) copy-start(bf16[2048,128]{1,0:T(8,128)(2,1)} %range_probe.1) | copy-start | bytes 1572868
  0.6 10.7 %copy-start = (bf16[2560,2048]{1,0:T(8,128)(2,1)S(1)}, bf16[2560,2048]{1,0:T(8,128)(2,1)}, u32[]{:S(2)}) copy-start(bf16[2560,2048]{1,0:T(8,128)(2,1)} %record.3) | copy-start | bytes 31457284
  1.6 6.6 %collective-permute-start.2 = (bf16[64,128]{1,0:T(8,128)(2,1)S(1)}, bf16[64,128]{1,0:T(8,128)(2,1)S(1)}, u32[]{:S(2)}, u32[]{:S(2)}) collective-permute-start(bf16[64,128]{1,0:T(8,128)(2,1)S(1)} %get-tuple-element.19), channel_id=1, source_target_pairs={{0,1},{1,2},{2,3},{5,4},{6,5},{7,6},{8,9},{9,10},{10,11},{13,12},{... | collective-permute-start | bytes 49160 | tf_op jit(solution)/shard_map/ppermute | solution.py:374
  6.8 4.5 %collective-permute-start = (bf16[8,2048]{1,0:T(8,128)(2,1)S(1)}, bf16[8,2048]{1,0:T(8,128)(2,1)S(1)}, u32[]{:S(2)}, u32[]{:S(2)}) collective-permute-start(bf16[8,2048]{1,0:T(8,128)(2,1)S(1)} %get-tuple-element.17), channel_id=1, source_target_pairs={{0,4},{4,0},{8,12},{12,8},{16,20},{20,16},{24,28},{28,24},{1,5},{5... | collective-permute-start | bytes 98312 | tf_op jit(solution)/shard_map/ppermute | solution.py:331
  6.9 4.4 %collective-permute-start.1 = (bf16[8,2048]{1,0:T(8,128)(2,1)S(1)}, bf16[8,2048]{1,0:T(8,128)(2,1)S(1)}, u32[]{:S(2)}, u32[]{:S(2)}) collective-permute-start(bf16[8,2048]{1,0:T(8,128)(2,1)S(1)} %get-tuple-element.18), channel_id=1, source_target_pairs={{4,8},{12,16},{20,24},{8,4},{16,12},{24,20},{5,9},{13,17},{21,25},... | collective-permute-start | bytes 98312 | tf_op jit(solution)/shard_map/ppermute | solution.py:331
  8.2 3.1 %collective-permute-start.3 = (bf16[64,128]{1,0:T(8,128)(2,1)S(1)}, bf16[64,128]{1,0:T(8,128)(2,1)S(1)}, u32[]{:S(2)}, u32[]{:S(2)}) collective-permute-start(bf16[64,128]{1,0:T(8,128)(2,1)S(1)} %collective-permute-done.2.probe_a), channel_id=1, source_target_pairs={{0,4},{4,0},{8,12},{12,8},{16,20},{20,16},{24,28},{28,24},{1,5},{5... | collective-permute-start | bytes 49160 | tf_op jit(solution)/shard_map/ppermute | solution.py:375
  22.3 3.0 %collective-permute-start.5 = (bf16[4,32,2176]{2,1,0:T(8,128)(2,1)S(1)}, bf16[4,32,2176]{2,1,0:T(8,128)(2,1)S(1)}, u32[]{:S(2)}, u32[]{:S(2)}) collective-permute-start(bf16[4,32,2176]{2,1,0:T(8,128)(2,1)S(1)} %get-tuple-element.23), channel_id=1, source_target_pairs={{0,4},{4,0},{8,12},{12,8},{16,20},{20,16},{24,28},{28,24},{1,5},{5... | collective-permute-start | bytes 1671176 | tf_op jit(solution)/shard_map/ppermute | solution.py:387
  23.7 12.8 %collective-permute-start.4 = (bf16[2,656,128]{2,1,0:T(8,128)(2,1)S(1)}, bf16[2,656,128]{2,1,0:T(8,128)(2,1)S(1)}, u32[]{:S(2)}, u32[]{:S(2)}) collective-permute-start(bf16[2,656,128]{2,1,0:T(8,128)(2,1)S(1)} %get-tuple-element.21), channel_id=1, source_target_pairs={{0,1},{1,0},{2,3},{3,2},{4,5},{5,4},{6,7},{7,6},{8,9},{9,8},{10,11... | collective-permute-start | bytes 1007624 | tf_op jit(solution)/shard_map/ppermute | solution.py:217
  25.4 6.9 %collective-permute-start.6 = (bf16[32,2176]{1,0:T(8,128)(2,1)S(1)}, bf16[32,2176]{1,0:T(8,128)(2,1)S(1)}, u32[]{:S(2)}, u32[]{:S(2)}) collective-permute-start(bf16[32,2176]{1,0:T(8,128)(2,1)S(1)} %get-tuple-element.25), channel_id=1, source_target_pairs={{0,8},{4,12},{8,0},{12,4},{16,24},{20,28},{24,16},{28,20},{1,9},{5... | collective-permute-start | bytes 417800 | tf_op jit(solution)/shard_map/ppermute | solution.py:392
  27.8 8.6 %collective-permute-start.7 = (bf16[32,2176]{1,0:T(8,128)(2,1)S(1)}, bf16[32,2176]{1,0:T(8,128)(2,1)S(1)}, u32[]{:S(2)}, u32[]{:S(2)}) collective-permute-start(bf16[32,2176]{1,0:T(8,128)(2,1)S(1)} %get-tuple-element.26), channel_id=1, source_target_pairs={{0,16},{4,20},{8,24},{12,28},{16,0},{20,4},{24,8},{28,12},{1,17},{... | collective-permute-start | bytes 417800 | tf_op jit(solution)/shard_map/ppermute | solution.py:392
  28.3 8.2 %collective-permute-start.8 = (bf16[32,2176]{1,0:T(8,128)(2,1)S(1)}, bf16[32,2176]{1,0:T(8,128)(2,1)S(1)}, u32[]{:S(2)}, u32[]{:S(2)}) collective-permute-start(bf16[32,2176]{1,0:T(8,128)(2,1)S(1)} %get-tuple-element.27), channel_id=1, source_target_pairs={{0,24},{4,28},{8,16},{12,20},{16,8},{20,12},{24,0},{28,4},{1,25},{... | collective-permute-start | bytes 417800 | tf_op jit(solution)/shard_map/ppermute | solution.py:392
  36.6 9.7 %collective-permute-start.9 = (bf16[1,656,128]{2,1,0:T(8,128)(2,1)S(1)}, bf16[1,656,128]{2,1,0:T(8,128)(2,1)S(1)}, u32[]{:S(2)}, u32[]{:S(2)}) collective-permute-start(bf16[1,656,128]{2,1,0:T(8,128)(2,1)S(1)} %get-tuple-element.30), channel_id=1, source_target_pairs={{0,2},{1,3},{2,0},{3,1},{4,6},{5,7},{6,4},{7,5},{8,10},{9,11},{10,... | collective-permute-start | bytes 503816 | tf_op jit(solution)/shard_map/ppermute | solution.py:217
  39.3 2.9 %collective-permute-start.11 = (f32[32,128]{1,0:T(8,128)S(1)}, f32[32,128]{1,0:T(8,128)S(1)}, u32[]{:S(2)}, u32[]{:S(2)}) collective-permute-start(f32[32,128]{1,0:T(8,128)S(1)} %get-tuple-element.31), channel_id=1, source_target_pairs={{1,2},{2,1},{5,6},{6,5},{9,10},{10,9},{13,14},{14,13},{17,18},{18,... | collective-permute-start | bytes 49160 | tf_op jit(solution)/shard_map/ppermute | solution.py:331
  40.0 3.9 %collective-permute-start.10 = (f32[32,128]{1,0:T(8,128)S(1)}, f32[32,128]{1,0:T(8,128)S(1)}, u32[]{:S(2)}, u32[]{:S(2)}) collective-permute-start(f32[32,128]{1,0:T(8,128)S(1)} %get-tuple-element.31), channel_id=1, source_target_pairs={{0,1},{1,0},{2,3},{3,2},{4,5},{5,4},{6,7},{7,6},{8,9},{9,8},{10,11... | collective-permute-start | bytes 49160 | tf_op jit(solution)/shard_map/ppermute | solution.py:331

commit v3 on v2

--- a/solution.py
+++ b/solution.py
@@ -50,19 +50,74 @@
     return jnp.concatenate([taps, jnp.zeros((1, 512 - TAPS), F32)], axis=1)
 
 
-def range_part(give, keep, record, row_a, row_b, probe, probe_a, probe_b, fir, padded, probes, total):
+def prepare_kernel(source, fir, space, filtered, ends, lead, band, last_band, probe, padded, sem):
+    channels, width = probe.shape
+    copy = pltpu.make_async_copy(source, probe, sem)
+    copy.start()
+    taps = taps_row(fir)
+    lead[...] = diagonals(taps, 256, 512, -128)[:, :128].T.astype(BF16)
+    late = pltpu.roll(jnp.broadcast_to(taps, (8, 512)), HALF, 1)[:1]
+    band[...] = diagonals(late, 256, 512, 0).astype(BF16)
+    lane = lax.broadcasted_iota(jnp.int32, (1, 256), 1)
+    row = jnp.zeros((1, 256), F32)
+    last_row = jnp.zeros((1, 256), F32)
+    for tap in range(CHTAPS):
+        row = jnp.where(lane == tap + 188, space[tap], row)
+        last_row = jnp.where(lane == tap + 4, space[tap], last_row)
+    last_band[...] = jnp.concatenate(list(split(diagonals(last_row[:, :128], 64, 128, 0))), axis=0)
+    both = jnp.concatenate(list(split(diagonals(row, 256, 256, 0)[:, :128].T)), axis=0)
+    padded[:192, :] = jnp.zeros((192, width), BF16)
+    padded[192 + channels :, :] = jnp.zeros((192, width), BF16)
+    copy.wait()
+    padded[192 : 192 + channels, :] = probe[...]
+
+    def block_of(block):
+        pair = jnp.dot(both, padded[128 * block : 128 * block + 256, :], preferred_element_type=F32)
+        return (pair[:128] + pair[128:]).T
+
+    last = channels // 128 + 1
+    for block in range(1, last):
+        filtered[:, 128 * block - 128 : 128 * block] = block_of(block).astype(BF16)
+    lanes = lax.broadcasted_iota(jnp.int32, (width, 128), 1)
+    ends[...] = jnp.where(lanes < 64, block_of(last), block_of(0)).astype(BF16)
+
+
+def prepare(probe, fir, space):
+    channels, width = probe.shape
+    return pl.pallas_call(
+        prepare_kernel,
+        in_specs=[anywhere(), whole(), smem()],
+        out_specs=[whole()] * 5,
+        out_shape=[
+            pltpu.VMEM((width, channels), BF16),
+            pltpu.VMEM((width, 128), BF16),
+            pltpu.VMEM((128, 256), BF16),
+            pltpu.VMEM((256, 512), BF16),
+            pltpu.VMEM((128, 128), BF16),
+        ],
+        scratch_shapes=[
+            pltpu.VMEM(probe.shape, BF16),
+            pltpu.VMEM((channels + 384, width), BF16),
+            pltpu.SemaphoreType.DMA,
+        ],
+        compiler_params=params,
+        cost_estimate=pl.CostEstimate(flops=0, bytes_accessed=8 << 20, transcendentals=0),
+        name="prepare",
+    )(far(probe), fir, far(space))
+
+
+def range_part(give, keep, record, row_a, row_b, probe, probe_a, probe_b, lead, padded, probes, total):
     channels, samples = record.shape
     width = probe.shape[1]
     tm, chan = lax.axis_index("tm"), lax.axis_index("chan")
     count = lax.axis_size("tm")
-    lead = diagonals(taps_row(fir), 256, 512, -128)[:, :128].T.astype(BF16)
     odd = lax.rem(chan, 2)
     padded[HALF : HALF + samples, :] = probe[...]
     padded[pl.ds(pl.multiple_of(odd * (HALF + samples), HALF), HALF), :] = probe_a[...]
     padded[pl.ds(pl.multiple_of((1 - odd) * (HALF + samples), HALF), HALF), :] = probe_b[...]
     for block in range(samples // 128):
         high, low = split(
-            jnp.dot(lead, padded[128 * block : 128 * block + 256, :], preferred_element_type=F32)
+            jnp.dot(lead[...], padded[128 * block : 128 * block + 256, :], preferred_element_type=F32)
         )
         probes[128 * block : 128 * block + 128, :width] = high
         probes[128 * block : 128 * block + 128, width:] = low
@@ -72,11 +127,9 @@
     total[pl.ds(pl.multiple_of((1 - odd) * (EDGE + channels), EDGE), EDGE), :] = sums[:EDGE]
     total[pl.ds(pl.multiple_of(odd * (EDGE + channels), EDGE), EDGE), :] = sums[EDGE:]
     rows = channels // CHUNKS
-    @pl.loop(0, CHUNKS)
-    def _(step):
-        start = pl.multiple_of(step * rows, 16)
-        pair = jnp.dot(record[pl.ds(start, rows), :], probes[...], preferred_element_type=F32)
-        total[pl.ds(pl.multiple_of(start + EDGE, EDGE), rows), :] = pair[:, :width] + pair[:, width:]
+    for start in range(0, channels, rows):
+        pair = jnp.dot(record[start : start + rows, :], probes[...], preferred_element_type=F32)
+        total[EDGE + start : EDGE + start + rows, :] = pair[:, :width] + pair[:, width:]
 
     share = channels // count
     for target, first in ((give, lax.bitwise_xor(tm, 1)), (keep, tm)):
@@ -85,30 +138,10 @@
             target[index] = total[pl.ds(start, share + 2 * EDGE), :].astype(target.dtype)
 
 
-def corange_part(other, mine, record, row_a, row_b, probe, fir, space, padded, filtered, rim, pairs, full):
+def corange_part(other, mine, record, row_a, row_b, filtered, ends, band, rim, pairs, full):
     channels, samples = record.shape
-    width = probe.shape[1]
+    width = filtered.shape[0]
     count = lax.axis_size("chan")
-    late = pltpu.roll(jnp.broadcast_to(taps_row(fir), (8, 512)), HALF, 1)[:1]
-    band = diagonals(late, 256, 512, 0).astype(BF16)
-    lane = lax.broadcasted_iota(jnp.int32, (1, 256), 1)
-    row = jnp.zeros((1, 256), F32)
-    for tap in range(CHTAPS):
-        row = jnp.where(lane == tap + 188, space[tap], row)
-    both = jnp.concatenate(list(split(diagonals(row, 256, 256, 0)[:, :128].T)), axis=0)
-    padded[:192, :] = jnp.zeros((192, width), BF16)
-    padded[192 : 192 + channels, :] = probe[...]
-    padded[192 + channels :, :] = jnp.zeros((192, width), BF16)
-
-    def block_of(block):
-        pair = jnp.dot(both, padded[128 * block : 128 * block + 256, :], preferred_element_type=F32)
-        return (pair[:128] + pair[128:]).T
-
-    last = channels // 128 + 1
-    for block in range(1, last):
-        filtered[:, 128 * block - 128 : 128 * block] = block_of(block).astype(BF16)
-    lanes = lax.broadcasted_iota(jnp.int32, (width, 128), 1)
-    ends = jnp.where(lanes < 64, block_of(last), block_of(0)).astype(BF16)
     chan = lax.axis_index("chan")
     odd = lax.rem(chan, 2)
     rim[...] = jnp.zeros_like(rim)
@@ -119,14 +152,14 @@
     for block in range(0, samples, 512):
         value = jnp.dot(filtered[...], record[:, block : block + 512], preferred_element_type=F32)
         value = value + jnp.dot(
-            ends, rim[:, block : block + 512].astype(BF16), preferred_element_type=F32
+            ends[...], rim[:, block : block + 512].astype(BF16), preferred_element_type=F32
         )
         high, low = split(value)
         pairs[:width, 128 + block : 640 + block] = high
         pairs[width:, 128 + block : 640 + block] = low
     for block in range(samples // 256):
         pair = lax.dot_general(
-            pairs[:, 256 * block : 256 * block + 512], band, NT, preferred_element_type=F32
+            pairs[:, 256 * block : 256 * block + 512], band[...], NT, preferred_element_type=F32
         )
         full[:, 256 * block : 256 * block + 256] = pair[:width] + pair[width:]
     pair = lax.dot_general(pairs[:, 128:256], band[:128, 256:384], NT, preferred_element_type=F32)
@@ -145,25 +178,21 @@
 
 
 def partials_kernel(
-    record, row_a, row_b, range_probe, probe_a, probe_b, corange_source, fir, space, other, mine, give, keep,
-    corange_probe, sem, *scratch,
+    record, row_a, row_b, range_probe, probe_a, probe_b, filtered, ends, lead, band, other, mine, give, keep, *scratch
 ):
-    copy = pltpu.make_async_copy(corange_source, corange_probe, sem)
-    copy.start()
-    range_part(give, keep, record, row_a, row_b, range_probe, probe_a, probe_b, fir, *scratch[:3])
-    copy.wait()
-    corange_part(other, mine, record, row_a, row_b, corange_probe, fir, space, *scratch[3:])
-
-
-def partials(record, row_a, row_b, range_probe, probe_a, probe_b, corange_probe, fir, space):
+    range_part(give, keep, record, row_a, row_b, range_probe, probe_a, probe_b, lead, *scratch[:3])
+    corange_part(other, mine, record, row_a, row_b, filtered, ends, band, *scratch[3:])
+
+
+def partials(record, row_a, row_b, range_probe, probe_a, probe_b, filtered, ends, lead, band):
     n_tm, n_chan = lax.axis_size("tm"), lax.axis_size("chan")
     channels, samples = record.shape
-    sketch, corange = range_probe.shape[1], corange_probe.shape[1]
+    sketch, corange = range_probe.shape[1], filtered.shape[0]
     shape = (n_chan // 2, corange // n_chan, samples + 128)
     shares = (n_tm // 2, channels // n_tm + 2 * EDGE, sketch)
     return pl.pallas_call(
         partials_kernel,
-        in_specs=[whole()] * 6 + [anywhere(), whole(), smem()],
+        in_specs=[whole()] * 10,
         out_specs=[whole()] * 4,
         out_shape=[
             pltpu.VMEM(shape, BF16),
@@ -172,23 +201,19 @@
             pltpu.VMEM(shares, F32),
         ],
         scratch_shapes=[
-            pltpu.VMEM(corange_probe.shape, BF16),
-            pltpu.SemaphoreType.DMA,
             pltpu.VMEM((samples + 2 * HALF, sketch), BF16),
             pltpu.VMEM((samples, 2 * sketch), BF16),
             pltpu.VMEM((channels + 2 * EDGE, sketch), F32),
-            pltpu.VMEM((channels + 384, corange), BF16),
-            pltpu.VMEM((corange, channels), BF16),
             pltpu.VMEM((128, samples), F32),
             pltpu.VMEM((2 * corange, samples + 256), BF16),
             pltpu.VMEM((corange, samples + 128), F32),
         ],
-        compiler_params=pltpu.CompilerParams(vmem_limit_bytes=30 << 20),
+        compiler_params=params,
         cost_estimate=quick(),
         name="partials",
     )(
         near(record), near(row_a), near(row_b), near(range_probe), near(probe_a), near(probe_b),
-        far(corange_probe), fir, far(space),
+        filtered, ends, lead, band,
     )
 
 
@@ -290,7 +315,7 @@
     )(main, near(edge_a), near(edge_b))
 
 
-def range_sum_kernel(space, *refs):
+def range_sum_kernel(band, *refs):
     parts, out, total = refs[:-2], refs[-2], refs[-1]
     value = parts[0][0] + parts[1][0].astype(F32)
     rows, width = value.shape
@@ -298,29 +323,24 @@
     total[:rows, :width] = high
     total[:rows, width:] = low
     total[rows:, :] = jnp.zeros((total.shape[0] - rows, 2 * width), BF16)
-    lane = lax.broadcasted_iota(jnp.int32, (1, 128), 1)
-    row = jnp.zeros((1, 128), F32)
-    for tap in range(CHTAPS):
-        row = jnp.where(lane == tap + 4, space[tap], row)
-    band = jnp.concatenate(list(split(diagonals(row, 64, 128, 0))), axis=0)
     for start in range(0, out.shape[0], 64):
-        pair = jnp.dot(band, total[start : start + 128, :], preferred_element_type=F32)
+        pair = jnp.dot(band[...], total[start : start + 128, :], preferred_element_type=F32)
         pair = pair[:64] + pair[64:]
         out[start : start + 64, :] = pair[:, :width] + pair[:, width:]
 
 
-def range_sum(space, parts):
+def range_sum(band, parts):
     _, rows, width = parts[0].shape
     return pl.pallas_call(
         range_sum_kernel,
-        in_specs=[smem()] + [whole()] * len(parts),
+        in_specs=[whole()] * (1 + len(parts)),
         out_specs=whole(),
         out_shape=jax.ShapeDtypeStruct((rows - 2 * EDGE, width), F32),
         scratch_shapes=[pltpu.VMEM((rows - 2 * EDGE + 64, 2 * width), BF16)],
         compiler_params=params,
         cost_estimate=quick(),
         name="range_sum",
-    )(far(space), *[near(part) for part in parts])
+    )(band, *[near(part) for part in parts])
 
 
 def swaps(first, second, axis):
@@ -381,8 +401,9 @@
     probe_a, probe_b = probe_ends(edge)
     row_a, row_b = swaps(row_a, row_b, "chan")
     fir = far(fir_taps)
+    filtered, ends, lead, band, last_band = prepare(corange_probe, fir, space_taps)
     other, mine, give, keep = partials(
-        record, row_a, row_b, range_probe, probe_a, probe_b, corange_probe, fir, space_taps
+        record, row_a, row_b, range_probe, probe_a, probe_b, filtered, ends, lead, band
     )
     other = lax.ppermute(other, "chan", [(i, i ^ 1) for i in range(n_chan)])
     sums = pair_sum(mine, other)
@@ -393,7 +414,7 @@
     main, edge = corange_sum(parts)
     got = range_exchange(give, keep, main)
     corange_sketch = corange_edges(main, *swaps(edge, edge, "tm"))
-    range_sketch = range_sum(space_taps, got)
+    range_sketch = range_sum(last_band, got)
     return (range_sketch, corange_sketch)
 
 

time: 48.4 us -> 45.7 us (0.944)
  starting transfers between devices: 20.6 us -> 19 us
  Pallas kernels: 14.7 us -> 14 us
    ppermute x1, starting transfers between devices: 1.38 us -> 0.1 us  [on_device(): other = lax.ppermute(other, 'chan', [(i, i ^ 1) for i in range(n_chan)])]
    ppermute x1, waiting for transfers between devices: 0.84 us -> 0.01 us  [probe_ends(): return (got, lax.ppermute(got, 'chan', [(i, i ^ 1) for i in range(n_chan)]))]
    ppermute x2, waiting for transfers between devices: 1.76 us -> 2.52 us  [range_exchange(): got = lax.ppermute(give, 'tm', [(i, i ^ distance) for i in range(count)])]
    pallas_call x2 -> x3, Pallas kernels: 12.7 us -> 12 us  [the longest x1 7.82 us: partials(): pl.pallas_call(partials_kernel, in_specs=[whole()] * 10, out_specs=[whole...]
    ppermute x3, waiting for transfers between devices: 7.1 us -> 6.47 us  [on_device(): parts.append(lax.ppermute(sums[distance], 'chan', pairs))]
  transfers between devices with their start and end apart: 12 -> 12, of which waited for: 6 -> 7; matrix products, arithmetic and copies ran while one was open for 0% -> 0% of each run, Pallas kernels for 2% -> 9%
where the time goes in v3:
time: 45.7 us; the launch traced here: 45.4 us
  starting transfers between devices  19 us (42%)
  Pallas kernels  14 us (31%)
  waiting for transfers between devices  11.7 us (26%)
  between operations  0.77 us (2%)
    pallas_call x1, Pallas kernels, partials(): pl.pallas_call(partials_kernel, in_specs=[whole()] * 10, out_specs=[whole...  7.82 us
    ppermute x3, waiting for transfers between devices, on_device(): parts.append(lax.ppermute(sums[distance], 'chan', pairs))  6.47 us
    ppermute x1, starting transfers between devices, probe_ends(): got = lax.ppermute(edge, ('chan', 'tm'), pairs)  5.19 us
    ppermute x2, starting transfers between devices, range_exchange(): got = lax.ppermute(give, 'tm', [(i, i ^ distance) for i in range(count)])  4.29 us
    ppermute x4, starting transfers between devices, swaps(): return (lax.ppermute(first, axis, low), lax.ppermute(second, axis, high))  3.59 us
    ppermute x3, starting transfers between devices, on_device(): parts.append(lax.ppermute(sums[distance], 'chan', pairs))  3.55 us
    pallas_call x1, Pallas kernels, prepare(): pl.pallas_call(prepare_kernel, in_specs=[anywhere(), whole(), smem()], ou...  3.12 us
    ppermute x2, waiting for transfers between devices, range_exchange(): got = lax.ppermute(give, 'tm', [(i, i ^ distance) for i in range(count)])  2.52 us
  transfers between devices with their start and end apart: 12, of which 7 were waited for; matrix products, arithmetic and copies ran while one was open for 0% of the time, Pallas kernels for 9%

profile of v3, /device:TPU:0, one launch (start us, length us, event | category | flops | bytes accessed | tf_op | source)
XLA Modules:
  0.0 45.4 jit_solution(5007549694766813970)
XLA Ops:
  0.6 0.0 copy-start
  0.6 1.0 %pick.1 = (bf16[8,2048]{1,0:T(8,128)(2,1)S(1)}, bf16[8,2048]{1,0:T(8,128)(2,1)S(1)}, bf16[64,128]{1,0:T(8,128)(2,1)S(1)}) custom-call(bf16[2560,2048]{1,0:T(8,128)(2,1)} %record.3, bf16[2048,128]{1,0:T(8,128)(2,1)} %range_probe.1), custom_call_target="tpu_custom_call" | custom-call | bytes 20971520 | tf_op jit(solution)/shard_map/pick/pallas_call | solution.py:375
  1.6 0.0 copy-start.1
  1.6 5.2 %collective-permute-start.2 = (bf16[64,128]{1,0:T(8,128)(2,1)S(1)}, bf16[64,128]{1,0:T(8,128)(2,1)S(1)}, u32[]{:S(2)}, u32[]{:S(2)}) collective-permute-start(bf16[64,128]{1,0:T(8,128)(2,1)S(1)} %get-tuple-element.25), channel_id=1, source_target_pairs={{0,1},{1,2},{2,3},{5,4},{6,5},{7,6},{8,9},{9,10},{10,11},{13,12},{... | collective-permute-start | bytes 49160 | tf_op jit(solution)/shard_map/ppermute | solution.py:394
  6.8 0.1 collective-permute-start
  6.9 0.7 %collective-permute-start.1 = (bf16[8,2048]{1,0:T(8,128)(2,1)S(1)}, bf16[8,2048]{1,0:T(8,128)(2,1)S(1)}, u32[]{:S(2)}, u32[]{:S(2)}) collective-permute-start(bf16[8,2048]{1,0:T(8,128)(2,1)S(1)} %get-tuple-element.24), channel_id=1, source_target_pairs={{4,8},{12,16},{20,24},{8,4},{16,12},{24,20},{5,9},{13,17},{21,25},... | collective-permute-start | bytes 98312 | tf_op jit(solution)/shard_map/ppermute | solution.py:351
  7.6 0.7 %collective-permute-done.2.probe_a = bf16[64,128]{1,0:T(8,128)(2,1)S(1)} collective-permute-done((bf16[64,128]{1,0:T(8,128)(2,1)S(1)}, bf16[64,128]{1,0:T(8,128)(2,1)S(1)}, u32[]{:S(2)}, u32[]{:S(2)}) %collective-permute-start.2) | collective-permute-done | bytes 16416 | tf_op jit(solution)/shard_map/ppermute | solution.py:394
  8.3 2.3 %collective-permute-start.3 = (bf16[64,128]{1,0:T(8,128)(2,1)S(1)}, bf16[64,128]{1,0:T(8,128)(2,1)S(1)}, u32[]{:S(2)}, u32[]{:S(2)}) collective-permute-start(bf16[64,128]{1,0:T(8,128)(2,1)S(1)} %collective-permute-done.2.probe_a), channel_id=1, source_target_pairs={{0,4},{4,0},{8,12},{12,8},{16,20},{20,16},{24,28},{28,24},{1,5},{5... | collective-permute-start | bytes 49160 | tf_op jit(solution)/shard_map/ppermute | solution.py:395
  10.5 3.1 %prepare.1 = (bf16[256,2560]{1,0:T(8,128)(2,1)S(1)}, bf16[256,128]{1,0:T(8,128)(2,1)S(1)}, bf16[128,256]{1,0:T(8,128)(2,1)S(1)}, bf16[256,512]{1,0:T(8,128)(2,1)S(1)}, bf16[128,128]{1,0:T(8,128)(2,1)S(1)}) custom-call(bf16[2560,256]{1,0:T(8,128)(2,1)} %source.1, bf16[129]{0:T(256)(128)(2,1)} %fir.1, f32[9]{0:T(128)} %space.1), custom_call_target="tpu_custom_call" | custom-call | bytes 8388608 | tf_op jit(solution)/shard_map/prepare/pallas_call | solution.py:87
  13.6 0.0 collective-permute-done.3.probe_b
  13.6 0.0 collective-permute-done.row_a
  13.6 0.0 collective-permute-done.1.row_b
  13.7 0.0 copy-done
  13.7 0.0 copy-done.1
  13.7 7.8 %partials.1 = (bf16[4,32,2176]{2,1,0:T(8,128)(2,1)S(1)}, f32[4,32,2176]{2,1,0:T(8,128)S(1)}, bf16[2,656,128]{2,1,0:T(8,128)(2,1)S(1)}, f32[2,656,128]{2,1,0:T(8,128)S(1)}) custom-call(bf16[2560,2048]{1,0:T(8,128)(2,1)S(1)} %copy-done, bf16[8,2048]{1,0:T(8,128)(2,1)S(1)} %collective-permute-done.row_a, bf16[8,2048]{1,0:T(8,128)(2,1)S(1)} %collective-permute-done.1.row_b, ...), custom_call_target="tpu_custom_call" | custom-call | tf_op jit(solution)/shard_map/partials/pallas_call | solution.py:193
  21.5 0.1 collective-permute-start.5
  21.6 1.6 %collective-permute-start.4 = (bf16[2,656,128]{2,1,0:T(8,128)(2,1)S(1)}, bf16[2,656,128]{2,1,0:T(8,128)(2,1)S(1)}, u32[]{:S(2)}, u32[]{:S(2)}) collective-permute-start(bf16[2,656,128]{2,1,0:T(8,128)(2,1)S(1)} %get-tuple-element.31), channel_id=1, source_target_pairs={{0,1},{1,0},{2,3},{3,2},{4,5},{5,4},{6,7},{7,6},{8,9},{9,8},{10,11... | collective-permute-start | bytes 1007624 | tf_op jit(solution)/shard_map/ppermute | solution.py:242
  23.2 0.3 collective-permute-done.5.got
  23.5 0.1 pair_sum.1
  23.6 1.6 %collective-permute-start.6 = (bf16[32,2176]{1,0:T(8,128)(2,1)S(1)}, bf16[32,2176]{1,0:T(8,128)(2,1)S(1)}, u32[]{:S(2)}, u32[]{:S(2)}) collective-permute-start(bf16[32,2176]{1,0:T(8,128)(2,1)S(1)} %get-tuple-element.35), channel_id=1, source_target_pairs={{0,8},{4,12},{8,0},{12,4},{16,24},{20,28},{24,16},{28,20},{1,9},{5... | collective-permute-start | bytes 417800 | tf_op jit(solution)/shard_map/ppermute | solution.py:413
  25.2 0.7 %collective-permute-start.7 = (bf16[32,2176]{1,0:T(8,128)(2,1)S(1)}, bf16[32,2176]{1,0:T(8,128)(2,1)S(1)}, u32[]{:S(2)}, u32[]{:S(2)}) collective-permute-start(bf16[32,2176]{1,0:T(8,128)(2,1)S(1)} %get-tuple-element.36), channel_id=1, source_target_pairs={{0,16},{4,20},{8,24},{12,28},{16,0},{20,4},{24,8},{28,12},{1,17},{... | collective-permute-start | bytes 417800 | tf_op jit(solution)/shard_map/ppermute | solution.py:413
  25.9 1.3 %collective-permute-start.8 = (bf16[32,2176]{1,0:T(8,128)(2,1)S(1)}, bf16[32,2176]{1,0:T(8,128)(2,1)S(1)}, u32[]{:S(2)}, u32[]{:S(2)}) collective-permute-start(bf16[32,2176]{1,0:T(8,128)(2,1)S(1)} %get-tuple-element.37), channel_id=1, source_target_pairs={{0,24},{4,28},{8,16},{12,20},{16,8},{20,12},{24,0},{28,4},{1,25},{... | collective-permute-start | bytes 417800 | tf_op jit(solution)/shard_map/ppermute | solution.py:413
  27.2 2.7 %collective-permute-done.6.refs_1_ = bf16[32,2176]{1,0:T(8,128)(2,1)S(1)} collective-permute-done((bf16[32,2176]{1,0:T(8,128)(2,1)S(1)}, bf16[32,2176]{1,0:T(8,128)(2,1)S(1)}, u32[]{:S(2)}, u32[]{:S(2)}) %collective-permute-start.6) | collective-permute-done | bytes 139296 | tf_op jit(solution)/shard_map/ppermute | solution.py:413
  29.9 2.2 %collective-permute-done.7.refs_2_ = bf16[32,2176]{1,0:T(8,128)(2,1)S(1)} collective-permute-done((bf16[32,2176]{1,0:T(8,128)(2,1)S(1)}, bf16[32,2176]{1,0:T(8,128)(2,1)S(1)}, u32[]{:S(2)}, u32[]{:S(2)}) %collective-permute-start.7) | collective-permute-done | bytes 139296 | tf_op jit(solution)/shard_map/ppermute | solution.py:413
  32.1 1.6 %collective-permute-done.8.refs_3_ = bf16[32,2176]{1,0:T(8,128)(2,1)S(1)} collective-permute-done((bf16[32,2176]{1,0:T(8,128)(2,1)S(1)}, bf16[32,2176]{1,0:T(8,128)(2,1)S(1)}, u32[]{:S(2)}, u32[]{:S(2)}) %collective-permute-start.8) | collective-permute-done | bytes 139296 | tf_op jit(solution)/shard_map/ppermute | solution.py:413
  33.7 0.1 corange_sum.1
  33.7 0.0 collective-permute-done.4.got
  33.7 0.1 halve.1
  33.8 2.7 %collective-permute-start.9 = (bf16[1,656,128]{2,1,0:T(8,128)(2,1)S(1)}, bf16[1,656,128]{2,1,0:T(8,128)(2,1)S(1)}, u32[]{:S(2)}, u32[]{:S(2)}) collective-permute-start(bf16[1,656,128]{2,1,0:T(8,128)(2,1)S(1)} %get-tuple-element.40), channel_id=1, source_target_pairs={{0,2},{1,3},{2,0},{3,1},{4,6},{5,7},{6,4},{7,5},{8,10},{9,11},{10,... | collective-permute-start | bytes 503816 | tf_op jit(solution)/shard_map/ppermute | solution.py:242
  36.5 0.7 %collective-permute-start.11 = (f32[32,128]{1,0:T(8,128)S(1)}, f32[32,128]{1,0:T(8,128)S(1)}, u32[]{:S(2)}, u32[]{:S(2)}) collective-permute-start(f32[32,128]{1,0:T(8,128)S(1)} %get-tuple-element.41), channel_id=1, source_target_pairs={{1,2},{2,1},{5,6},{6,5},{9,10},{10,9},{13,14},{14,13},{17,18},{18,... | collective-permute-start | bytes 49160 | tf_op jit(solution)/shard_map/ppermute | solution.py:351
  37.1 2.2 %collective-permute-start.10 = (f32[32,128]{1,0:T(8,128)S(1)}, f32[32,128]{1,0:T(8,128)S(1)}, u32[]{:S(2)}, u32[]{:S(2)}) collective-permute-start(f32[32,128]{1,0:T(8,128)S(1)} %get-tuple-element.41), channel_id=1, source_target_pairs={{0,1},{1,0},{2,3},{3,2},{4,5},{5,4},{6,7},{7,6},{8,9},{9,8},{10,11... | collective-permute-start | bytes 49160 | tf_op jit(solution)/shard_map/ppermute | solution.py:351
  39.3 0.0 collective-permute-done.11.edge_b
  39.4 1.7 %collective-permute-done.10.edge_a = f32[32,128]{1,0:T(8,128)S(1)} collective-permute-done((f32[32,128]{1,0:T(8,128)S(1)}, f32[32,128]{1,0:T(8,128)S(1)}, u32[]{:S(2)}, u32[]{:S(2)}) %collective-permute-start.10) | collective-permute-done | bytes 16416 | tf_op jit(solution)/shard_map/ppermute | solution.py:351
  41.1 0.7 %corange_edges.1 = f32[32,2048]{1,0:T(8,128)} custom-call(f32[32,2048]{1,0:T(8,128)S(1)} %get-tuple-element.38.after.main, f32[32,128]{1,0:T(8,128)S(1)} %collective-permute-done.10.edge_a, f32[32,128]{1,0:T(8,128)S(1)} %collective-permute-done.11.edge_b), custom_call_target="tpu_custom_call" | custom-call | tf_op jit(solution)/shard_map/corange_edges/pallas_call | solution.py:307
  41.8 2.5 %collective-permute-done.9.refs_1_ = bf16[1,656,128]{2,1,0:T(8,128)(2,1)S(1)} collective-permute-done((bf16[1,656,128]{2,1,0:T(8,128)(2,1)S(1)}, bf16[1,656,128]{2,1,0:T(8,128)(2,1)S(1)}, u32[]{:S(2)}, u32[]{:S(2)}) %collective-permute-start.9) | collective-permute-done | bytes 167968 | tf_op jit(solution)/shard_map/ppermute | solution.py:242
  44.3 1.1 %range_sum.1 = f32[640,128]{1,0:T(8,128)} custom-call(bf16[128,128]{1,0:T(8,128)(2,1)S(1)} %get-tuple-element.22.band, f32[1,656,128]{2,1,0:T(8,128)S(1)} %get-tuple-element.39.refs_0_, bf16[1,656,128]{2,1,0:T(8,128)(2,1)S(1)} %collective-permute-done.9.refs_1_), custom_call_target="tpu_custom_call" | custom-call | tf_op jit(solution)/shard_map/range_sum/pallas_call | solution.py:334
Async XLA Ops:
  0.6 13.0 %copy-start = (bf16[2560,2048]{1,0:T(8,128)(2,1)S(1)}, bf16[2560,2048]{1,0:T(8,128)(2,1)}, u32[]{:S(2)}) copy-start(bf16[2560,2048]{1,0:T(8,128)(2,1)} %record.3) | copy-start | bytes 31457284
  1.6 12.1 %copy-start.1 = (bf16[2048,128]{1,0:T(8,128)(2,1)S(1)}, bf16[2048,128]{1,0:T(8,128)(2,1)}, u32[]{:S(2)}) copy-start(bf16[2048,128]{1,0:T(8,128)(2,1)} %range_probe.1) | copy-start | bytes 1572868
  1.6 6.6 %collective-permute-start.2 = (bf16[64,128]{1,0:T(8,128)(2,1)S(1)}, bf16[64,128]{1,0:T(8,128)(2,1)S(1)}, u32[]{:S(2)}, u32[]{:S(2)}) collective-permute-start(bf16[64,128]{1,0:T(8,128)(2,1)S(1)} %get-tuple-element.25), channel_id=1, source_target_pairs={{0,1},{1,2},{2,3},{5,4},{6,5},{7,6},{8,9},{9,10},{10,11},{13,12},{... | collective-permute-start | bytes 49160 | tf_op jit(solution)/shard_map/ppermute | solution.py:394
  6.8 6.8 %collective-permute-start = (bf16[8,2048]{1,0:T(8,128)(2,1)S(1)}, bf16[8,2048]{1,0:T(8,128)(2,1)S(1)}, u32[]{:S(2)}, u32[]{:S(2)}) collective-permute-start(bf16[8,2048]{1,0:T(8,128)(2,1)S(1)} %get-tuple-element.23), channel_id=1, source_target_pairs={{0,4},{4,0},{8,12},{12,8},{16,20},{20,16},{24,28},{28,24},{1,5},{5... | collective-permute-start | bytes 98312 | tf_op jit(solution)/shard_map/ppermute | solution.py:351
  6.9 6.7 %collective-permute-start.1 = (bf16[8,2048]{1,0:T(8,128)(2,1)S(1)}, bf16[8,2048]{1,0:T(8,128)(2,1)S(1)}, u32[]{:S(2)}, u32[]{:S(2)}) collective-permute-start(bf16[8,2048]{1,0:T(8,128)(2,1)S(1)} %get-tuple-element.24), channel_id=1, source_target_pairs={{4,8},{12,16},{20,24},{8,4},{16,12},{24,20},{5,9},{13,17},{21,25},... | collective-permute-start | bytes 98312 | tf_op jit(solution)/shard_map/ppermute | solution.py:351
  8.3 5.4 %collective-permute-start.3 = (bf16[64,128]{1,0:T(8,128)(2,1)S(1)}, bf16[64,128]{1,0:T(8,128)(2,1)S(1)}, u32[]{:S(2)}, u32[]{:S(2)}) collective-permute-start(bf16[64,128]{1,0:T(8,128)(2,1)S(1)} %collective-permute-done.2.probe_a), channel_id=1, source_target_pairs={{0,4},{4,0},{8,12},{12,8},{16,20},{20,16},{24,28},{28,24},{1,5},{5... | collective-permute-start | bytes 49160 | tf_op jit(solution)/shard_map/ppermute | solution.py:395
  21.5 2.0 %collective-permute-start.5 = (bf16[4,32,2176]{2,1,0:T(8,128)(2,1)S(1)}, bf16[4,32,2176]{2,1,0:T(8,128)(2,1)S(1)}, u32[]{:S(2)}, u32[]{:S(2)}) collective-permute-start(bf16[4,32,2176]{2,1,0:T(8,128)(2,1)S(1)} %get-tuple-element.33), channel_id=1, source_target_pairs={{0,4},{4,0},{8,12},{12,8},{16,20},{20,16},{24,28},{28,24},{1,5},{5... | collective-permute-start | bytes 1671176 | tf_op jit(solution)/shard_map/ppermute | solution.py:408
  21.6 12.1 %collective-permute-start.4 = (bf16[2,656,128]{2,1,0:T(8,128)(2,1)S(1)}, bf16[2,656,128]{2,1,0:T(8,128)(2,1)S(1)}, u32[]{:S(2)}, u32[]{:S(2)}) collective-permute-start(bf16[2,656,128]{2,1,0:T(8,128)(2,1)S(1)} %get-tuple-element.31), channel_id=1, source_target_pairs={{0,1},{1,0},{2,3},{3,2},{4,5},{5,4},{6,7},{7,6},{8,9},{9,8},{10,11... | collective-permute-start | bytes 1007624 | tf_op jit(solution)/shard_map/ppermute | solution.py:242
  23.6 6.3 %collective-permute-start.6 = (bf16[32,2176]{1,0:T(8,128)(2,1)S(1)}, bf16[32,2176]{1,0:T(8,128)(2,1)S(1)}, u32[]{:S(2)}, u32[]{:S(2)}) collective-permute-start(bf16[32,2176]{1,0:T(8,128)(2,1)S(1)} %get-tuple-element.35), channel_id=1, source_target_pairs={{0,8},{4,12},{8,0},{12,4},{16,24},{20,28},{24,16},{28,20},{1,9},{5... | collective-permute-start | bytes 417800 | tf_op jit(solution)/shard_map/ppermute | solution.py:413
  25.2 6.9 %collective-permute-start.7 = (bf16[32,2176]{1,0:T(8,128)(2,1)S(1)}, bf16[32,2176]{1,0:T(8,128)(2,1)S(1)}, u32[]{:S(2)}, u32[]{:S(2)}) collective-permute-start(bf16[32,2176]{1,0:T(8,128)(2,1)S(1)} %get-tuple-element.36), channel_id=1, source_target_pairs={{0,16},{4,20},{8,24},{12,28},{16,0},{20,4},{24,8},{28,12},{1,17},{... | collective-permute-start | bytes 417800 | tf_op jit(solution)/shard_map/ppermute | solution.py:413
  25.9 7.8 %collective-permute-start.8 = (bf16[32,2176]{1,0:T(8,128)(2,1)S(1)}, bf16[32,2176]{1,0:T(8,128)(2,1)S(1)}, u32[]{:S(2)}, u32[]{:S(2)}) collective-permute-start(bf16[32,2176]{1,0:T(8,128)(2,1)S(1)} %get-tuple-element.37), channel_id=1, source_target_pairs={{0,24},{4,28},{8,16},{12,20},{16,8},{20,12},{24,0},{28,4},{1,25},{... | collective-permute-start | bytes 417800 | tf_op jit(solution)/shard_map/ppermute | solution.py:413
  33.8 10.5 %collective-permute-start.9 = (bf16[1,656,128]{2,1,0:T(8,128)(2,1)S(1)}, bf16[1,656,128]{2,1,0:T(8,128)(2,1)S(1)}, u32[]{:S(2)}, u32[]{:S(2)}) collective-permute-start(bf16[1,656,128]{2,1,0:T(8,128)(2,1)S(1)} %get-tuple-element.40), channel_id=1, source_target_pairs={{0,2},{1,3},{2,0},{3,1},{4,6},{5,7},{6,4},{7,5},{8,10},{9,11},{10,... | collective-permute-start | bytes 503816 | tf_op jit(solution)/shard_map/ppermute | solution.py:242
  36.5 2.9 %collective-permute-start.11 = (f32[32,128]{1,0:T(8,128)S(1)}, f32[32,128]{1,0:T(8,128)S(1)}, u32[]{:S(2)}, u32[]{:S(2)}) collective-permute-start(f32[32,128]{1,0:T(8,128)S(1)} %get-tuple-element.41), channel_id=1, source_target_pairs={{1,2},{2,1},{5,6},{6,5},{9,10},{10,9},{13,14},{14,13},{17,18},{18,... | collective-permute-start | bytes 49160 | tf_op jit(solution)/shard_map/ppermute | solution.py:351
  37.1 3.9 %collective-permute-start.10 = (f32[32,128]{1,0:T(8,128)S(1)}, f32[32,128]{1,0:T(8,128)S(1)}, u32[]{:S(2)}, u32[]{:S(2)}) collective-permute-start(f32[32,128]{1,0:T(8,128)S(1)} %get-tuple-element.41), channel_id=1, source_target_pairs={{0,1},{1,0},{2,3},{3,2},{4,5},{5,4},{6,7},{7,6},{8,9},{9,8},{10,11... | collective-permute-start | bytes 49160 | tf_op jit(solution)/shard_map/ppermute | solution.py:351

commit v4 on v3

--- a/solution.py
+++ b/solution.py
@@ -50,10 +50,8 @@
     return jnp.concatenate([taps, jnp.zeros((1, 512 - TAPS), F32)], axis=1)
 
 
-def prepare_kernel(source, fir, space, filtered, ends, lead, band, last_band, probe, padded, sem):
+def prepare_kernel(probe, fir, space, filtered, ends, lead, band, last_band, padded):
     channels, width = probe.shape
-    copy = pltpu.make_async_copy(source, probe, sem)
-    copy.start()
     taps = taps_row(fir)
     lead[...] = diagonals(taps, 256, 512, -128)[:, :128].T.astype(BF16)
     late = pltpu.roll(jnp.broadcast_to(taps, (8, 512)), HALF, 1)[:1]
@@ -68,25 +66,37 @@
     both = jnp.concatenate(list(split(diagonals(row, 256, 256, 0)[:, :128].T)), axis=0)
     padded[:192, :] = jnp.zeros((192, width), BF16)
     padded[192 + channels :, :] = jnp.zeros((192, width), BF16)
-    copy.wait()
     padded[192 : 192 + channels, :] = probe[...]
 
     def block_of(block):
         pair = jnp.dot(both, padded[128 * block : 128 * block + 256, :], preferred_element_type=F32)
         return (pair[:128] + pair[128:]).T
 
+    count = lax.axis_size("chan")
+    chan = lax.axis_index("chan")
+    share = width // count
+    places = []
+    for owner in range(count):
+        here = lax.rem(chan, 2) == owner % 2
+        place = lax.bitwise_xor(lax.div(chan, 2), owner // 2) + jnp.where(here, count // 2, 0)
+        places.append(pl.multiple_of(place * share, share))
+
+    def put(target, columns, value):
+        for owner, place in enumerate(places):
+            target[pl.ds(place, share), columns] = value[owner * share : (owner + 1) * share, :]
+
     last = channels // 128 + 1
     for block in range(1, last):
-        filtered[:, 128 * block - 128 : 128 * block] = block_of(block).astype(BF16)
+        put(filtered, slice(128 * block - 128, 128 * block), block_of(block).astype(BF16))
     lanes = lax.broadcasted_iota(jnp.int32, (width, 128), 1)
-    ends[...] = jnp.where(lanes < 64, block_of(last), block_of(0)).astype(BF16)
+    put(ends, slice(0, 128), jnp.where(lanes < 64, block_of(last), block_of(0)).astype(BF16))
 
 
 def prepare(probe, fir, space):
     channels, width = probe.shape
     return pl.pallas_call(
         prepare_kernel,
-        in_specs=[anywhere(), whole(), smem()],
+        in_specs=[whole(), whole(), smem()],
         out_specs=[whole()] * 5,
         out_shape=[
             pltpu.VMEM((width, channels), BF16),
@@ -96,14 +106,12 @@
             pltpu.VMEM((128, 128), BF16),
         ],
         scratch_shapes=[
-            pltpu.VMEM(probe.shape, BF16),
             pltpu.VMEM((channels + 384, width), BF16),
-            pltpu.SemaphoreType.DMA,
         ],
         compiler_params=params,
         cost_estimate=pl.CostEstimate(flops=0, bytes_accessed=8 << 20, transcendentals=0),
         name="prepare",
-    )(far(probe), fir, far(space))
+    )(near(probe), fir, far(space))
 
 
 def range_part(give, keep, record, row_a, row_b, probe, probe_a, probe_b, lead, padded, probes, total):
@@ -138,7 +146,7 @@
             target[index] = total[pl.ds(start, share + 2 * EDGE), :].astype(target.dtype)
 
 
-def corange_part(other, mine, record, row_a, row_b, filtered, ends, band, rim, pairs, full):
+def corange_part(other, mine, record, row_a, row_b, filtered, ends, band, rim, pairs):
     channels, samples = record.shape
     width = filtered.shape[0]
     count = lax.axis_size("chan")
@@ -157,24 +165,24 @@
         high, low = split(value)
         pairs[:width, 128 + block : 640 + block] = high
         pairs[width:, 128 + block : 640 + block] = low
-    for block in range(samples // 256):
+    share = width // count
+
+    def leave(columns, value):
+        for index in range(count // 2):
+            other[index, :, columns] = value[index * share : (index + 1) * share].astype(BF16)
+            start = width // 2 + index * share
+            mine[index, :, columns] = value[start : start + share]
+
+    for block in range(0, samples, 256):
         pair = lax.dot_general(
-            pairs[:, 256 * block : 256 * block + 512], band[...], NT, preferred_element_type=F32
+            pairs[:, block : block + 512], band[...], NT, preferred_element_type=F32
         )
-        full[:, 256 * block : 256 * block + 256] = pair[:width] + pair[width:]
+        leave(slice(block, block + 256), pair[:width] + pair[width:])
     pair = lax.dot_general(pairs[:, 128:256], band[:128, 256:384], NT, preferred_element_type=F32)
     pair = pair + lax.dot_general(
         pairs[:, samples : 128 + samples], band[:128, :128], NT, preferred_element_type=F32
     )
-    full[:, samples:] = pair[:width] + pair[width:]
-    share = width // count
-    chip = lax.div(chan, 2)
-    for distance in range(count // 2):
-        base = 2 * lax.bitwise_xor(chip, distance)
-        keep = pl.multiple_of((base + odd) * share, share)
-        give = pl.multiple_of((base + 1 - odd) * share, share)
-        mine[distance] = full[pl.ds(keep, share), :]
-        other[distance] = full[pl.ds(give, share), :].astype(BF16)
+    leave(slice(samples, samples + 128), pair[:width] + pair[width:])
 
 
 def partials_kernel(
@@ -206,7 +214,6 @@
             pltpu.VMEM((channels + 2 * EDGE, sketch), F32),
             pltpu.VMEM((128, samples), F32),
             pltpu.VMEM((2 * corange, samples + 256), BF16),
-            pltpu.VMEM((corange, samples + 128), F32),
         ],
         compiler_params=params,
         cost_estimate=quick(),
@@ -408,7 +415,7 @@
     other = lax.ppermute(other, "chan", [(i, i ^ 1) for i in range(n_chan)])
     sums = pair_sum(mine, other)
     parts = [sums[0]]
-    for distance in range(1, n_chan // 2):
+    for distance in range(n_chan // 2 - 1, 0, -1):
         pairs = [(i, i ^ (2 * distance)) for i in range(n_chan)]
         parts.append(lax.ppermute(sums[distance], "chan", pairs))
     main, edge = corange_sum(parts)

time: 45.7 us -> 44.6 us (0.976)
  Pallas kernels: 14 us -> 12.7 us
    pallas_call x1, Pallas kernels: 3.12 us -> 2.01 us  [prepare(): pl.pallas_call(prepare_kernel, in_specs=[whole(), whole(), smem()], out_s...]
  transfers between devices with their start and end apart: 12 -> 12, of which waited for: 7 -> 7; matrix products, arithmetic and copies ran while one was open for 0% -> 0% of each run, Pallas kernels for 9% -> 7%
where the time goes in v4:
time: 44.6 us; the launch traced here: 44.3 us
  starting transfers between devices  19.1 us (43%)
  Pallas kernels  12.7 us (28%)
  waiting for transfers between devices  11.7 us (26%)
  between operations  0.77 us (2%)
    pallas_call x1, Pallas kernels, partials(): pl.pallas_call(partials_kernel, in_specs=[whole()] * 10, out_specs=[whole...  7.69 us
    ppermute x3, waiting for transfers between devices, on_device(): parts.append(lax.ppermute(sums[distance], 'chan', pairs))  6.64 us
    ppermute x1, starting transfers between devices, probe_ends(): got = lax.ppermute(edge, ('chan', 'tm'), pairs)  5.19 us
    ppermute x2, starting transfers between devices, range_exchange(): got = lax.ppermute(give, 'tm', [(i, i ^ distance) for i in range(count)])  4.24 us
    ppermute x3, starting transfers between devices, on_device(): parts.append(lax.ppermute(sums[distance], 'chan', pairs))  3.62 us
    ppermute x4, starting transfers between devices, swaps(): return (lax.ppermute(first, axis, low), lax.ppermute(second, axis, high))  3.59 us
    ppermute x2, waiting for transfers between devices, range_exchange(): got = lax.ppermute(give, 'tm', [(i, i ^ distance) for i in range(count)])  2.39 us
    ppermute x1, starting transfers between devices, probe_ends(): return (got, lax.ppermute(got, 'chan', [(i, i ^ 1) for i in range(n_chan)]))  2.25 us
  transfers between devices with their start and end apart: 12, of which 7 were waited for; matrix products, arithmetic and copies ran while one was open for 0% of the time, Pallas kernels for 7%

profile of v4, /device:TPU:0, one launch (start us, length us, event | category | flops | bytes accessed | tf_op | source)
XLA Modules:
  0.0 44.3 jit_solution(7349787356631646432)
XLA Ops:
  0.6 0.0 copy-start.2
  0.6 0.0 copy-start
  0.6 1.0 %pick.1 = (bf16[8,2048]{1,0:T(8,128)(2,1)S(1)}, bf16[8,2048]{1,0:T(8,128)(2,1)S(1)}, bf16[64,128]{1,0:T(8,128)(2,1)S(1)}) custom-call(bf16[2560,2048]{1,0:T(8,128)(2,1)} %record.3, bf16[2048,128]{1,0:T(8,128)(2,1)} %range_probe.1), custom_call_target="tpu_custom_call" | custom-call | bytes 20971520 | tf_op jit(solution)/shard_map/pick/pallas_call | solution.py:382
  1.6 0.0 copy-start.1
  1.6 5.2 %collective-permute-start.2 = (bf16[64,128]{1,0:T(8,128)(2,1)S(1)}, bf16[64,128]{1,0:T(8,128)(2,1)S(1)}, u32[]{:S(2)}, u32[]{:S(2)}) collective-permute-start(bf16[64,128]{1,0:T(8,128)(2,1)S(1)} %get-tuple-element.25), channel_id=1, source_target_pairs={{0,1},{1,2},{2,3},{5,4},{6,5},{7,6},{8,9},{9,10},{10,11},{13,12},{... | collective-permute-start | bytes 49160 | tf_op jit(solution)/shard_map/ppermute | solution.py:401
  6.8 0.1 collective-permute-start
  6.9 0.7 %collective-permute-start.1 = (bf16[8,2048]{1,0:T(8,128)(2,1)S(1)}, bf16[8,2048]{1,0:T(8,128)(2,1)S(1)}, u32[]{:S(2)}, u32[]{:S(2)}) collective-permute-start(bf16[8,2048]{1,0:T(8,128)(2,1)S(1)} %get-tuple-element.24), channel_id=1, source_target_pairs={{4,8},{12,16},{20,24},{8,4},{16,12},{24,20},{5,9},{13,17},{21,25},... | collective-permute-start | bytes 98312 | tf_op jit(solution)/shard_map/ppermute | solution.py:358
  7.6 0.7 %collective-permute-done.2.probe_a = bf16[64,128]{1,0:T(8,128)(2,1)S(1)} collective-permute-done((bf16[64,128]{1,0:T(8,128)(2,1)S(1)}, bf16[64,128]{1,0:T(8,128)(2,1)S(1)}, u32[]{:S(2)}, u32[]{:S(2)}) %collective-permute-start.2) | collective-permute-done | bytes 16416 | tf_op jit(solution)/shard_map/ppermute | solution.py:401
  8.3 2.3 %collective-permute-start.3 = (bf16[64,128]{1,0:T(8,128)(2,1)S(1)}, bf16[64,128]{1,0:T(8,128)(2,1)S(1)}, u32[]{:S(2)}, u32[]{:S(2)}) collective-permute-start(bf16[64,128]{1,0:T(8,128)(2,1)S(1)} %collective-permute-done.2.probe_a), channel_id=1, source_target_pairs={{0,4},{4,0},{8,12},{12,8},{16,20},{20,16},{24,28},{28,24},{1,5},{5... | collective-permute-start | bytes 49160 | tf_op jit(solution)/shard_map/ppermute | solution.py:402
  10.5 0.0 copy-done.2
  10.5 2.0 %prepare.1 = (bf16[256,2560]{1,0:T(8,128)(2,1)S(1)}, bf16[256,128]{1,0:T(8,128)(2,1)S(1)}, bf16[128,256]{1,0:T(8,128)(2,1)S(1)}, bf16[256,512]{1,0:T(8,128)(2,1)S(1)}, bf16[128,128]{1,0:T(8,128)(2,1)S(1)}) custom-call(bf16[2560,256]{1,0:T(8,128)(2,1)S(1)} %copy-done.2, bf16[129]{0:T(256)(128)(2,1)} %fir.1, f32[9]{0:T(128)} %space.1), custom_call_target="tpu_custom_call" | custom-call | bytes 8388608 | tf_op jit(solution)/shard_map/prepare/pallas_call | solution.py:97
  12.5 0.0 collective-permute-done.3.probe_b
  12.5 0.0 collective-permute-done.row_a
  12.6 0.0 collective-permute-done.1.row_b
  12.6 0.0 copy-done
  12.6 0.0 copy-done.1
  12.6 7.7 %partials.1 = (bf16[4,32,2176]{2,1,0:T(8,128)(2,1)S(1)}, f32[4,32,2176]{2,1,0:T(8,128)S(1)}, bf16[2,656,128]{2,1,0:T(8,128)(2,1)S(1)}, f32[2,656,128]{2,1,0:T(8,128)S(1)}) custom-call(bf16[2560,2048]{1,0:T(8,128)(2,1)S(1)} %copy-done, bf16[8,2048]{1,0:T(8,128)(2,1)S(1)} %collective-permute-done.row_a, bf16[8,2048]{1,0:T(8,128)(2,1)S(1)} %collective-permute-done.1.row_b, ...), custom_call_target="tpu_custom_call" | custom-call | tf_op jit(solution)/shard_map/partials/pallas_call | solution.py:201
  20.3 0.2 collective-permute-start.5
  20.5 1.6 %collective-permute-start.4 = (bf16[2,656,128]{2,1,0:T(8,128)(2,1)S(1)}, bf16[2,656,128]{2,1,0:T(8,128)(2,1)S(1)}, u32[]{:S(2)}, u32[]{:S(2)}) collective-permute-start(bf16[2,656,128]{2,1,0:T(8,128)(2,1)S(1)} %get-tuple-element.31), channel_id=1, source_target_pairs={{0,1},{1,0},{2,3},{3,2},{4,5},{5,4},{6,7},{7,6},{8,9},{9,8},{10,11... | collective-permute-start | bytes 1007624 | tf_op jit(solution)/shard_map/ppermute | solution.py:249
  22.0 0.3 collective-permute-done.5.got
  22.3 0.1 pair_sum.1
  22.4 2.1 %collective-permute-start.6 = (bf16[32,2176]{1,0:T(8,128)(2,1)S(1)}, bf16[32,2176]{1,0:T(8,128)(2,1)S(1)}, u32[]{:S(2)}, u32[]{:S(2)}) collective-permute-start(bf16[32,2176]{1,0:T(8,128)(2,1)S(1)} %get-tuple-element.35), channel_id=1, source_target_pairs={{0,24},{4,28},{8,16},{12,20},{16,8},{20,12},{24,0},{28,4},{1,25},{... | collective-permute-start | bytes 417800 | tf_op jit(solution)/shard_map/ppermute | solution.py:420
  24.5 1.5 %collective-permute-start.7 = (bf16[32,2176]{1,0:T(8,128)(2,1)S(1)}, bf16[32,2176]{1,0:T(8,128)(2,1)S(1)}, u32[]{:S(2)}, u32[]{:S(2)}) collective-permute-start(bf16[32,2176]{1,0:T(8,128)(2,1)S(1)} %get-tuple-element.36), channel_id=1, source_target_pairs={{0,16},{4,20},{8,24},{12,28},{16,0},{20,4},{24,8},{28,12},{1,17},{... | collective-permute-start | bytes 417800 | tf_op jit(solution)/shard_map/ppermute | solution.py:420
  26.1 0.0 collective-permute-start.8
  26.1 3.9 %collective-permute-done.6.refs_1_ = bf16[32,2176]{1,0:T(8,128)(2,1)S(1)} collective-permute-done((bf16[32,2176]{1,0:T(8,128)(2,1)S(1)}, bf16[32,2176]{1,0:T(8,128)(2,1)S(1)}, u32[]{:S(2)}, u32[]{:S(2)}) %collective-permute-start.6) | collective-permute-done | bytes 139296 | tf_op jit(solution)/shard_map/ppermute | solution.py:420
  29.9 2.2 %collective-permute-done.7.refs_2_ = bf16[32,2176]{1,0:T(8,128)(2,1)S(1)} collective-permute-done((bf16[32,2176]{1,0:T(8,128)(2,1)S(1)}, bf16[32,2176]{1,0:T(8,128)(2,1)S(1)}, u32[]{:S(2)}, u32[]{:S(2)}) %collective-permute-start.7) | collective-permute-done | bytes 139296 | tf_op jit(solution)/shard_map/ppermute | solution.py:420
  32.1 0.6 %collective-permute-done.8.refs_3_ = bf16[32,2176]{1,0:T(8,128)(2,1)S(1)} collective-permute-done((bf16[32,2176]{1,0:T(8,128)(2,1)S(1)}, bf16[32,2176]{1,0:T(8,128)(2,1)S(1)}, u32[]{:S(2)}, u32[]{:S(2)}) %collective-permute-start.8) | collective-permute-done | bytes 139296 | tf_op jit(solution)/shard_map/ppermute | solution.py:420
  32.7 0.1 corange_sum.1
  32.8 0.0 collective-permute-done.4.got
  32.8 0.1 halve.1
  32.9 2.7 %collective-permute-start.9 = (bf16[1,656,128]{2,1,0:T(8,128)(2,1)S(1)}, bf16[1,656,128]{2,1,0:T(8,128)(2,1)S(1)}, u32[]{:S(2)}, u32[]{:S(2)}) collective-permute-start(bf16[1,656,128]{2,1,0:T(8,128)(2,1)S(1)} %get-tuple-element.40), channel_id=1, source_target_pairs={{0,2},{1,3},{2,0},{3,1},{4,6},{5,7},{6,4},{7,5},{8,10},{9,11},{10,... | collective-permute-start | bytes 503816 | tf_op jit(solution)/shard_map/ppermute | solution.py:249
  35.5 0.7 %collective-permute-start.11 = (f32[32,128]{1,0:T(8,128)S(1)}, f32[32,128]{1,0:T(8,128)S(1)}, u32[]{:S(2)}, u32[]{:S(2)}) collective-permute-start(f32[32,128]{1,0:T(8,128)S(1)} %get-tuple-element.41), channel_id=1, source_target_pairs={{1,2},{2,1},{5,6},{6,5},{9,10},{10,9},{13,14},{14,13},{17,18},{18,... | collective-permute-start | bytes 49160 | tf_op jit(solution)/shard_map/ppermute | solution.py:358
  36.2 2.2 %collective-permute-start.10 = (f32[32,128]{1,0:T(8,128)S(1)}, f32[32,128]{1,0:T(8,128)S(1)}, u32[]{:S(2)}, u32[]{:S(2)}) collective-permute-start(f32[32,128]{1,0:T(8,128)S(1)} %get-tuple-element.41), channel_id=1, source_target_pairs={{0,1},{1,0},{2,3},{3,2},{4,5},{5,4},{6,7},{7,6},{8,9},{9,8},{10,11... | collective-permute-start | bytes 49160 | tf_op jit(solution)/shard_map/ppermute | solution.py:358
  38.4 0.0 collective-permute-done.11.edge_b
  38.4 1.7 %collective-permute-done.10.edge_a = f32[32,128]{1,0:T(8,128)S(1)} collective-permute-done((f32[32,128]{1,0:T(8,128)S(1)}, f32[32,128]{1,0:T(8,128)S(1)}, u32[]{:S(2)}, u32[]{:S(2)}) %collective-permute-start.10) | collective-permute-done | bytes 16416 | tf_op jit(solution)/shard_map/ppermute | solution.py:358
  40.1 0.7 %corange_edges.1 = f32[32,2048]{1,0:T(8,128)} custom-call(f32[32,2048]{1,0:T(8,128)S(1)} %get-tuple-element.38.after.main, f32[32,128]{1,0:T(8,128)S(1)} %collective-permute-done.10.edge_a, f32[32,128]{1,0:T(8,128)S(1)} %collective-permute-done.11.edge_b), custom_call_target="tpu_custom_call" | custom-call | tf_op jit(solution)/shard_map/corange_edges/pallas_call | solution.py:314
  40.8 2.4 %collective-permute-done.9.refs_1_ = bf16[1,656,128]{2,1,0:T(8,128)(2,1)S(1)} collective-permute-done((bf16[1,656,128]{2,1,0:T(8,128)(2,1)S(1)}, bf16[1,656,128]{2,1,0:T(8,128)(2,1)S(1)}, u32[]{:S(2)}, u32[]{:S(2)}) %collective-permute-start.9) | collective-permute-done | bytes 167968 | tf_op jit(solution)/shard_map/ppermute | solution.py:249
  43.2 1.1 %range_sum.1 = f32[640,128]{1,0:T(8,128)} custom-call(bf16[128,128]{1,0:T(8,128)(2,1)S(1)} %get-tuple-element.22.band, f32[1,656,128]{2,1,0:T(8,128)S(1)} %get-tuple-element.39.refs_0_, bf16[1,656,128]{2,1,0:T(8,128)(2,1)S(1)} %collective-permute-done.9.refs_1_), custom_call_target="tpu_custom_call" | custom-call | tf_op jit(solution)/shard_map/range_sum/pallas_call | solution.py:341
Async XLA Ops:
  0.6 9.9 %copy-start.2 = (bf16[2560,256]{1,0:T(8,128)(2,1)S(1)}, bf16[2560,256]{1,0:T(8,128)(2,1)}, u32[]{:S(2)}) copy-start(bf16[2560,256]{1,0:T(8,128)(2,1)} %probe.2) | copy-start | bytes 3932164
  0.6 11.9 %copy-start = (bf16[2560,2048]{1,0:T(8,128)(2,1)S(1)}, bf16[2560,2048]{1,0:T(8,128)(2,1)}, u32[]{:S(2)}) copy-start(bf16[2560,2048]{1,0:T(8,128)(2,1)} %record.3) | copy-start | bytes 31457284
  1.6 11.0 %copy-start.1 = (bf16[2048,128]{1,0:T(8,128)(2,1)S(1)}, bf16[2048,128]{1,0:T(8,128)(2,1)}, u32[]{:S(2)}) copy-start(bf16[2048,128]{1,0:T(8,128)(2,1)} %range_probe.1) | copy-start | bytes 1572868
  1.6 6.6 %collective-permute-start.2 = (bf16[64,128]{1,0:T(8,128)(2,1)S(1)}, bf16[64,128]{1,0:T(8,128)(2,1)S(1)}, u32[]{:S(2)}, u32[]{:S(2)}) collective-permute-start(bf16[64,128]{1,0:T(8,128)(2,1)S(1)} %get-tuple-element.25), channel_id=1, source_target_pairs={{0,1},{1,2},{2,3},{5,4},{6,5},{7,6},{8,9},{9,10},{10,11},{13,12},{... | collective-permute-start | bytes 49160 | tf_op jit(solution)/shard_map/ppermute | solution.py:401
  6.8 5.7 %collective-permute-start = (bf16[8,2048]{1,0:T(8,128)(2,1)S(1)}, bf16[8,2048]{1,0:T(8,128)(2,1)S(1)}, u32[]{:S(2)}, u32[]{:S(2)}) collective-permute-start(bf16[8,2048]{1,0:T(8,128)(2,1)S(1)} %get-tuple-element.23), channel_id=1, source_target_pairs={{0,4},{4,0},{8,12},{12,8},{16,20},{20,16},{24,28},{28,24},{1,5},{5... | collective-permute-start | bytes 98312 | tf_op jit(solution)/shard_map/ppermute | solution.py:358
  6.9 5.6 %collective-permute-start.1 = (bf16[8,2048]{1,0:T(8,128)(2,1)S(1)}, bf16[8,2048]{1,0:T(8,128)(2,1)S(1)}, u32[]{:S(2)}, u32[]{:S(2)}) collective-permute-start(bf16[8,2048]{1,0:T(8,128)(2,1)S(1)} %get-tuple-element.24), channel_id=1, source_target_pairs={{4,8},{12,16},{20,24},{8,4},{16,12},{24,20},{5,9},{13,17},{21,25},... | collective-permute-start | bytes 98312 | tf_op jit(solution)/shard_map/ppermute | solution.py:358
  8.3 4.3 %collective-permute-start.3 = (bf16[64,128]{1,0:T(8,128)(2,1)S(1)}, bf16[64,128]{1,0:T(8,128)(2,1)S(1)}, u32[]{:S(2)}, u32[]{:S(2)}) collective-permute-start(bf16[64,128]{1,0:T(8,128)(2,1)S(1)} %collective-permute-done.2.probe_a), channel_id=1, source_target_pairs={{0,4},{4,0},{8,12},{12,8},{16,20},{20,16},{24,28},{28,24},{1,5},{5... | collective-permute-start | bytes 49160 | tf_op jit(solution)/shard_map/ppermute | solution.py:402
  20.3 2.0 %collective-permute-start.5 = (bf16[4,32,2176]{2,1,0:T(8,128)(2,1)S(1)}, bf16[4,32,2176]{2,1,0:T(8,128)(2,1)S(1)}, u32[]{:S(2)}, u32[]{:S(2)}) collective-permute-start(bf16[4,32,2176]{2,1,0:T(8,128)(2,1)S(1)} %get-tuple-element.33), channel_id=1, source_target_pairs={{0,4},{4,0},{8,12},{12,8},{16,20},{20,16},{24,28},{28,24},{1,5},{5... | collective-permute-start | bytes 1671176 | tf_op jit(solution)/shard_map/ppermute | solution.py:415
  20.5 12.3 %collective-permute-start.4 = (bf16[2,656,128]{2,1,0:T(8,128)(2,1)S(1)}, bf16[2,656,128]{2,1,0:T(8,128)(2,1)S(1)}, u32[]{:S(2)}, u32[]{:S(2)}) collective-permute-start(bf16[2,656,128]{2,1,0:T(8,128)(2,1)S(1)} %get-tuple-element.31), channel_id=1, source_target_pairs={{0,1},{1,0},{2,3},{3,2},{4,5},{5,4},{6,7},{7,6},{8,9},{9,8},{10,11... | collective-permute-start | bytes 1007624 | tf_op jit(solution)/shard_map/ppermute | solution.py:249
  22.4 7.5 %collective-permute-start.6 = (bf16[32,2176]{1,0:T(8,128)(2,1)S(1)}, bf16[32,2176]{1,0:T(8,128)(2,1)S(1)}, u32[]{:S(2)}, u32[]{:S(2)}) collective-permute-start(bf16[32,2176]{1,0:T(8,128)(2,1)S(1)} %get-tuple-element.35), channel_id=1, source_target_pairs={{0,24},{4,28},{8,16},{12,20},{16,8},{20,12},{24,0},{28,4},{1,25},{... | collective-permute-start | bytes 417800 | tf_op jit(solution)/shard_map/ppermute | solution.py:420
  24.5 7.6 %collective-permute-start.7 = (bf16[32,2176]{1,0:T(8,128)(2,1)S(1)}, bf16[32,2176]{1,0:T(8,128)(2,1)S(1)}, u32[]{:S(2)}, u32[]{:S(2)}) collective-permute-start(bf16[32,2176]{1,0:T(8,128)(2,1)S(1)} %get-tuple-element.36), channel_id=1, source_target_pairs={{0,16},{4,20},{8,24},{12,28},{16,0},{20,4},{24,8},{28,12},{1,17},{... | collective-permute-start | bytes 417800 | tf_op jit(solution)/shard_map/ppermute | solution.py:420
  26.1 6.6 %collective-permute-start.8 = (bf16[32,2176]{1,0:T(8,128)(2,1)S(1)}, bf16[32,2176]{1,0:T(8,128)(2,1)S(1)}, u32[]{:S(2)}, u32[]{:S(2)}) collective-permute-start(bf16[32,2176]{1,0:T(8,128)(2,1)S(1)} %get-tuple-element.37), channel_id=1, source_target_pairs={{0,8},{4,12},{8,0},{12,4},{16,24},{20,28},{24,16},{28,20},{1,9},{5... | collective-permute-start | bytes 417800 | tf_op jit(solution)/shard_map/ppermute | solution.py:420
  32.9 10.4 %collective-permute-start.9 = (bf16[1,656,128]{2,1,0:T(8,128)(2,1)S(1)}, bf16[1,656,128]{2,1,0:T(8,128)(2,1)S(1)}, u32[]{:S(2)}, u32[]{:S(2)}) collective-permute-start(bf16[1,656,128]{2,1,0:T(8,128)(2,1)S(1)} %get-tuple-element.40), channel_id=1, source_target_pairs={{0,2},{1,3},{2,0},{3,1},{4,6},{5,7},{6,4},{7,5},{8,10},{9,11},{10,... | collective-permute-start | bytes 503816 | tf_op jit(solution)/shard_map/ppermute | solution.py:249
  35.5 2.9 %collective-permute-start.11 = (f32[32,128]{1,0:T(8,128)S(1)}, f32[32,128]{1,0:T(8,128)S(1)}, u32[]{:S(2)}, u32[]{:S(2)}) collective-permute-start(f32[32,128]{1,0:T(8,128)S(1)} %get-tuple-element.41), channel_id=1, source_target_pairs={{1,2},{2,1},{5,6},{6,5},{9,10},{10,9},{13,14},{14,13},{17,18},{18,... | collective-permute-start | bytes 49160 | tf_op jit(solution)/shard_map/ppermute | solution.py:358
  36.2 3.9 %collective-permute-start.10 = (f32[32,128]{1,0:T(8,128)S(1)}, f32[32,128]{1,0:T(8,128)S(1)}, u32[]{:S(2)}, u32[]{:S(2)}) collective-permute-start(f32[32,128]{1,0:T(8,128)S(1)} %get-tuple-element.41), channel_id=1, source_target_pairs={{0,1},{1,0},{2,3},{3,2},{4,5},{5,4},{6,7},{7,6},{8,9},{9,8},{10,11... | collective-permute-start | bytes 49160 | tf_op jit(solution)/shard_map/ppermute | solution.py:358

commit v5 on v4

--- a/solution.py
+++ b/solution.py
@@ -89,7 +89,11 @@
     for block in range(1, last):
         put(filtered, slice(128 * block - 128, 128 * block), block_of(block).astype(BF16))
     lanes = lax.broadcasted_iota(jnp.int32, (width, 128), 1)
-    put(ends, slice(0, 128), jnp.where(lanes < 64, block_of(last), block_of(0)).astype(BF16))
+    odd = lax.rem(chan, 2) == 1
+    after, before = block_of(last), pltpu.roll(block_of(0), EDGE, 1)
+    first = jnp.where(odd, before, after)
+    second = pltpu.roll(jnp.where(odd, after, before), EDGE, 1)
+    put(ends, slice(0, 128), jnp.where(lanes < EDGE, first, second).astype(BF16))
 
 
 def prepare(probe, fir, space):
@@ -146,21 +150,17 @@
             target[index] = total[pl.ds(start, share + 2 * EDGE), :].astype(target.dtype)
 
 
-def corange_part(other, mine, record, row_a, row_b, filtered, ends, band, rim, pairs):
+def corange_part(other, mine, record, row_a, row_b, filtered, ends, band, pairs):
     channels, samples = record.shape
     width = filtered.shape[0]
     count = lax.axis_size("chan")
-    chan = lax.axis_index("chan")
-    odd = lax.rem(chan, 2)
-    rim[...] = jnp.zeros_like(rim)
-    rim[pl.ds(pl.multiple_of(odd * (128 - EDGE), EDGE), EDGE), :] = row_a[...].astype(F32)
-    rim[pl.ds(pl.multiple_of((1 - odd) * (128 - EDGE), EDGE), EDGE), :] = row_b[...].astype(F32)
+    edges = jnp.concatenate([row_a[...], row_b[...]], axis=0)
     pairs[:, :128] = jnp.zeros((2 * width, 128), BF16)
     pairs[:, 128 + samples :] = jnp.zeros((2 * width, 128), BF16)
     for block in range(0, samples, 512):
         value = jnp.dot(filtered[...], record[:, block : block + 512], preferred_element_type=F32)
         value = value + jnp.dot(
-            ends[...], rim[:, block : block + 512].astype(BF16), preferred_element_type=F32
+            ends[:, : 2 * EDGE], edges[:, block : block + 512], preferred_element_type=F32
         )
         high, low = split(value)
         pairs[:width, 128 + block : 640 + block] = high
@@ -212,7 +212,6 @@
             pltpu.VMEM((samples + 2 * HALF, sketch), BF16),
             pltpu.VMEM((samples, 2 * sketch), BF16),
             pltpu.VMEM((channels + 2 * EDGE, sketch), F32),
-            pltpu.VMEM((128, samples), F32),
             pltpu.VMEM((2 * corange, samples + 256), BF16),
         ],
         compiler_params=params,

time: 44.6 us -> 44.7 us (level)
  no operation moved by 1% of the time
where the time goes in v5:
time: 44.7 us; the launch traced here: 44.4 us
  starting transfers between devices  19 us (43%)
  Pallas kernels  12.9 us (29%)
  waiting for transfers between devices  11.8 us (26%)
  between operations  0.77 us (2%)
    pallas_call x1, Pallas kernels, partials(): pl.pallas_call(partials_kernel, in_specs=[whole()] * 10, out_specs=[whole...  7.69 us
    ppermute x3, waiting for transfers between devices, on_device(): parts.append(lax.ppermute(sums[distance], 'chan', pairs))  6.57 us
    ppermute x1, starting transfers between devices, probe_ends(): got = lax.ppermute(edge, ('chan', 'tm'), pairs)  5.19 us
    ppermute x2, starting transfers between devices, range_exchange(): got = lax.ppermute(give, 'tm', [(i, i ^ distance) for i in range(count)])  4.29 us
    ppermute x4, starting transfers between devices, swaps(): return (lax.ppermute(first, axis, low), lax.ppermute(second, axis, high))  3.59 us
    ppermute x3, starting transfers between devices, on_device(): parts.append(lax.ppermute(sums[distance], 'chan', pairs))  3.55 us
    ppermute x2, waiting for transfers between devices, range_exchange(): got = lax.ppermute(give, 'tm', [(i, i ^ distance) for i in range(count)])  2.52 us
    ppermute x1, starting transfers between devices, probe_ends(): return (got, lax.ppermute(got, 'chan', [(i, i ^ 1) for i in range(n_chan)]))  2.25 us
  transfers between devices with their start and end apart: 12, of which 7 were waited for; matrix products, arithmetic and copies ran while one was open for 0% of the time, Pallas kernels for 7%

profile of v5, /device:TPU:0, one launch (start us, length us, event | category | flops | bytes accessed | tf_op | source)
XLA Modules:
  0.0 44.4 jit_solution(17252137487975425155)
XLA Ops:
  0.6 0.0 copy-start.2
  0.6 0.0 copy-start
  0.6 1.0 %pick.1 = (bf16[8,2048]{1,0:T(8,128)(2,1)S(1)}, bf16[8,2048]{1,0:T(8,128)(2,1)S(1)}, bf16[64,128]{1,0:T(8,128)(2,1)S(1)}) custom-call(bf16[2560,2048]{1,0:T(8,128)(2,1)} %record.3, bf16[2048,128]{1,0:T(8,128)(2,1)} %range_probe.1), custom_call_target="tpu_custom_call" | custom-call | bytes 20971520 | tf_op jit(solution)/shard_map/pick/pallas_call | solution.py:381
  1.6 0.0 copy-start.1
  1.6 5.2 %collective-permute-start.2 = (bf16[64,128]{1,0:T(8,128)(2,1)S(1)}, bf16[64,128]{1,0:T(8,128)(2,1)S(1)}, u32[]{:S(2)}, u32[]{:S(2)}) collective-permute-start(bf16[64,128]{1,0:T(8,128)(2,1)S(1)} %get-tuple-element.25), channel_id=1, source_target_pairs={{0,1},{1,2},{2,3},{5,4},{6,5},{7,6},{8,9},{9,10},{10,11},{13,12},{... | collective-permute-start | bytes 49160 | tf_op jit(solution)/shard_map/ppermute | solution.py:400
  6.8 0.1 collective-permute-start
  6.9 0.7 %collective-permute-start.1 = (bf16[8,2048]{1,0:T(8,128)(2,1)S(1)}, bf16[8,2048]{1,0:T(8,128)(2,1)S(1)}, u32[]{:S(2)}, u32[]{:S(2)}) collective-permute-start(bf16[8,2048]{1,0:T(8,128)(2,1)S(1)} %get-tuple-element.24), channel_id=1, source_target_pairs={{4,8},{12,16},{20,24},{8,4},{16,12},{24,20},{5,9},{13,17},{21,25},... | collective-permute-start | bytes 98312 | tf_op jit(solution)/shard_map/ppermute | solution.py:357
  7.6 0.7 %collective-permute-done.2.probe_a = bf16[64,128]{1,0:T(8,128)(2,1)S(1)} collective-permute-done((bf16[64,128]{1,0:T(8,128)(2,1)S(1)}, bf16[64,128]{1,0:T(8,128)(2,1)S(1)}, u32[]{:S(2)}, u32[]{:S(2)}) %collective-permute-start.2) | collective-permute-done | bytes 16416 | tf_op jit(solution)/shard_map/ppermute | solution.py:400
  8.3 2.3 %collective-permute-start.3 = (bf16[64,128]{1,0:T(8,128)(2,1)S(1)}, bf16[64,128]{1,0:T(8,128)(2,1)S(1)}, u32[]{:S(2)}, u32[]{:S(2)}) collective-permute-start(bf16[64,128]{1,0:T(8,128)(2,1)S(1)} %collective-permute-done.2.probe_a), channel_id=1, source_target_pairs={{0,4},{4,0},{8,12},{12,8},{16,20},{20,16},{24,28},{28,24},{1,5},{5... | collective-permute-start | bytes 49160 | tf_op jit(solution)/shard_map/ppermute | solution.py:401
  10.5 0.0 copy-done.2
  10.5 2.1 %prepare.1 = (bf16[256,2560]{1,0:T(8,128)(2,1)S(1)}, bf16[256,128]{1,0:T(8,128)(2,1)S(1)}, bf16[128,256]{1,0:T(8,128)(2,1)S(1)}, bf16[256,512]{1,0:T(8,128)(2,1)S(1)}, bf16[128,128]{1,0:T(8,128)(2,1)S(1)}) custom-call(bf16[2560,256]{1,0:T(8,128)(2,1)S(1)} %copy-done.2, bf16[129]{0:T(256)(128)(2,1)} %fir.1, f32[9]{0:T(128)} %space.1), custom_call_target="tpu_custom_call" | custom-call | bytes 8388608 | tf_op jit(solution)/shard_map/prepare/pallas_call | solution.py:101
  12.7 0.0 collective-permute-done.3.probe_b
  12.7 0.0 collective-permute-done.row_a
  12.7 0.0 collective-permute-done.1.row_b
  12.7 0.0 copy-done
  12.7 0.0 copy-done.1
  12.7 7.7 %partials.1 = (bf16[4,32,2176]{2,1,0:T(8,128)(2,1)S(1)}, f32[4,32,2176]{2,1,0:T(8,128)S(1)}, bf16[2,656,128]{2,1,0:T(8,128)(2,1)S(1)}, f32[2,656,128]{2,1,0:T(8,128)S(1)}) custom-call(bf16[2560,2048]{1,0:T(8,128)(2,1)S(1)} %copy-done, bf16[8,2048]{1,0:T(8,128)(2,1)S(1)} %collective-permute-done.row_a, bf16[8,2048]{1,0:T(8,128)(2,1)S(1)} %collective-permute-done.1.row_b, ...), custom_call_target="tpu_custom_call" | custom-call | tf_op jit(solution)/shard_map/partials/pallas_call | solution.py:201
  20.4 0.1 collective-permute-start.5
  20.5 1.6 %collective-permute-start.4 = (bf16[2,656,128]{2,1,0:T(8,128)(2,1)S(1)}, bf16[2,656,128]{2,1,0:T(8,128)(2,1)S(1)}, u32[]{:S(2)}, u32[]{:S(2)}) collective-permute-start(bf16[2,656,128]{2,1,0:T(8,128)(2,1)S(1)} %get-tuple-element.31), channel_id=1, source_target_pairs={{0,1},{1,0},{2,3},{3,2},{4,5},{5,4},{6,7},{7,6},{8,9},{9,8},{10,11... | collective-permute-start | bytes 1007624 | tf_op jit(solution)/shard_map/ppermute | solution.py:248
  22.1 0.3 collective-permute-done.5.got
  22.4 0.1 pair_sum.1
  22.6 1.9 %collective-permute-start.6 = (bf16[32,2176]{1,0:T(8,128)(2,1)S(1)}, bf16[32,2176]{1,0:T(8,128)(2,1)S(1)}, u32[]{:S(2)}, u32[]{:S(2)}) collective-permute-start(bf16[32,2176]{1,0:T(8,128)(2,1)S(1)} %get-tuple-element.35), channel_id=1, source_target_pairs={{0,24},{4,28},{8,16},{12,20},{16,8},{20,12},{24,0},{28,4},{1,25},{... | collective-permute-start | bytes 417800 | tf_op jit(solution)/shard_map/ppermute | solution.py:419
  24.5 1.5 %collective-permute-start.7 = (bf16[32,2176]{1,0:T(8,128)(2,1)S(1)}, bf16[32,2176]{1,0:T(8,128)(2,1)S(1)}, u32[]{:S(2)}, u32[]{:S(2)}) collective-permute-start(bf16[32,2176]{1,0:T(8,128)(2,1)S(1)} %get-tuple-element.36), channel_id=1, source_target_pairs={{0,16},{4,20},{8,24},{12,28},{16,0},{20,4},{24,8},{28,12},{1,17},{... | collective-permute-start | bytes 417800 | tf_op jit(solution)/shard_map/ppermute | solution.py:419
  26.1 0.1 collective-permute-start.8
  26.1 3.9 %collective-permute-done.6.refs_1_ = bf16[32,2176]{1,0:T(8,128)(2,1)S(1)} collective-permute-done((bf16[32,2176]{1,0:T(8,128)(2,1)S(1)}, bf16[32,2176]{1,0:T(8,128)(2,1)S(1)}, u32[]{:S(2)}, u32[]{:S(2)}) %collective-permute-start.6) | collective-permute-done | bytes 139296 | tf_op jit(solution)/shard_map/ppermute | solution.py:419
  30.1 2.2 %collective-permute-done.7.refs_2_ = bf16[32,2176]{1,0:T(8,128)(2,1)S(1)} collective-permute-done((bf16[32,2176]{1,0:T(8,128)(2,1)S(1)}, bf16[32,2176]{1,0:T(8,128)(2,1)S(1)}, u32[]{:S(2)}, u32[]{:S(2)}) %collective-permute-start.7) | collective-permute-done | bytes 139296 | tf_op jit(solution)/shard_map/ppermute | solution.py:419
  32.2 0.5 %collective-permute-done.8.refs_3_ = bf16[32,2176]{1,0:T(8,128)(2,1)S(1)} collective-permute-done((bf16[32,2176]{1,0:T(8,128)(2,1)S(1)}, bf16[32,2176]{1,0:T(8,128)(2,1)S(1)}, u32[]{:S(2)}, u32[]{:S(2)}) %collective-permute-start.8) | collective-permute-done | bytes 139296 | tf_op jit(solution)/shard_map/ppermute | solution.py:419
  32.7 0.1 corange_sum.1
  32.8 0.0 collective-permute-done.4.got
  32.8 0.1 halve.1
  32.9 2.7 %collective-permute-start.9 = (bf16[1,656,128]{2,1,0:T(8,128)(2,1)S(1)}, bf16[1,656,128]{2,1,0:T(8,128)(2,1)S(1)}, u32[]{:S(2)}, u32[]{:S(2)}) collective-permute-start(bf16[1,656,128]{2,1,0:T(8,128)(2,1)S(1)} %get-tuple-element.40), channel_id=1, source_target_pairs={{0,2},{1,3},{2,0},{3,1},{4,6},{5,7},{6,4},{7,5},{8,10},{9,11},{10,... | collective-permute-start | bytes 503816 | tf_op jit(solution)/shard_map/ppermute | solution.py:248
  35.5 0.7 %collective-permute-start.11 = (f32[32,128]{1,0:T(8,128)S(1)}, f32[32,128]{1,0:T(8,128)S(1)}, u32[]{:S(2)}, u32[]{:S(2)}) collective-permute-start(f32[32,128]{1,0:T(8,128)S(1)} %get-tuple-element.41), channel_id=1, source_target_pairs={{1,2},{2,1},{5,6},{6,5},{9,10},{10,9},{13,14},{14,13},{17,18},{18,... | collective-permute-start | bytes 49160 | tf_op jit(solution)/shard_map/ppermute | solution.py:357
  36.2 2.2 %collective-permute-start.10 = (f32[32,128]{1,0:T(8,128)S(1)}, f32[32,128]{1,0:T(8,128)S(1)}, u32[]{:S(2)}, u32[]{:S(2)}) collective-permute-start(f32[32,128]{1,0:T(8,128)S(1)} %get-tuple-element.41), channel_id=1, source_target_pairs={{0,1},{1,0},{2,3},{3,2},{4,5},{5,4},{6,7},{7,6},{8,9},{9,8},{10,11... | collective-permute-start | bytes 49160 | tf_op jit(solution)/shard_map/ppermute | solution.py:357
  38.4 0.0 collective-permute-done.11.edge_b
  38.4 1.7 %collective-permute-done.10.edge_a = f32[32,128]{1,0:T(8,128)S(1)} collective-permute-done((f32[32,128]{1,0:T(8,128)S(1)}, f32[32,128]{1,0:T(8,128)S(1)}, u32[]{:S(2)}, u32[]{:S(2)}) %collective-permute-start.10) | collective-permute-done | bytes 16416 | tf_op jit(solution)/shard_map/ppermute | solution.py:357
  40.1 0.7 %corange_edges.1 = f32[32,2048]{1,0:T(8,128)} custom-call(f32[32,2048]{1,0:T(8,128)S(1)} %get-tuple-element.38.after.main, f32[32,128]{1,0:T(8,128)S(1)} %collective-permute-done.10.edge_a, f32[32,128]{1,0:T(8,128)S(1)} %collective-permute-done.11.edge_b), custom_call_target="tpu_custom_call" | custom-call | tf_op jit(solution)/shard_map/corange_edges/pallas_call | solution.py:313
  40.8 2.5 %collective-permute-done.9.refs_1_ = bf16[1,656,128]{2,1,0:T(8,128)(2,1)S(1)} collective-permute-done((bf16[1,656,128]{2,1,0:T(8,128)(2,1)S(1)}, bf16[1,656,128]{2,1,0:T(8,128)(2,1)S(1)}, u32[]{:S(2)}, u32[]{:S(2)}) %collective-permute-start.9) | collective-permute-done | bytes 167968 | tf_op jit(solution)/shard_map/ppermute | solution.py:248
  43.3 1.1 %range_sum.1 = f32[640,128]{1,0:T(8,128)} custom-call(bf16[128,128]{1,0:T(8,128)(2,1)S(1)} %get-tuple-element.22.band, f32[1,656,128]{2,1,0:T(8,128)S(1)} %get-tuple-element.39.refs_0_, bf16[1,656,128]{2,1,0:T(8,128)(2,1)S(1)} %collective-permute-done.9.refs_1_), custom_call_target="tpu_custom_call" | custom-call | tf_op jit(solution)/shard_map/range_sum/pallas_call | solution.py:340
Async XLA Ops:
  0.6 9.9 %copy-start.2 = (bf16[2560,256]{1,0:T(8,128)(2,1)S(1)}, bf16[2560,256]{1,0:T(8,128)(2,1)}, u32[]{:S(2)}) copy-start(bf16[2560,256]{1,0:T(8,128)(2,1)} %probe.2) | copy-start | bytes 3932164
  0.6 12.1 %copy-start = (bf16[2560,2048]{1,0:T(8,128)(2,1)S(1)}, bf16[2560,2048]{1,0:T(8,128)(2,1)}, u32[]{:S(2)}) copy-start(bf16[2560,2048]{1,0:T(8,128)(2,1)} %record.3) | copy-start | bytes 31457284
  1.6 11.1 %copy-start.1 = (bf16[2048,128]{1,0:T(8,128)(2,1)S(1)}, bf16[2048,128]{1,0:T(8,128)(2,1)}, u32[]{:S(2)}) copy-start(bf16[2048,128]{1,0:T(8,128)(2,1)} %range_probe.1) | copy-start | bytes 1572868
  1.6 6.6 %collective-permute-start.2 = (bf16[64,128]{1,0:T(8,128)(2,1)S(1)}, bf16[64,128]{1,0:T(8,128)(2,1)S(1)}, u32[]{:S(2)}, u32[]{:S(2)}) collective-permute-start(bf16[64,128]{1,0:T(8,128)(2,1)S(1)} %get-tuple-element.25), channel_id=1, source_target_pairs={{0,1},{1,2},{2,3},{5,4},{6,5},{7,6},{8,9},{9,10},{10,11},{13,12},{... | collective-permute-start | bytes 49160 | tf_op jit(solution)/shard_map/ppermute | solution.py:400
  6.8 5.8 %collective-permute-start = (bf16[8,2048]{1,0:T(8,128)(2,1)S(1)}, bf16[8,2048]{1,0:T(8,128)(2,1)S(1)}, u32[]{:S(2)}, u32[]{:S(2)}) collective-permute-start(bf16[8,2048]{1,0:T(8,128)(2,1)S(1)} %get-tuple-element.23), channel_id=1, source_target_pairs={{0,4},{4,0},{8,12},{12,8},{16,20},{20,16},{24,28},{28,24},{1,5},{5... | collective-permute-start | bytes 98312 | tf_op jit(solution)/shard_map/ppermute | solution.py:357
  6.9 5.8 %collective-permute-start.1 = (bf16[8,2048]{1,0:T(8,128)(2,1)S(1)}, bf16[8,2048]{1,0:T(8,128)(2,1)S(1)}, u32[]{:S(2)}, u32[]{:S(2)}) collective-permute-start(bf16[8,2048]{1,0:T(8,128)(2,1)S(1)} %get-tuple-element.24), channel_id=1, source_target_pairs={{4,8},{12,16},{20,24},{8,4},{16,12},{24,20},{5,9},{13,17},{21,25},... | collective-permute-start | bytes 98312 | tf_op jit(solution)/shard_map/ppermute | solution.py:357
  8.3 4.4 %collective-permute-start.3 = (bf16[64,128]{1,0:T(8,128)(2,1)S(1)}, bf16[64,128]{1,0:T(8,128)(2,1)S(1)}, u32[]{:S(2)}, u32[]{:S(2)}) collective-permute-start(bf16[64,128]{1,0:T(8,128)(2,1)S(1)} %collective-permute-done.2.probe_a), channel_id=1, source_target_pairs={{0,4},{4,0},{8,12},{12,8},{16,20},{20,16},{24,28},{28,24},{1,5},{5... | collective-permute-start | bytes 49160 | tf_op jit(solution)/shard_map/ppermute | solution.py:401
  20.4 2.0 %collective-permute-start.5 = (bf16[4,32,2176]{2,1,0:T(8,128)(2,1)S(1)}, bf16[4,32,2176]{2,1,0:T(8,128)(2,1)S(1)}, u32[]{:S(2)}, u32[]{:S(2)}) collective-permute-start(bf16[4,32,2176]{2,1,0:T(8,128)(2,1)S(1)} %get-tuple-element.33), channel_id=1, source_target_pairs={{0,4},{4,0},{8,12},{12,8},{16,20},{20,16},{24,28},{28,24},{1,5},{5... | collective-permute-start | bytes 1671176 | tf_op jit(solution)/shard_map/ppermute | solution.py:414
  20.5 12.3 %collective-permute-start.4 = (bf16[2,656,128]{2,1,0:T(8,128)(2,1)S(1)}, bf16[2,656,128]{2,1,0:T(8,128)(2,1)S(1)}, u32[]{:S(2)}, u32[]{:S(2)}) collective-permute-start(bf16[2,656,128]{2,1,0:T(8,128)(2,1)S(1)} %get-tuple-element.31), channel_id=1, source_target_pairs={{0,1},{1,0},{2,3},{3,2},{4,5},{5,4},{6,7},{7,6},{8,9},{9,8},{10,11... | collective-permute-start | bytes 1007624 | tf_op jit(solution)/shard_map/ppermute | solution.py:248
  22.6 7.5 %collective-permute-start.6 = (bf16[32,2176]{1,0:T(8,128)(2,1)S(1)}, bf16[32,2176]{1,0:T(8,128)(2,1)S(1)}, u32[]{:S(2)}, u32[]{:S(2)}) collective-permute-start(bf16[32,2176]{1,0:T(8,128)(2,1)S(1)} %get-tuple-element.35), channel_id=1, source_target_pairs={{0,24},{4,28},{8,16},{12,20},{16,8},{20,12},{24,0},{28,4},{1,25},{... | collective-permute-start | bytes 417800 | tf_op jit(solution)/shard_map/ppermute | solution.py:419
  24.5 7.7 %collective-permute-start.7 = (bf16[32,2176]{1,0:T(8,128)(2,1)S(1)}, bf16[32,2176]{1,0:T(8,128)(2,1)S(1)}, u32[]{:S(2)}, u32[]{:S(2)}) collective-permute-start(bf16[32,2176]{1,0:T(8,128)(2,1)S(1)} %get-tuple-element.36), channel_id=1, source_target_pairs={{0,16},{4,20},{8,24},{12,28},{16,0},{20,4},{24,8},{28,12},{1,17},{... | collective-permute-start | bytes 417800 | tf_op jit(solution)/shard_map/ppermute | solution.py:419
  26.1 6.7 %collective-permute-start.8 = (bf16[32,2176]{1,0:T(8,128)(2,1)S(1)}, bf16[32,2176]{1,0:T(8,128)(2,1)S(1)}, u32[]{:S(2)}, u32[]{:S(2)}) collective-permute-start(bf16[32,2176]{1,0:T(8,128)(2,1)S(1)} %get-tuple-element.37), channel_id=1, source_target_pairs={{0,8},{4,12},{8,0},{12,4},{16,24},{20,28},{24,16},{28,20},{1,9},{5... | collective-permute-start | bytes 417800 | tf_op jit(solution)/shard_map/ppermute | solution.py:419
  32.9 10.5 %collective-permute-start.9 = (bf16[1,656,128]{2,1,0:T(8,128)(2,1)S(1)}, bf16[1,656,128]{2,1,0:T(8,128)(2,1)S(1)}, u32[]{:S(2)}, u32[]{:S(2)}) collective-permute-start(bf16[1,656,128]{2,1,0:T(8,128)(2,1)S(1)} %get-tuple-element.40), channel_id=1, source_target_pairs={{0,2},{1,3},{2,0},{3,1},{4,6},{5,7},{6,4},{7,5},{8,10},{9,11},{10,... | collective-permute-start | bytes 503816 | tf_op jit(solution)/shard_map/ppermute | solution.py:248
  35.5 2.9 %collective-permute-start.11 = (f32[32,128]{1,0:T(8,128)S(1)}, f32[32,128]{1,0:T(8,128)S(1)}, u32[]{:S(2)}, u32[]{:S(2)}) collective-permute-start(f32[32,128]{1,0:T(8,128)S(1)} %get-tuple-element.41), channel_id=1, source_target_pairs={{1,2},{2,1},{5,6},{6,5},{9,10},{10,9},{13,14},{14,13},{17,18},{18,... | collective-permute-start | bytes 49160 | tf_op jit(solution)/shard_map/ppermute | solution.py:357
  36.2 3.9 %collective-permute-start.10 = (f32[32,128]{1,0:T(8,128)S(1)}, f32[32,128]{1,0:T(8,128)S(1)}, u32[]{:S(2)}, u32[]{:S(2)}) collective-permute-start(f32[32,128]{1,0:T(8,128)S(1)} %get-tuple-element.41), channel_id=1, source_target_pairs={{0,1},{1,0},{2,3},{3,2},{4,5},{5,4},{6,7},{7,6},{8,9},{9,8},{10,11... | collective-permute-start | bytes 49160 | tf_op jit(solution)/shard_map/ppermute | solution.py:357

commit v6 on v4

--- a/solution.py
+++ b/solution.py
@@ -157,14 +157,14 @@
     rim[pl.ds(pl.multiple_of((1 - odd) * (128 - EDGE), EDGE), EDGE), :] = row_b[...].astype(F32)
     pairs[:, :128] = jnp.zeros((2 * width, 128), BF16)
     pairs[:, 128 + samples :] = jnp.zeros((2 * width, 128), BF16)
-    for block in range(0, samples, 512):
-        value = jnp.dot(filtered[...], record[:, block : block + 512], preferred_element_type=F32)
+    for block in range(0, samples, 256):
+        value = jnp.dot(filtered[...], record[:, block : block + 256], preferred_element_type=F32)
         value = value + jnp.dot(
-            ends[...], rim[:, block : block + 512].astype(BF16), preferred_element_type=F32
+            ends[...], rim[:, block : block + 256].astype(BF16), preferred_element_type=F32
         )
         high, low = split(value)
-        pairs[:width, 128 + block : 640 + block] = high
-        pairs[width:, 128 + block : 640 + block] = low
+        pairs[:width, 128 + block : 384 + block] = high
+        pairs[width:, 128 + block : 384 + block] = low
     share = width // count
 
     def leave(columns, value):

time: 44.6 us -> 44.5 us (level)
  no operation moved by 1% of the time
where the time goes in v6:
time: 44.5 us; the launch traced here: 44.3 us
  starting transfers between devices  19.1 us (43%)
  Pallas kernels  12.7 us (29%)
  waiting for transfers between devices  11.7 us (26%)
  between operations  0.77 us (2%)
    pallas_call x1, Pallas kernels, partials(): pl.pallas_call(partials_kernel, in_specs=[whole()] * 10, out_specs=[whole...  7.68 us
    ppermute x3, waiting for transfers between devices, on_device(): parts.append(lax.ppermute(sums[distance], 'chan', pairs))  6.64 us
    ppermute x1, starting transfers between devices, probe_ends(): got = lax.ppermute(edge, ('chan', 'tm'), pairs)  5.19 us
    ppermute x2, starting transfers between devices, range_exchange(): got = lax.ppermute(give, 'tm', [(i, i ^ distance) for i in range(count)])  4.24 us
    ppermute x3, starting transfers between devices, on_device(): parts.append(lax.ppermute(sums[distance], 'chan', pairs))  3.62 us
    ppermute x4, starting transfers between devices, swaps(): return (lax.ppermute(first, axis, low), lax.ppermute(second, axis, high))  3.59 us
    ppermute x2, waiting for transfers between devices, range_exchange(): got = lax.ppermute(give, 'tm', [(i, i ^ distance) for i in range(count)])  2.39 us
    ppermute x1, starting transfers between devices, probe_ends(): return (got, lax.ppermute(got, 'chan', [(i, i ^ 1) for i in range(n_chan)]))  2.25 us
  transfers between devices with their start and end apart: 12, of which 7 were waited for; matrix products, arithmetic and copies ran while one was open for 0% of the time, Pallas kernels for 7%

profile of v6, /device:TPU:0, one launch (start us, length us, event | category | flops | bytes accessed | tf_op | source)
XLA Modules:
  0.0 44.3 jit_solution(3930488713548135321)
XLA Ops:
  0.6 0.0 copy-start.2
  0.6 0.0 copy-start
  0.6 1.0 %pick.1 = (bf16[8,2048]{1,0:T(8,128)(2,1)S(1)}, bf16[8,2048]{1,0:T(8,128)(2,1)S(1)}, bf16[64,128]{1,0:T(8,128)(2,1)S(1)}) custom-call(bf16[2560,2048]{1,0:T(8,128)(2,1)} %record.3, bf16[2048,128]{1,0:T(8,128)(2,1)} %range_probe.1), custom_call_target="tpu_custom_call" | custom-call | bytes 20971520 | tf_op jit(solution)/shard_map/pick/pallas_call | solution.py:382
  1.6 0.0 copy-start.1
  1.6 5.2 %collective-permute-start.2 = (bf16[64,128]{1,0:T(8,128)(2,1)S(1)}, bf16[64,128]{1,0:T(8,128)(2,1)S(1)}, u32[]{:S(2)}, u32[]{:S(2)}) collective-permute-start(bf16[64,128]{1,0:T(8,128)(2,1)S(1)} %get-tuple-element.25), channel_id=1, source_target_pairs={{0,1},{1,2},{2,3},{5,4},{6,5},{7,6},{8,9},{9,10},{10,11},{13,12},{... | collective-permute-start | bytes 49160 | tf_op jit(solution)/shard_map/ppermute | solution.py:401
  6.8 0.1 collective-permute-start
  6.9 0.7 %collective-permute-start.1 = (bf16[8,2048]{1,0:T(8,128)(2,1)S(1)}, bf16[8,2048]{1,0:T(8,128)(2,1)S(1)}, u32[]{:S(2)}, u32[]{:S(2)}) collective-permute-start(bf16[8,2048]{1,0:T(8,128)(2,1)S(1)} %get-tuple-element.24), channel_id=1, source_target_pairs={{4,8},{12,16},{20,24},{8,4},{16,12},{24,20},{5,9},{13,17},{21,25},... | collective-permute-start | bytes 98312 | tf_op jit(solution)/shard_map/ppermute | solution.py:358
  7.6 0.7 %collective-permute-done.2.probe_a = bf16[64,128]{1,0:T(8,128)(2,1)S(1)} collective-permute-done((bf16[64,128]{1,0:T(8,128)(2,1)S(1)}, bf16[64,128]{1,0:T(8,128)(2,1)S(1)}, u32[]{:S(2)}, u32[]{:S(2)}) %collective-permute-start.2) | collective-permute-done | bytes 16416 | tf_op jit(solution)/shard_map/ppermute | solution.py:401
  8.3 2.3 %collective-permute-start.3 = (bf16[64,128]{1,0:T(8,128)(2,1)S(1)}, bf16[64,128]{1,0:T(8,128)(2,1)S(1)}, u32[]{:S(2)}, u32[]{:S(2)}) collective-permute-start(bf16[64,128]{1,0:T(8,128)(2,1)S(1)} %collective-permute-done.2.probe_a), channel_id=1, source_target_pairs={{0,4},{4,0},{8,12},{12,8},{16,20},{20,16},{24,28},{28,24},{1,5},{5... | collective-permute-start | bytes 49160 | tf_op jit(solution)/shard_map/ppermute | solution.py:402
  10.5 0.0 copy-done.2
  10.5 2.0 %prepare.1 = (bf16[256,2560]{1,0:T(8,128)(2,1)S(1)}, bf16[256,128]{1,0:T(8,128)(2,1)S(1)}, bf16[128,256]{1,0:T(8,128)(2,1)S(1)}, bf16[256,512]{1,0:T(8,128)(2,1)S(1)}, bf16[128,128]{1,0:T(8,128)(2,1)S(1)}) custom-call(bf16[2560,256]{1,0:T(8,128)(2,1)S(1)} %copy-done.2, bf16[129]{0:T(256)(128)(2,1)} %fir.1, f32[9]{0:T(128)} %space.1), custom_call_target="tpu_custom_call" | custom-call | bytes 8388608 | tf_op jit(solution)/shard_map/prepare/pallas_call | solution.py:97
  12.5 0.0 collective-permute-done.3.probe_b
  12.5 0.0 collective-permute-done.row_a
  12.6 0.0 collective-permute-done.1.row_b
  12.6 0.0 copy-done
  12.6 0.0 copy-done.1
  12.6 7.7 %partials.1 = (bf16[4,32,2176]{2,1,0:T(8,128)(2,1)S(1)}, f32[4,32,2176]{2,1,0:T(8,128)S(1)}, bf16[2,656,128]{2,1,0:T(8,128)(2,1)S(1)}, f32[2,656,128]{2,1,0:T(8,128)S(1)}) custom-call(bf16[2560,2048]{1,0:T(8,128)(2,1)S(1)} %copy-done, bf16[8,2048]{1,0:T(8,128)(2,1)S(1)} %collective-permute-done.row_a, bf16[8,2048]{1,0:T(8,128)(2,1)S(1)} %collective-permute-done.1.row_b, ...), custom_call_target="tpu_custom_call" | custom-call | tf_op jit(solution)/shard_map/partials/pallas_call | solution.py:201
  20.3 0.2 collective-permute-start.5
  20.4 1.6 %collective-permute-start.4 = (bf16[2,656,128]{2,1,0:T(8,128)(2,1)S(1)}, bf16[2,656,128]{2,1,0:T(8,128)(2,1)S(1)}, u32[]{:S(2)}, u32[]{:S(2)}) collective-permute-start(bf16[2,656,128]{2,1,0:T(8,128)(2,1)S(1)} %get-tuple-element.31), channel_id=1, source_target_pairs={{0,1},{1,0},{2,3},{3,2},{4,5},{5,4},{6,7},{7,6},{8,9},{9,8},{10,11... | collective-permute-start | bytes 1007624 | tf_op jit(solution)/shard_map/ppermute | solution.py:249
  22.0 0.3 collective-permute-done.5.got
  22.3 0.1 pair_sum.1
  22.4 2.1 %collective-permute-start.6 = (bf16[32,2176]{1,0:T(8,128)(2,1)S(1)}, bf16[32,2176]{1,0:T(8,128)(2,1)S(1)}, u32[]{:S(2)}, u32[]{:S(2)}) collective-permute-start(bf16[32,2176]{1,0:T(8,128)(2,1)S(1)} %get-tuple-element.35), channel_id=1, source_target_pairs={{0,24},{4,28},{8,16},{12,20},{16,8},{20,12},{24,0},{28,4},{1,25},{... | collective-permute-start | bytes 417800 | tf_op jit(solution)/shard_map/ppermute | solution.py:420
  24.5 1.5 %collective-permute-start.7 = (bf16[32,2176]{1,0:T(8,128)(2,1)S(1)}, bf16[32,2176]{1,0:T(8,128)(2,1)S(1)}, u32[]{:S(2)}, u32[]{:S(2)}) collective-permute-start(bf16[32,2176]{1,0:T(8,128)(2,1)S(1)} %get-tuple-element.36), channel_id=1, source_target_pairs={{0,16},{4,20},{8,24},{12,28},{16,0},{20,4},{24,8},{28,12},{1,17},{... | collective-permute-start | bytes 417800 | tf_op jit(solution)/shard_map/ppermute | solution.py:420
  26.0 0.0 collective-permute-start.8
  26.0 3.9 %collective-permute-done.6.refs_1_ = bf16[32,2176]{1,0:T(8,128)(2,1)S(1)} collective-permute-done((bf16[32,2176]{1,0:T(8,128)(2,1)S(1)}, bf16[32,2176]{1,0:T(8,128)(2,1)S(1)}, u32[]{:S(2)}, u32[]{:S(2)}) %collective-permute-start.6) | collective-permute-done | bytes 139296 | tf_op jit(solution)/shard_map/ppermute | solution.py:420
  29.9 2.2 %collective-permute-done.7.refs_2_ = bf16[32,2176]{1,0:T(8,128)(2,1)S(1)} collective-permute-done((bf16[32,2176]{1,0:T(8,128)(2,1)S(1)}, bf16[32,2176]{1,0:T(8,128)(2,1)S(1)}, u32[]{:S(2)}, u32[]{:S(2)}) %collective-permute-start.7) | collective-permute-done | bytes 139296 | tf_op jit(solution)/shard_map/ppermute | solution.py:420
  32.1 0.6 %collective-permute-done.8.refs_3_ = bf16[32,2176]{1,0:T(8,128)(2,1)S(1)} collective-permute-done((bf16[32,2176]{1,0:T(8,128)(2,1)S(1)}, bf16[32,2176]{1,0:T(8,128)(2,1)S(1)}, u32[]{:S(2)}, u32[]{:S(2)}) %collective-permute-start.8) | collective-permute-done | bytes 139296 | tf_op jit(solution)/shard_map/ppermute | solution.py:420
  32.7 0.1 corange_sum.1
  32.8 0.0 collective-permute-done.4.got
  32.8 0.1 halve.1
  32.8 2.7 %collective-permute-start.9 = (bf16[1,656,128]{2,1,0:T(8,128)(2,1)S(1)}, bf16[1,656,128]{2,1,0:T(8,128)(2,1)S(1)}, u32[]{:S(2)}, u32[]{:S(2)}) collective-permute-start(bf16[1,656,128]{2,1,0:T(8,128)(2,1)S(1)} %get-tuple-element.40), channel_id=1, source_target_pairs={{0,2},{1,3},{2,0},{3,1},{4,6},{5,7},{6,4},{7,5},{8,10},{9,11},{10,... | collective-permute-start | bytes 503816 | tf_op jit(solution)/shard_map/ppermute | solution.py:249
  35.5 0.7 %collective-permute-start.11 = (f32[32,128]{1,0:T(8,128)S(1)}, f32[32,128]{1,0:T(8,128)S(1)}, u32[]{:S(2)}, u32[]{:S(2)}) collective-permute-start(f32[32,128]{1,0:T(8,128)S(1)} %get-tuple-element.41), channel_id=1, source_target_pairs={{1,2},{2,1},{5,6},{6,5},{9,10},{10,9},{13,14},{14,13},{17,18},{18,... | collective-permute-start | bytes 49160 | tf_op jit(solution)/shard_map/ppermute | solution.py:358
  36.2 2.2 %collective-permute-start.10 = (f32[32,128]{1,0:T(8,128)S(1)}, f32[32,128]{1,0:T(8,128)S(1)}, u32[]{:S(2)}, u32[]{:S(2)}) collective-permute-start(f32[32,128]{1,0:T(8,128)S(1)} %get-tuple-element.41), channel_id=1, source_target_pairs={{0,1},{1,0},{2,3},{3,2},{4,5},{5,4},{6,7},{7,6},{8,9},{9,8},{10,11... | collective-permute-start | bytes 49160 | tf_op jit(solution)/shard_map/ppermute | solution.py:358
  38.4 0.0 collective-permute-done.11.edge_b
  38.4 1.7 %collective-permute-done.10.edge_a = f32[32,128]{1,0:T(8,128)S(1)} collective-permute-done((f32[32,128]{1,0:T(8,128)S(1)}, f32[32,128]{1,0:T(8,128)S(1)}, u32[]{:S(2)}, u32[]{:S(2)}) %collective-permute-start.10) | collective-permute-done | bytes 16416 | tf_op jit(solution)/shard_map/ppermute | solution.py:358
  40.1 0.7 %corange_edges.1 = f32[32,2048]{1,0:T(8,128)} custom-call(f32[32,2048]{1,0:T(8,128)S(1)} %get-tuple-element.38.after.main, f32[32,128]{1,0:T(8,128)S(1)} %collective-permute-done.10.edge_a, f32[32,128]{1,0:T(8,128)S(1)} %collective-permute-done.11.edge_b), custom_call_target="tpu_custom_call" | custom-call | tf_op jit(solution)/shard_map/corange_edges/pallas_call | solution.py:314
  40.8 2.4 %collective-permute-done.9.refs_1_ = bf16[1,656,128]{2,1,0:T(8,128)(2,1)S(1)} collective-permute-done((bf16[1,656,128]{2,1,0:T(8,128)(2,1)S(1)}, bf16[1,656,128]{2,1,0:T(8,128)(2,1)S(1)}, u32[]{:S(2)}, u32[]{:S(2)}) %collective-permute-start.9) | collective-permute-done | bytes 167968 | tf_op jit(solution)/shard_map/ppermute | solution.py:249
  43.2 1.1 %range_sum.1 = f32[640,128]{1,0:T(8,128)} custom-call(bf16[128,128]{1,0:T(8,128)(2,1)S(1)} %get-tuple-element.22.band, f32[1,656,128]{2,1,0:T(8,128)S(1)} %get-tuple-element.39.refs_0_, bf16[1,656,128]{2,1,0:T(8,128)(2,1)S(1)} %collective-permute-done.9.refs_1_), custom_call_target="tpu_custom_call" | custom-call | tf_op jit(solution)/shard_map/range_sum/pallas_call | solution.py:341
Async XLA Ops:
  0.6 9.9 %copy-start.2 = (bf16[2560,256]{1,0:T(8,128)(2,1)S(1)}, bf16[2560,256]{1,0:T(8,128)(2,1)}, u32[]{:S(2)}) copy-start(bf16[2560,256]{1,0:T(8,128)(2,1)} %probe.2) | copy-start | bytes 3932164
  0.6 11.9 %copy-start = (bf16[2560,2048]{1,0:T(8,128)(2,1)S(1)}, bf16[2560,2048]{1,0:T(8,128)(2,1)}, u32[]{:S(2)}) copy-start(bf16[2560,2048]{1,0:T(8,128)(2,1)} %record.3) | copy-start | bytes 31457284
  1.6 11.0 %copy-start.1 = (bf16[2048,128]{1,0:T(8,128)(2,1)S(1)}, bf16[2048,128]{1,0:T(8,128)(2,1)}, u32[]{:S(2)}) copy-start(bf16[2048,128]{1,0:T(8,128)(2,1)} %range_probe.1) | copy-start | bytes 1572868
  1.6 6.6 %collective-permute-start.2 = (bf16[64,128]{1,0:T(8,128)(2,1)S(1)}, bf16[64,128]{1,0:T(8,128)(2,1)S(1)}, u32[]{:S(2)}, u32[]{:S(2)}) collective-permute-start(bf16[64,128]{1,0:T(8,128)(2,1)S(1)} %get-tuple-element.25), channel_id=1, source_target_pairs={{0,1},{1,2},{2,3},{5,4},{6,5},{7,6},{8,9},{9,10},{10,11},{13,12},{... | collective-permute-start | bytes 49160 | tf_op jit(solution)/shard_map/ppermute | solution.py:401
  6.8 5.7 %collective-permute-start = (bf16[8,2048]{1,0:T(8,128)(2,1)S(1)}, bf16[8,2048]{1,0:T(8,128)(2,1)S(1)}, u32[]{:S(2)}, u32[]{:S(2)}) collective-permute-start(bf16[8,2048]{1,0:T(8,128)(2,1)S(1)} %get-tuple-element.23), channel_id=1, source_target_pairs={{0,4},{4,0},{8,12},{12,8},{16,20},{20,16},{24,28},{28,24},{1,5},{5... | collective-permute-start | bytes 98312 | tf_op jit(solution)/shard_map/ppermute | solution.py:358
  6.9 5.6 %collective-permute-start.1 = (bf16[8,2048]{1,0:T(8,128)(2,1)S(1)}, bf16[8,2048]{1,0:T(8,128)(2,1)S(1)}, u32[]{:S(2)}, u32[]{:S(2)}) collective-permute-start(bf16[8,2048]{1,0:T(8,128)(2,1)S(1)} %get-tuple-element.24), channel_id=1, source_target_pairs={{4,8},{12,16},{20,24},{8,4},{16,12},{24,20},{5,9},{13,17},{21,25},... | collective-permute-start | bytes 98312 | tf_op jit(solution)/shard_map/ppermute | solution.py:358
  8.3 4.3 %collective-permute-start.3 = (bf16[64,128]{1,0:T(8,128)(2,1)S(1)}, bf16[64,128]{1,0:T(8,128)(2,1)S(1)}, u32[]{:S(2)}, u32[]{:S(2)}) collective-permute-start(bf16[64,128]{1,0:T(8,128)(2,1)S(1)} %collective-permute-done.2.probe_a), channel_id=1, source_target_pairs={{0,4},{4,0},{8,12},{12,8},{16,20},{20,16},{24,28},{28,24},{1,5},{5... | collective-permute-start | bytes 49160 | tf_op jit(solution)/shard_map/ppermute | solution.py:402
  20.3 2.0 %collective-permute-start.5 = (bf16[4,32,2176]{2,1,0:T(8,128)(2,1)S(1)}, bf16[4,32,2176]{2,1,0:T(8,128)(2,1)S(1)}, u32[]{:S(2)}, u32[]{:S(2)}) collective-permute-start(bf16[4,32,2176]{2,1,0:T(8,128)(2,1)S(1)} %get-tuple-element.33), channel_id=1, source_target_pairs={{0,4},{4,0},{8,12},{12,8},{16,20},{20,16},{24,28},{28,24},{1,5},{5... | collective-permute-start | bytes 1671176 | tf_op jit(solution)/shard_map/ppermute | solution.py:415
  20.4 12.3 %collective-permute-start.4 = (bf16[2,656,128]{2,1,0:T(8,128)(2,1)S(1)}, bf16[2,656,128]{2,1,0:T(8,128)(2,1)S(1)}, u32[]{:S(2)}, u32[]{:S(2)}) collective-permute-start(bf16[2,656,128]{2,1,0:T(8,128)(2,1)S(1)} %get-tuple-element.31), channel_id=1, source_target_pairs={{0,1},{1,0},{2,3},{3,2},{4,5},{5,4},{6,7},{7,6},{8,9},{9,8},{10,11... | collective-permute-start | bytes 1007624 | tf_op jit(solution)/shard_map/ppermute | solution.py:249
  22.4 7.5 %collective-permute-start.6 = (bf16[32,2176]{1,0:T(8,128)(2,1)S(1)}, bf16[32,2176]{1,0:T(8,128)(2,1)S(1)}, u32[]{:S(2)}, u32[]{:S(2)}) collective-permute-start(bf16[32,2176]{1,0:T(8,128)(2,1)S(1)} %get-tuple-element.35), channel_id=1, source_target_pairs={{0,24},{4,28},{8,16},{12,20},{16,8},{20,12},{24,0},{28,4},{1,25},{... | collective-permute-start | bytes 417800 | tf_op jit(solution)/shard_map/ppermute | solution.py:420
  24.5 7.6 %collective-permute-start.7 = (bf16[32,2176]{1,0:T(8,128)(2,1)S(1)}, bf16[32,2176]{1,0:T(8,128)(2,1)S(1)}, u32[]{:S(2)}, u32[]{:S(2)}) collective-permute-start(bf16[32,2176]{1,0:T(8,128)(2,1)S(1)} %get-tuple-element.36), channel_id=1, source_target_pairs={{0,16},{4,20},{8,24},{12,28},{16,0},{20,4},{24,8},{28,12},{1,17},{... | collective-permute-start | bytes 417800 | tf_op jit(solution)/shard_map/ppermute | solution.py:420
  26.0 6.6 %collective-permute-start.8 = (bf16[32,2176]{1,0:T(8,128)(2,1)S(1)}, bf16[32,2176]{1,0:T(8,128)(2,1)S(1)}, u32[]{:S(2)}, u32[]{:S(2)}) collective-permute-start(bf16[32,2176]{1,0:T(8,128)(2,1)S(1)} %get-tuple-element.37), channel_id=1, source_target_pairs={{0,8},{4,12},{8,0},{12,4},{16,24},{20,28},{24,16},{28,20},{1,9},{5... | collective-permute-start | bytes 417800 | tf_op jit(solution)/shard_map/ppermute | solution.py:420
  32.8 10.4 %collective-permute-start.9 = (bf16[1,656,128]{2,1,0:T(8,128)(2,1)S(1)}, bf16[1,656,128]{2,1,0:T(8,128)(2,1)S(1)}, u32[]{:S(2)}, u32[]{:S(2)}) collective-permute-start(bf16[1,656,128]{2,1,0:T(8,128)(2,1)S(1)} %get-tuple-element.40), channel_id=1, source_target_pairs={{0,2},{1,3},{2,0},{3,1},{4,6},{5,7},{6,4},{7,5},{8,10},{9,11},{10,... | collective-permute-start | bytes 503816 | tf_op jit(solution)/shard_map/ppermute | solution.py:249
  35.5 2.9 %collective-permute-start.11 = (f32[32,128]{1,0:T(8,128)S(1)}, f32[32,128]{1,0:T(8,128)S(1)}, u32[]{:S(2)}, u32[]{:S(2)}) collective-permute-start(f32[32,128]{1,0:T(8,128)S(1)} %get-tuple-element.41), channel_id=1, source_target_pairs={{1,2},{2,1},{5,6},{6,5},{9,10},{10,9},{13,14},{14,13},{17,18},{18,... | collective-permute-start | bytes 49160 | tf_op jit(solution)/shard_map/ppermute | solution.py:358
  36.2 3.9 %collective-permute-start.10 = (f32[32,128]{1,0:T(8,128)S(1)}, f32[32,128]{1,0:T(8,128)S(1)}, u32[]{:S(2)}, u32[]{:S(2)}) collective-permute-start(f32[32,128]{1,0:T(8,128)S(1)} %get-tuple-element.41), channel_id=1, source_target_pairs={{0,1},{1,0},{2,3},{3,2},{4,5},{5,4},{6,7},{7,6},{8,9},{9,8},{10,11... | collective-permute-start | bytes 49160 | tf_op jit(solution)/shard_map/ppermute | solution.py:358
